TPU v7x, 128 devices: a whole 4x4x4 slice. The times are simulated.
128 devices in a mesh: blk: 16 (over y_hi, x, core), kv: 8 (over z, y_lo).
Axes of the slice: x: 4, y: 4 (y_hi: 2, y_lo: 2; y = y_hi * 2 + y_lo), z: 4, core: 2. Of those that a mesh axis runs over, the one named last changes fastest.
Arguments:
- tokens: bfloat16 [8192, 2560], P('blk'), may hold values from -6 to 6
- attn_gain: float32 [2560], replicated, may hold values from 0.1 to 1.9
- mlp_gain: float32 [2560], replicated, may hold values from 0.1 to 1.9
- w_query: float32 [2560, 2560], P(('blk', 'kv')), may hold values from -0.375 to 0.375
- w_key: float32 [2560, 640], P(('blk', 'kv')), may hold values from -0.125 to 0.125
- w_value: float32 [2560, 640], P(('blk', 'kv')), may hold values from -0.125 to 0.125
- w_gate: float32 [2560, 6912], P(('blk', 'kv')), may hold values from -0.125 to 0.125
- w_up: float32 [2560, 6912], P(('blk', 'kv')), may hold values from -0.125 to 0.125
- w_out: bfloat16 [2560, 2560], P('kv'), may hold values from -0.125 to 0.125
- w_down: bfloat16 [6912, 2560], P('kv'), may hold values from -0.078125 to 0.078125
- cache: bfloat16 [2, 128, 8, 80, 128], P(None, 'blk', 'kv'), may hold values from -300 to 300
- slot_prompt: int32 [128], replicated, may hold values from 0 to 15, as said below
- prefix_len: int32 [16], replicated, may hold values from 1 to 4096, as said below
- new_len: int32 [16], replicated, may hold values from 256 to 512, as said below
Outputs:
- mixed: bfloat16 [8192, 2560], P('blk', 'kv')
Inputs may be any that keep to these rules, and one draw needn't show every extreme that they name: `slot_prompt`: the 8 slots of one index of blk hold at most 2 blocks of one prompt. One prompt, drawn afresh, has exactly 2 blocks on every index of blk; the other 6 slots of an index hold blocks of distinct prompts; every prompt has at least one block. `prefix_len`: A prompt with c slots has a prefix longer than (c - 1) * 128 and at most c * 128. Rows i >= new_len[p] of prompt p are padding.
All inputs are finite; a program needn't handle non-finite values.
Results may differ from a plain program's by a relative error of at most 0.019.
The roundings to bfloat16 on the way count: a program that leaves them out, or rounds other values in their place, can miss the bound.
Values may be sent and summed in bfloat16 or wider, within the bound.
A program may use at most 128 MiB of HBM per device.

v0:
```python
import math

import jax
import jax.numpy as jnp
from jax import lax
from jax.sharding import PartitionSpec as P

HEADS = 32
KV_HEADS = 8
HD = 80
WINDOW = 4096
SINKS = 4
BLOCK = 128
CAP = 2


FLOOR_SCORE = -1e30
EPSILON = 1e-05
ROPE_BASE = 10000.0


def rms_scale(row_data, gain_vec):
    values = row_data.astype(jnp.float32)
    mean_square = jnp.mean(values * values, axis=-1, keepdims=True)
    return (values * lax.rsqrt(mean_square + EPSILON) * gain_vec).astype(jnp.bfloat16)


def rotate(values, positions):
    head_width = values.shape[-1]
    half_width = head_width // 2
    frequency = ROPE_BASE ** (-2.0 * jnp.arange(half_width, dtype=jnp.float32) / head_width)
    angles = positions.astype(jnp.float32)[:, None] * frequency[None, :]
    cosine = jnp.cos(angles)[:, None, :]
    sine_wave = jnp.sin(angles)[:, None, :]
    first_half = values[..., :half_width]
    second_half = values[..., half_width:]
    return jnp.concatenate(
        [
            first_half * cosine - second_half * sine_wave,
            second_half * cosine + first_half * sine_wave,
        ],
        axis=-1,
    )


def slot_ranks(slot_prompt, prompts, slots):
    onehot = (slot_prompt[:, None] == jnp.arange(prompts, dtype=jnp.int32)[None, :]).astype(
        jnp.int32
    )
    running = jnp.cumsum(onehot, axis=0)
    global_rank = jnp.sum(onehot * (running - 1), axis=1)
    local_count = jnp.cumsum(onehot.reshape(-1, slots, prompts), axis=1).reshape(-1, prompts)
    local_rank = jnp.sum(onehot * (local_count - 1), axis=1)
    return (global_rank, local_rank)


def visible(query_pos, key_pos):
    distance = query_pos - key_pos
    return (distance >= 0) & ((distance < WINDOW) | (key_pos < SINKS))


def partial_block(scores, seen_mask):
    masked = jnp.where(seen_mask, scores, FLOOR_SCORE)
    row_max = jnp.max(masked, axis=-1)
    weights = jnp.where(seen_mask, jnp.exp(masked - row_max[..., None]), 0.0)
    return (row_max, jnp.sum(weights, axis=-1), weights.astype(jnp.bfloat16))


def combine(first_part, second_part):
    maxima = jnp.maximum(first_part[0], second_part[0])
    scale_first = jnp.exp(first_part[0] - maxima)
    scale_second = jnp.exp(second_part[0] - maxima)
    totals = first_part[1] * scale_first + second_part[1] * scale_second
    outputs = first_part[2] * scale_first[..., None] + second_part[2] * scale_second[..., None]
    return (maxima, totals, outputs)


def pack_groups(matrices, groups):
    pieces = [
        matrix.reshape(matrix.shape[0], groups, matrix.shape[1] // groups) for matrix in matrices
    ]
    joined = jnp.concatenate(pieces, axis=2)
    return joined.reshape(matrices[0].shape[0], -1).astype(jnp.bfloat16)


def restack(moved_rows, groups, n_blocks):
    columns = moved_rows.shape[1]
    ordered = moved_rows.reshape(groups, n_blocks, -1, columns)
    return jnp.transpose(ordered, (1, 0, 2, 3)).reshape(-1, columns)


def shards(
    tokens,
    attn_gain,
    mlp_gain,
    w_query,
    w_key,
    w_value,
    w_gate,
    w_up,
    w_out,
    w_down,
    cache,
    slot_prompt,
    prefix_len,
    new_len,
):
    groups = lax.axis_size("kv")
    n_blocks = lax.axis_size("blk")
    blk_index = lax.axis_index("blk")
    kv_index = lax.axis_index("kv")
    merged_attn = pack_groups((w_query, w_key, w_value), groups)
    merged_mlp = pack_groups((w_gate, w_up), groups)
    collected = (
        lax.all_gather(merged_attn, "blk", axis=0, tiled=True),
        lax.all_gather(merged_mlp, "blk", axis=0, tiled=True),
    )
    moved_attn, moved_mlp = (
        lax.all_to_all(collected[0], "kv", split_axis=1, concat_axis=0, tiled=True),
        lax.all_to_all(collected[1], "kv", split_axis=1, concat_axis=0, tiled=True),
    )
    w_qkv = restack(moved_attn, groups, n_blocks)
    w_pair = restack(moved_mlp, groups, n_blocks)
    query_width = w_query.shape[1] // groups
    key_width = w_key.shape[1] // groups
    kv_local = key_width // HD
    per_group = HEADS // KV_HEADS
    new_rows = tokens.shape[0]
    prompts = prefix_len.shape[0]
    slots = cache.shape[1]
    score_scale = 1.0 / math.sqrt(HD)
    prefix_here = prefix_len[blk_index]
    live_count = new_len[blk_index]
    row_ids = jnp.arange(new_rows, dtype=jnp.int32)
    positions = prefix_here + row_ids
    offsets = jnp.arange(BLOCK, dtype=jnp.int32)
    normed = rms_scale(tokens, attn_gain)
    projected = jnp.dot(normed, w_qkv, preferred_element_type=jnp.float32)
    queries = rotate(projected[:, :query_width].reshape(new_rows, -1, HD), positions).astype(
        jnp.bfloat16
    )
    key_new = rotate(
        projected[:, query_width : query_width + key_width].reshape(new_rows, kv_local, HD),
        positions,
    ).astype(jnp.bfloat16)
    value_new = (
        projected[:, query_width + key_width :].reshape(new_rows, kv_local, HD).astype(jnp.bfloat16)
    )
    grouped_q = queries.reshape(new_rows, kv_local, per_group, HD)
    own_scores = (
        jnp.einsum("qgnd,kgd->gnqk", grouped_q, key_new, preferred_element_type=jnp.float32)
        * score_scale
    )
    own_mask = (row_ids[None, :] < live_count) & visible(positions[:, None], positions[None, :])
    own_max, own_sum, own_weights = partial_block(own_scores, own_mask)
    own_out = jnp.einsum(
        "gnqk,kgd->gnqd", own_weights, value_new, preferred_element_type=jnp.float32
    )
    running = (own_max, own_sum, own_out)
    global_rank, local_rank = slot_ranks(slot_prompt, prompts, slots)
    own_prompts = lax.dynamic_slice_in_dim(slot_prompt, blk_index * slots, slots)
    own_ranks = lax.dynamic_slice_in_dim(local_rank, blk_index * slots, slots)
    placed = own_prompts * CAP + own_ranks
    buffer_ids = jnp.arange(prompts * CAP, dtype=jnp.int32)
    matches = placed[None, :] == buffer_ids[:, None]
    source_slot = jnp.sum(
        jnp.where(matches, jnp.arange(slots, dtype=jnp.int32)[None, :], 0), axis=1
    )
    filled = jnp.any(matches, axis=1)
    outgoing = jnp.where(
        filled[None, :, None, None, None],
        jnp.take(cache, source_slot, axis=1),
        jnp.zeros((), cache.dtype),
    )
    arrived = lax.all_to_all(outgoing, "blk", split_axis=1, concat_axis=1, tiled=True)
    slot_ids = jnp.arange(prompts * slots, dtype=jnp.int32)
    landing = slot_ids // slots * CAP + local_rank
    for_me = slot_prompt == blk_index
    received = (landing[None, :] == buffer_ids[:, None]) & for_me[None, :]
    block_number = jnp.sum(jnp.where(received, global_rank[None, :], 0), axis=1)
    block_live = jnp.any(received, axis=1)
    total_slots = prompts * CAP
    group_slots = min(total_slots, max(1, 512 // BLOCK))
    step_count = total_slots // group_slots
    key_blocks = arrived[0].reshape(step_count, group_slots, kv_local, HD, BLOCK)
    value_blocks = arrived[1].reshape(step_count, group_slots, kv_local, HD, BLOCK)
    numbers = block_number.reshape(step_count, group_slots)
    live_flags = block_live.reshape(step_count, group_slots)

    def prefix_step(running_state, inputs):
        key_part, value_part, number_part, flag_part = inputs
        scores = (
            jnp.einsum("qgnd,sgdt->gnqst", grouped_q, key_part, preferred_element_type=jnp.float32)
            * score_scale
        )
        scores = scores.reshape(kv_local, per_group, new_rows, group_slots * BLOCK)
        key_pos = number_part[:, None] * BLOCK + offsets[None, :]
        key_live = (flag_part[:, None] & (key_pos < prefix_here)).reshape(-1)
        seen_mask = key_live[None, :] & visible(positions[:, None], key_pos.reshape(-1)[None, :])
        block_max, block_sum, weights = partial_block(scores, seen_mask)
        weights = weights.reshape(kv_local, per_group, new_rows, group_slots, BLOCK)
        block_out = jnp.einsum(
            "gnqst,sgdt->gnqd", weights, value_part, preferred_element_type=jnp.float32
        )
        return (combine(running_state, (block_max, block_sum, block_out)), None)

    running = lax.scan(prefix_step, running, (key_blocks, value_blocks, numbers, live_flags))[0]
    totals = running[1]
    outputs = running[2]
    attended = (
        jnp.transpose(outputs / totals[..., None], (2, 0, 1, 3))
        .reshape(new_rows, -1)
        .astype(jnp.bfloat16)
    )
    projected_out = jnp.dot(attended, w_out, preferred_element_type=jnp.float32)
    summed = lax.psum(projected_out.astype(jnp.bfloat16), "kv").astype(jnp.float32)
    middle = (tokens.astype(jnp.float32) + summed).astype(jnp.bfloat16)
    normed_mid = rms_scale(middle, mlp_gain)
    paired = jnp.dot(normed_mid, w_pair, preferred_element_type=jnp.float32)
    hidden_width = w_pair.shape[1] // 2
    hidden = (jax.nn.silu(paired[:, :hidden_width]) * paired[:, hidden_width:]).astype(jnp.bfloat16)
    down_part = jnp.dot(hidden, w_down, preferred_element_type=jnp.float32)
    reduced = lax.psum_scatter(
        down_part.astype(jnp.bfloat16), "kv", scatter_dimension=1, tiled=True
    ).astype(jnp.float32)
    out_width = reduced.shape[1]
    residual = lax.dynamic_slice_in_dim(middle, kv_index * out_width, out_width, 1).astype(
        jnp.float32
    )
    mixed = jnp.where((row_ids < live_count)[:, None], residual + reduced, 0.0)
    return mixed.astype(jnp.bfloat16)


def solution(mesh):
    return jax.shard_map(
        shards,
        mesh=mesh,
        in_specs=(
            P("blk", None),
            P(),
            P(),
            P(("blk", "kv"), None),
            P(("blk", "kv"), None),
            P(("blk", "kv"), None),
            P(("blk", "kv"), None),
            P(("blk", "kv"), None),
            P("kv", None),
            P("kv", None),
            P(None, "blk", "kv", None, None),
            P(),
            P(),
            P(),
        ),
        out_specs=P("blk", "kv"),
        check_vma=False,
    )
```

profile of v0, /device:TPU:1, one launch (start us, length us, event | category | flops | bytes accessed | tf_op | source)
XLA Modules:
  0.0 535.5 jit_solution(12732997169242167067)
XLA Ops:
  18.9 8.4 %all-to-all-start.1 = ((bf16[2,32,1,80,128]{4,3,0,2,1:T(8,128)(2,1)}), bf16[2,32,1,80,128]{4,3,0,2,1:T(8,128)(2,1)S(1)}, u32[]{:S(2)}, u32[]{:S(2)}) async-start(bf16[2,32,1,80,128]{4,3,0,2,1:T(8,128)(2,1)} %fusion.68), calls=%async_computation.1 | async-start | bytes 2621440 | tf_op jit(solution)/shard_map/all_to_all | solution.py:175
  27.4 41.5 %all-gather.5.cloned.1.call-done = bf16[16,20,3840]{2,1,0:T(8,128)(2,1)} async-done(((bf16[1,20,3840]{2,1,0:T(8,128)(2,1)}), bf16[16,20,3840]{2,1,0:T(8,128)(2,1)}) %all-gather.5.cloned.1.call-update) | async-done | bytes 2457616 | tf_op jit(solution)/shard_map/all_gather | solution.py:115
  68.9 6.6 %all_to_all.27 = bf16[320,8,480]{2,1,0:T(8,128)(2,1)} reshape(bf16[16,20,3840]{2,1,0:T(8,128)(2,1)} %all-gather.5.cloned.1.call-done) | data formatting | bytes 4915200 | tf_op jit(solution)/shard_map/all_to_all | solution.py:119
  75.4 4.2 copy.61
  79.6 4.7 all-to-all-start
  85.6 4.4 copy.60
  97.2 29.5 %all-to-all-done = bf16[320,8,480]{2,0,1:T(8,128)(2,1)} async-done(((bf16[320,8,480]{2,0,1:T(8,128)(2,1)}), bf16[320,8,480]{2,0,1:T(8,128)(2,1)}, u32[]{:S(2)}, u32[]{:S(2)}) %all-to-all-start) | async-done | bytes 2457632 | tf_op jit(solution)/shard_map/all_to_all | solution.py:119
  126.7 3.3 copy.62
  132.9 5.5 %reshape.470 = bf16[2560,480]{1,0:T(8,128)(2,1)} reshape(bf16[16,8,20,480]{3,2,1,0:T(8,128)(2,1)} %copy.63) | data formatting | bytes 4915200 | tf_op jit(solution)/shard_map/reshape | solution.py:89
  138.4 4.2 fusion.55
  146.5 16.6 %all-gather.7.cloned.1.call-done = bf16[16,20,13824]{2,1,0:T(8,128)(2,1)} async-done(((bf16[1,20,13824]{2,1,0:T(8,128)(2,1)}), bf16[16,20,13824]{2,1,0:T(8,128)(2,1)}) %all-gather.7.cloned.1.call-update) | async-done | bytes 8847376 | tf_op jit(solution)/shard_map/all_gather | solution.py:116
  163.1 16.9 %all_to_all.31 = bf16[320,8,1728]{2,1,0:T(8,128)(2,1)} reshape(bf16[16,20,13824]{2,1,0:T(8,128)(2,1)} %all-gather.7.cloned.1.call-done) | data formatting | bytes 17694720 | tf_op jit(solution)/shard_map/all_to_all | solution.py:120
  180.0 8.9 %copy.68 = bf16[320,8,1728]{2,0,1:T(8,128)(2,1)} copy(bf16[320,8,1728]{2,1,0:T(8,128)(2,1)} %all_to_all.31) | data formatting | bytes 17694720 | tf_op jit(solution)/shard_map/all_to_all | solution.py:120
  189.0 5.0 all-to-all-start.2
  194.0 57.9 %while.16 = (s32[]{:T(128)}, f32[1,4,512]{2,1,0:T(4,128)S(1)}, f32[1,4,512]{2,1,0:T(4,128)S(1)}, f32[1,4,512,80]{2,3,1,0:T(8,128)S(1)}, pred[8,4]{1,0:T(8,128)(4...) while((s32[]{:T(128)}, f32[1,4,512]{2,1,0:T(4,128)S(1)}, ...), condition=%wide.region_14.15_spmd.clone.clone, body=%wide.region_11.14_spmd.clone.clone.sunk | while | flops 351253504 | bytes 15599833 | solution.py:207
  252.0 3.1 convolution_convert_fusion.1
  255.3 151.3 %all-reduce.2.cloned.1.call-done = bf16[512,2560]{0,1:T(8,128)(2,1)} async-done(((bf16[512,2560]{0,1:T(8,128)(2,1)}), bf16[512,2560]{0,1:T(8,128)(2,1)}) %all-reduce.2.cloned.1.call-update) | async-done | bytes 2621456 | tf_op jit(solution)/shard_map/psum | solution.py:216
  406.6 5.1 fusion.44
  411.7 12.2 %copy.69 = bf16[320,8,1728]{2,1,0:T(8,128)(2,1)} copy(bf16[320,8,1728]{2,0,1:T(8,128)(2,1)} %all-to-all-done.2) | data formatting | bytes 17694720 | tf_op jit(solution)/shard_map/all_to_all | solution.py:120
  423.9 10.4 %copy.70 = bf16[16,8,20,1728]{3,2,1,0:T(8,128)(2,1)} copy(bf16[16,8,20,1728]{3,1,2,0:T(8,128)(2,1)} %bitcast.203) | data formatting | bytes 17694720 | tf_op jit(solution)/shard_map/transpose | solution.py:89
  434.3 14.4 %reshape.479 = bf16[2560,1728]{1,0:T(8,128)(2,1)} reshape(bf16[16,8,20,1728]{3,2,1,0:T(8,128)(2,1)} %copy.70) | data formatting | bytes 17694720 | tf_op jit(solution)/shard_map/reshape | solution.py:89
  448.6 8.9 %fusion.57 = f32[512,1728]{0,1:T(8,128)S(1)} fusion(bf16[2560,1728]{1,0:T(8,128)(2,1)} %reshape.479, bf16[512,2560]{0,1:T(8,128)(2,1)} %get-tuple-element.184, f32[2560]{0:T(1024)S(1)} %copy-done.4, f32[512]{0:T(512)S(1)} %add_rsqrt_fusion), kind=kOutput, calls=%fused_computation.68 | convolution fusion | flops 4535091200 | bytes 15020032 | tf_op jit(solution)/shard_map/dot_general | solution.py:219
  457.5 7.4 %fusion.51 = bf16[2560,512]{1,0:T(8,128)(2,1)} fusion(bf16[864,2560]{1,0:T(8,128)(2,1)} %param.25, f32[512,1728]{0,1:T(8,128)S(1)} %fusion.57), kind=kOutput, calls=%fused_computation.63 | convolution fusion | flops 2268889088 | bytes 10584064 | tf_op jit(solution)/shard_map/dot_general | solution.py:222
  465.0 61.9 %reduce-scatter.4.cloned.1.call-done = bf16[320,512]{1,0:T(8,128)(2,1)} async-done(((bf16[2560,512]{1,0:T(8,128)(2,1)}), bf16[320,512]{1,0:T(8,128)(2,1)}) %reduce-scatter.4.cloned.1.call-update) | async-done | bytes 327696
  (178 shorter events, 87.0 us)
Async XLA Ops:
  6.5 245.4 %copy-start = (bf16[320,2560]{1,0:T(8,128)(2,1)S(1)}, bf16[320,2560]{1,0:T(8,128)(2,1)}, u32[]{:S(2)}) copy-start(bf16[320,2560]{1,0:T(8,128)(2,1)} %param.24) | copy-start | bytes 4915204
  6.5 9.2 %copy-start.2 = (s32[128]{0:T(128)S(1)}, s32[128]{0:T(128)}, u32[]{:S(2)}) copy-start(s32[128]{0:T(128)} %param.27) | copy-start | bytes 1540
  6.5 62.3 %all-gather.5.cloned.1.call-start = ((), (), s32[]{:S(2)}) async-start(), calls=%async_computation.5 | async-start | bytes 3133440 | tf_op jit(solution)/shard_map/all_gather | solution.py:115
  7.5 9.2 %copy-start.1 = (bf16[2,8,1,80,128]{4,3,2,1,0:T(8,128)(2,1)S(1)}, bf16[2,8,1,80,128]{4,3,2,1,0:T(8,128)(2,1)}, u32[]{:S(2)}) copy-start(bf16[2,8,1,80,128]{4,3,2,1,0:T(8,128)(2,1)} %param.26) | copy-start | bytes 983044
  10.8 152.4 %all-gather.7.cloned.1.call-start = ((), (), s32[]{:S(2)}) async-start(), calls=%async_computation.6 | async-start | bytes 11280384 | tf_op jit(solution)/shard_map/all_gather | solution.py:116
  18.9 60.7 %all-to-all-start.1 = ((bf16[2,32,1,80,128]{4,3,0,2,1:T(8,128)(2,1)}), bf16[2,32,1,80,128]{4,3,0,2,1:T(8,128)(2,1)S(1)}, u32[]{:S(2)}, u32[]{:S(2)}) async-start(bf16[2,32,1,80,128]{4,3,0,2,1:T(8,128)(2,1)} %fusion.68), calls=%async_computation.1 | async-start | bytes 2621440 | tf_op jit(solution)/shard_map/all_to_all | solution.py:175
  75.4 8.9 %copy-start.5 = (s32[16]{0:T(128)S(1)}, s32[16]{0:T(128)}, u32[]{:S(2)}) copy-start(s32[16]{0:T(128)} %param.28) | copy-start | bytes 196
  75.4 9.6 %copy-start.6 = (s32[16]{0:T(128)S(1)}, s32[16]{0:T(128)}, u32[]{:S(2)}) copy-start(s32[16]{0:T(128)} %param.29) | copy-start | bytes 196
  79.6 47.1 %all-to-all-start = ((bf16[320,8,480]{2,0,1:T(8,128)(2,1)}), bf16[320,8,480]{2,0,1:T(8,128)(2,1)}, u32[]{:S(2)}, u32[]{:S(2)}) async-start(bf16[320,8,480]{2,0,1:T(8,128)(2,1)} %copy.61), calls=%async_computation | async-start | bytes 5242880 | tf_op jit(solution)/shard_map/all_to_all | solution.py:119
  132.9 5.5 %copy-start.3 = (f32[2560]{0:T(1024)S(1)}, f32[2560]{0:T(1024)}, u32[]{:S(2)}) copy-start(f32[2560]{0:T(1024)} %param.17) | copy-start | bytes 30724
  189.0 222.7 %all-to-all-start.2 = ((bf16[320,8,1728]{2,0,1:T(8,128)(2,1)}), bf16[320,8,1728]{2,0,1:T(8,128)(2,1)}, u32[]{:S(2)}, u32[]{:S(2)}) async-start(bf16[320,8,1728]{2,0,1:T(8,128)(2,1)} %copy.68), calls=%async_computation.2 | async-start | bytes 18350080 | tf_op jit(solution)/shard_map/all_to_all | solution.py:120
  194.0 212.6 %all-reduce.2.cloned.1.call-start = ((), (), s32[]{:S(2)}) async-start(), calls=%async_computation.4 | async-start | bytes 5242880 | tf_op jit(solution)/shard_map/psum | solution.py:216
  255.1 271.7 %reduce-scatter.4.cloned.1.call-start = ((), (), s32[]{:S(2)}) async-start(), calls=%async_computation.7 | async-start | bytes 2949120
  434.3 14.4 %copy-start.4 = (f32[2560]{0:T(1024)S(1)}, f32[2560]{0:T(1024)}, u32[]{:S(2)}) copy-start(f32[2560]{0:T(1024)} %param.18) | copy-start | bytes 30724
Sparse Core Ops, SparseCore 0:
  10.9 57.9 all-gather.4
  71.3 91.7 all-gather.6
  255.2 151.3 all-reduce.1
  465.1 61.6 reduce-scatter.3
where the time goes:
time: 543 us; the launch traced here: 536 us
  waiting for transfers between devices  301 us (55%)
  local copies, waits for them, and re-layouts  97.1 us (18%)
  matrix products  58.8 us (11%)
  other arithmetic  46.1 us (8%)
  starting transfers between devices  18.5 us (3%)
  between operations  13.6 us (3%)
    psum x1, waiting for transfers between devices, shards(): lax.psum(projected_out.astype(jnp.bfloat16), 'kv').astype(jnp.float32)  151 us
    unnamed x5, waiting for transfers between devices  61.9 us
    all_gather x1, waiting for transfers between devices, shards(): lax.all_gather(merged_attn, 'blk', axis=0, tiled=True)  41.5 us
    all_to_all x3, local copies, waits for them, and re-layouts, shards(): lax.all_to_all(collected[1], 'kv', split_axis=1, concat_axis=0, tiled=True)  38 us
    all_to_all x1, waiting for transfers between devices, shards(): lax.all_to_all(collected[0], 'kv', split_axis=1, concat_axis=0, tiled=True)  29.5 us
    reshape x2, local copies, waits for them, and re-layouts, restack(): return jnp.transpose(ordered, (1, 0, 2, 3)).reshape(-1, columns)  19.9 us
    dot_general x8, matrix products, prefix_step(): jnp.einsum('gnqst,sgdt->gnqd', weights, value_part, preferred_element_typ...  18.6 us
    all_gather x1, waiting for transfers between devices, shards(): lax.all_gather(merged_mlp, 'blk', axis=0, tiled=True)  16.6 us
  transfers between devices with their start and end apart: 7, of which 5 were waited for; matrix products, arithmetic and copies ran while one was open for 21% of the time, Pallas kernels for 0%

commit v1 on v0

--- a/solution.py
+++ b/solution.py
@@ -76,17 +76,14 @@
 
 
 def pack_groups(matrices, groups):
+    rows = matrices[0].shape[0]
     pieces = [
-        matrix.reshape(matrix.shape[0], groups, matrix.shape[1] // groups) for matrix in matrices
+        jnp.transpose(
+            matrix.astype(jnp.bfloat16).reshape(rows, groups, matrix.shape[1] // groups), (1, 0, 2)
+        )
+        for matrix in matrices
     ]
-    joined = jnp.concatenate(pieces, axis=2)
-    return joined.reshape(matrices[0].shape[0], -1).astype(jnp.bfloat16)
-
-
-def restack(moved_rows, groups, n_blocks):
-    columns = moved_rows.shape[1]
-    ordered = moved_rows.reshape(groups, n_blocks, -1, columns)
-    return jnp.transpose(ordered, (1, 0, 2, 3)).reshape(-1, columns)
+    return jnp.concatenate(pieces, axis=2)
 
 
 def shards(
@@ -109,18 +106,12 @@
     n_blocks = lax.axis_size("blk")
     blk_index = lax.axis_index("blk")
     kv_index = lax.axis_index("kv")
-    merged_attn = pack_groups((w_query, w_key, w_value), groups)
-    merged_mlp = pack_groups((w_gate, w_up), groups)
-    collected = (
-        lax.all_gather(merged_attn, "blk", axis=0, tiled=True),
-        lax.all_gather(merged_mlp, "blk", axis=0, tiled=True),
-    )
-    moved_attn, moved_mlp = (
-        lax.all_to_all(collected[0], "kv", split_axis=1, concat_axis=0, tiled=True),
-        lax.all_to_all(collected[1], "kv", split_axis=1, concat_axis=0, tiled=True),
-    )
-    w_qkv = restack(moved_attn, groups, n_blocks)
-    w_pair = restack(moved_mlp, groups, n_blocks)
+    packed = pack_groups((w_query, w_key, w_value, w_gate, w_up), groups)
+    attn_width = (w_query.shape[1] + w_key.shape[1] + w_value.shape[1]) // groups
+    mine = lax.all_to_all(packed, "kv", split_axis=0, concat_axis=0, tiled=True)
+    mine = mine.reshape(-1, mine.shape[-1])
+    w_qkv = lax.all_gather(mine[:, :attn_width], "blk", axis=0, tiled=True)
+    w_pair = lax.all_gather(mine[:, attn_width:], "blk", axis=0, tiled=True)
     query_width = w_query.shape[1] // groups
     key_width = w_key.shape[1] // groups
     kv_local = key_width // HD
@@ -213,7 +204,8 @@
         .astype(jnp.bfloat16)
     )
     projected_out = jnp.dot(attended, w_out, preferred_element_type=jnp.float32)
-    summed = lax.psum(projected_out.astype(jnp.bfloat16), "kv").astype(jnp.float32)
+    partial_out, w_pair = lax.optimization_barrier((projected_out.astype(jnp.bfloat16), w_pair))
+    summed = lax.psum(partial_out, "kv").astype(jnp.float32)
     middle = (tokens.astype(jnp.float32) + summed).astype(jnp.bfloat16)
     normed_mid = rms_scale(middle, mlp_gain)
     paired = jnp.dot(normed_mid, w_pair, preferred_element_type=jnp.float32)

time: 543 us -> 390 us (0.72); the launches traced: 536 us -> 388 us
  waiting for transfers between devices: 301 us -> 217 us
  local copies, waits for them, and re-layouts: 97.1 us -> 25.4 us
  blocking collectives: 0 us -> 19.9 us
  starting transfers between devices: 18.5 us -> 9.1 us
    all_to_all x6 -> x0, local copies, waits for them, and re-layouts: 52 us -> none  [the longest x3 38 us: shards(): lax.all_to_all(collected[1], 'kv', split_axis=1, concat_axis=0, tiled=True)]
    all_gather x2, waiting for transfers between devices: 58.1 us -> 24.5 us  [the longest x1 24.5 us: shards(): w_qkv = lax.all_gather(mine[:, :attn_width], 'blk', axis=0, tiled=True)]
    all_to_all x2 -> x0, waiting for transfers between devices: 29.5 us -> none  [the longest x1 29.5 us: shards(): lax.all_to_all(collected[0], 'kv', split_axis=1, concat_axis=0, tiled=True)]
    psum x1, waiting for transfers between devices: 151 us -> 124 us  [shards(): summed = lax.psum(partial_out, 'kv').astype(jnp.float32)]
    all_to_all x0 -> x1, blocking collectives: none -> 19.9 us  [shards(): mine = lax.all_to_all(packed, 'kv', split_axis=0, concat_axis=0, tiled=True)]
    reshape x7, local copies, waits for them, and re-layouts: 21.3 us -> 4.29 us  [the longest x6 2.79 us: pack_groups(): matrix.astype(jnp.bfloat16).reshape(rows, groups, matrix.shape[1] // groups)]
    transpose x2, local copies, waits for them, and re-layouts: 13.3 us -> 1.68 us  [pack_groups(): jnp.transpose(matrix.astype(jnp.bfloat16).reshape(rows, groups, matrix.sh...]
    all_to_all x2 -> x0, starting transfers between devices: 9.72 us -> none  [the longest x1 5.01 us: shards(): lax.all_to_all(collected[1], 'kv', split_axis=1, concat_axis=0, tiled=True)]
  transfers between devices with their start and end apart: 7 -> 5, of which waited for: 5 -> 4; matrix products, arithmetic and copies ran while one was open for 21% -> 23% of each run, Pallas kernels for 0% -> 0%
where the time goes in v1:
time: 390 us; the launch traced here: 388 us
  waiting for transfers between devices  217 us (56%)
  matrix products  57.4 us (15%)
  other arithmetic  45.1 us (12%)
  local copies, waits for them, and re-layouts  25.4 us (7%)
  blocking collectives  19.9 us (5%)
  between operations  13.5 us (3%)
  starting transfers between devices  9.1 us (2%)
    psum x1, waiting for transfers between devices, shards(): summed = lax.psum(partial_out, 'kv').astype(jnp.float32)  124 us
    unnamed x5, waiting for transfers between devices  61.9 us
    all_gather x1, waiting for transfers between devices, shards(): w_qkv = lax.all_gather(mine[:, :attn_width], 'blk', axis=0, tiled=True)  24.5 us
    all_to_all x1, blocking collectives, shards(): mine = lax.all_to_all(packed, 'kv', split_axis=0, concat_axis=0, tiled=True)  19.9 us
    dot_general x8, matrix products, prefix_step(): jnp.einsum('gnqst,sgdt->gnqd', weights, value_part, preferred_element_typ...  18.6 us
    dot_general x8, matrix products, prefix_step(): jnp.einsum('qgnd,sgdt->gnqst', grouped_q, key_part, preferred_element_typ...  14.8 us
    reduce_sum x9, other arithmetic, partial_block(): return (row_max, jnp.sum(weights, axis=-1), weights.astype(jnp.bfloat16))  9.39 us
    dot_general x1, matrix products, shards(): paired = jnp.dot(normed_mid, w_pair, preferred_element_type=jnp.float32)  9.11 us
  transfers between devices with their start and end apart: 5, of which 4 were waited for; matrix products, arithmetic and copies ran while one was open for 23% of the time, Pallas kernels for 0%

profile of v1, /device:TPU:1, one launch (start us, length us, event | category | flops | bytes accessed | tf_op | source)
XLA Modules:
  0.0 388.4 jit_solution(8976269910257673150)
XLA Ops:
  17.6 19.9 %all_to_all.10 = bf16[8,20,2208]{2,1,0:T(8,128)(2,1)} all-to-all(bf16[8,20,2208]{2,1,0:T(8,128)(2,1)S(1)} %concatenate.33), channel_id=1, replica_groups=mesh['blk'=16,'kv'=8] {'kv'}, dimensions={0} | all-to-all | bytes 1413120 | tf_op jit(solution)/shard_map/all_to_all | solution.py:111
  43.0 8.6 %all-to-all-start.1 = ((bf16[2,32,1,80,128]{4,3,0,2,1:T(8,128)(2,1)}), bf16[2,32,1,80,128]{4,3,0,2,1:T(8,128)(2,1)S(1)}, u32[]{:S(2)}, u32[]{:S(2)}) async-start(bf16[2,32,1,80,128]{4,3,0,2,1:T(8,128)(2,1)} %fusion.68), calls=%async_computation.1 | async-start | bytes 2621440 | tf_op jit(solution)/shard_map/all_to_all | solution.py:166
  55.0 4.4 %copy.51 = bf16[512,2560]{0,1:T(8,128)(2,1)} copy(bf16[512,2560]{1,0:T(8,128)(2,1)} %param.16) | data formatting | bytes 5242880 | tf_op args[0]
  60.8 2.4 fusion.47
  64.0 2.1 slice.65
  66.4 7.2 %all-to-all-done.1 = bf16[2,32,1,80,128]{4,3,0,2,1:T(8,128)(2,1)S(1)} async-done(((bf16[2,32,1,80,128]{4,3,0,2,1:T(8,128)(2,1)}), bf16[2,32,1,80,128]{4,3,0,2,1:T(8,128)(2,1)S(1)}, u32[]{:S(2)}, u32[]{:S(2)}) %all-to-all-start.1) | async-done | bytes 1310752 | tf_op jit(solution)/shard_map/all_to_all | solution.py:166
  74.7 24.5 %all-gather.3.cloned.1.call-done = bf16[2560,480]{1,0:T(8,128)(2,1)} async-done(((bf16[160,480]{1,0:T(8,128)(2,1)}), bf16[2560,480]{1,0:T(8,128)(2,1)}) %all-gather.3.cloned.1.call-update) | async-done | bytes 2457616 | tf_op jit(solution)/shard_map/all_gather | solution.py:113
  99.2 4.2 %fusion.55 = f32[512,480]{0,1:T(8,128)S(1)} fusion(bf16[2560,480]{1,0:T(8,128)(2,1)} %all-gather.3.cloned.1.call-done, bf16[512,2560]{0,1:T(8,128)(2,1)} %copy.51, f32[2560]{0:T(1024)S(1)} %copy-done.7, f32[512]{0:T(512)S(1)} %add_rsqrt_fusion.1), kind=kOutput, calls=%fused_computation.67 | convolution fusion | flops 1263534080 | bytes 6074368 | tf_op jit(solution)/shard_map/dot_general | solution.py:129
  106.0 2.2 fusion.69
  108.2 64.2 %while.16 = (s32[]{:T(128)}, f32[1,4,512]{2,1,0:T(4,128)S(1)}, f32[1,4,512]{2,1,0:T(4,128)S(1)}, f32[1,4,512,80]{2,3,1,0:T(8,128)}, pred[8,4]{1,0:T(8,128)(4,1)S...) while((s32[]{:T(128)}, f32[1,4,512]{2,1,0:T(4,128)S(1)}, ...), condition=%wide.region_14.15_spmd.clone.clone, body=%wide.region_11.14_spmd.clone.clone.sunk | while | flops 351253504 | bytes 20842768 | solution.py:198
  113.0 2.3 fusion.134
  121.1 2.3 fusion.134
  129.1 2.3 fusion.134
  137.1 2.3 fusion.134
  145.1 2.3 fusion.134
  153.1 2.3 fusion.134
  161.1 2.3 fusion.134
  169.2 2.3 fusion.134
  173.5 3.0 convolution_convert_fusion.1
  176.9 123.8 %all-reduce.2.cloned.1.call-done = bf16[512,2560]{0,1:T(8,128)(2,1)} async-done(((bf16[512,2560]{0,1:T(8,128)(2,1)}), bf16[512,2560]{0,1:T(8,128)(2,1)}) %all-reduce.2.cloned.1.call-update) | async-done | bytes 2621456 | tf_op jit(solution)/shard_map/psum | solution.py:208
  300.7 3.7 fusion.44
  304.5 9.1 %fusion.57 = f32[512,1728]{0,1:T(8,128)S(1)} fusion(bf16[2560,1728]{1,0:T(8,128)(2,1)} %all-gather.5.cloned.1.call-done, bf16[512,2560]{0,1:T(8,128)(2,1)S(1)} %get-tuple-element.178, f32[2560]{0:T(1024)S(1)} %copy-done.8, f32[512]{0:T(512)S(1)} %add_rsqrt_fusion), kind=kOutput, calls=%fused_computation.68 | convolution fusion | flops 4535091200 | bytes 15020032 | tf_op jit(solution)/shard_map/dot_general | solution.py:211
  313.6 4.4 %fusion.51 = bf16[2560,512]{1,0:T(8,128)(2,1)} fusion(bf16[864,2560]{1,0:T(8,128)(2,1)S(1)} %bitcast.216, f32[512,1728]{0,1:T(8,128)S(1)} %fusion.57), kind=kOutput, calls=%fused_computation.63 | convolution fusion | flops 2268889088 | bytes 10584064 | tf_op jit(solution)/shard_map/dot_general | solution.py:214
  318.1 61.9 %reduce-scatter.4.cloned.1.call-done = bf16[320,512]{1,0:T(8,128)(2,1)} async-done(((bf16[2560,512]{1,0:T(8,128)(2,1)}), bf16[320,512]{1,0:T(8,128)(2,1)}) %reduce-scatter.4.cloned.1.call-update) | async-done | bytes 327696
  (210 shorter events, 74.2 us)
Async XLA Ops:
  6.5 167.0 %copy-start = (bf16[320,2560]{1,0:T(8,128)(2,1)S(1)}, bf16[320,2560]{1,0:T(8,128)(2,1)}, u32[]{:S(2)}) copy-start(bf16[320,2560]{1,0:T(8,128)(2,1)} %param.24) | copy-start | bytes 4915204
  6.5 92.7 %all-gather.3.cloned.1.call-start = ((), (), s32[]{:S(2)}) async-start(), calls=%async_computation.3 | async-start | bytes 2785280 | tf_op jit(solution)/shard_map/all_gather | solution.py:113
  12.0 27.8 %copy-start.6 = (s32[128]{0:T(128)S(1)}, s32[128]{0:T(128)}, u32[]{:S(2)}) copy-start(s32[128]{0:T(128)} %param.27) | copy-start | bytes 1540
  13.1 27.6 %copy-start.1 = (bf16[2,8,1,80,128]{4,3,2,1,0:T(8,128)(2,1)S(1)}, bf16[2,8,1,80,128]{4,3,2,1,0:T(8,128)(2,1)}, u32[]{:S(2)}) copy-start(bf16[2,8,1,80,128]{4,3,2,1,0:T(8,128)(2,1)} %param.26) | copy-start | bytes 983044
  39.0 1.7 copy-start.3
  39.7 11.9 %copy-start.9 = (s32[16]{0:T(128)S(1)}, s32[16]{0:T(128)}, u32[]{:S(2)}) copy-start(s32[16]{0:T(128)} %param.28) | copy-start | bytes 196
  39.7 12.6 %copy-start.10 = (s32[16]{0:T(128)S(1)}, s32[16]{0:T(128)}, u32[]{:S(2)}) copy-start(s32[16]{0:T(128)} %param.29) | copy-start | bytes 196
  43.0 30.5 %all-to-all-start.1 = ((bf16[2,32,1,80,128]{4,3,0,2,1:T(8,128)(2,1)}), bf16[2,32,1,80,128]{4,3,0,2,1:T(8,128)(2,1)S(1)}, u32[]{:S(2)}, u32[]{:S(2)}) async-start(bf16[2,32,1,80,128]{4,3,0,2,1:T(8,128)(2,1)} %fusion.68), calls=%async_computation.1 | async-start | bytes 2621440 | tf_op jit(solution)/shard_map/all_to_all | solution.py:166
  51.6 124.9 %all-gather.5.cloned.1.call-start = ((), (), s32[]{:S(2)}) async-start(), calls=%async_computation.4 | async-start | bytes 9748480 | tf_op jit(solution)/shard_map/all_gather | solution.py:114
  59.4 39.8 %copy-start.7 = (f32[2560]{0:T(1024)S(1)}, f32[2560]{0:T(1024)}, u32[]{:S(2)}) copy-start(f32[2560]{0:T(1024)} %param.17) | copy-start | bytes 30724
  66.1 234.5 %all-reduce.2.cloned.1.call-start = ((), (), s32[]{:S(2)}) async-start(), calls=%async_computation.5 | async-start | bytes 5242880 | tf_op jit(solution)/shard_map/psum | solution.py:208
  110.1 3.0 copy-start.4
  118.1 3.0 copy-start.4
  126.1 3.0 copy-start.4
  134.1 3.0 copy-start.4
  142.1 3.0 copy-start.4
  150.2 3.0 copy-start.4
  158.2 3.0 copy-start.4
  166.2 3.0 copy-start.4
  176.6 127.9 %copy-start.8 = (f32[2560]{0:T(1024)S(1)}, f32[2560]{0:T(1024)}, u32[]{:S(2)}) copy-start(f32[2560]{0:T(1024)} %param.18) | copy-start | bytes 30724
  176.6 203.4 %reduce-scatter.4.cloned.1.call-start = ((), (), s32[]{:S(2)}) async-start(), calls=%async_computation.6 | async-start | bytes 2949120
  300.7 12.9 %slice-start = ((s8[4423680]{0:T(1024)(128)(4,1)}), s8[4194304]{0:T(1024)(128)(4,1)S(1)}, s32[]{:S(2)}) async-start(s8[4423680]{0:T(1024)(128)(4,1)} %bitcast.215), calls=%async_computation.7 | async-start | bytes 8388608
  304.4 9.2 %copy-start.2 = (bf16[512,2560]{0,1:T(8,128)(2,1)}, bf16[512,2560]{0,1:T(8,128)(2,1)S(1)}, u32[]{:S(2)}) copy-start(bf16[512,2560]{0,1:T(8,128)(2,1)S(1)} %get-tuple-element.178) | copy-start | bytes 7864324
  304.4 9.2 %slice-start.1 = ((s8[4423680]{0:T(1024)(128)(4,1)}), s8[229376]{0:T(1024)(128)(4,1)S(1)}, s32[]{:S(2)}) async-start(s8[4423680]{0:T(1024)(128)(4,1)} %bitcast.215), calls=%async_computation.8 | async-start | bytes 458752
  (8 other events, 6.8 us)
Sparse Core Ops, SparseCore 0:
  39.9 59.2 all-gather.2
  101.6 74.8 all-gather.4
  179.0 121.6 all-reduce.1
  318.2 61.7 reduce-scatter.3

commit v2 on v1

--- a/solution.py
+++ b/solution.py
@@ -1,8 +1,11 @@
+import functools
 import math
 
 import jax
 import jax.numpy as jnp
 from jax import lax
+from jax.experimental import pallas as pl
+from jax.experimental.pallas import tpu as pltpu
 from jax.sharding import PartitionSpec as P
 
 HEADS = 32
@@ -84,6 +87,124 @@
         for matrix in matrices
     ]
     return jnp.concatenate(pieces, axis=2)
+
+
+MESH = pl.DeviceIdType.MESH
+VMEM_SPEC = pl.BlockSpec(memory_space=pltpu.VMEM)
+
+
+def greet(n, me):
+    barrier = pltpu.get_barrier_semaphore()
+    for step in range(1, n):
+        peer = lax.rem(me + step, n)
+        pl.semaphore_signal(barrier, inc=1, device_id={"kv": peer}, device_id_type=MESH)
+    pl.semaphore_wait(barrier, n - 1)
+
+
+def exchange(n, me, piece_ref, landed, send_sem, recv_sem):
+    copies = []
+    for step in range(1, n):
+        peer = lax.rem(me + step, n)
+        copy = pltpu.make_async_remote_copy(
+            src_ref=piece_ref.at[peer],
+            dst_ref=landed.at[step - 1],
+            send_sem=send_sem.at[step - 1],
+            recv_sem=recv_sem.at[step - 1],
+            device_id={"kv": peer},
+            device_id_type=MESH,
+        )
+        copy.start()
+        copies.append(copy)
+    return copies
+
+
+def middle_kernel(
+    n, piece_ref, token_ref, gain_ref, middle_ref, normed_ref, landed, total, whole,
+    send_sem, recv_sem, share_sem, join_sem,
+):
+    me = lax.axis_index("kv")
+    rows = piece_ref.shape[1]
+    greet(n, me)
+    copies = exchange(n, me, piece_ref, landed, send_sem, recv_sem)
+    own = pl.ds(pl.multiple_of(me * rows, rows), rows)
+    total[...] = token_ref[own, :].astype(jnp.float32) + piece_ref[me].astype(jnp.float32)
+    for step in range(1, n):
+        copies[step - 1].wait_recv()
+        total[...] += landed[step - 1].astype(jnp.float32)
+    whole[0] = total[...].astype(jnp.bfloat16)
+    shares = []
+    for step in range(1, n):
+        peer = lax.rem(me + step, n)
+        share = pltpu.make_async_remote_copy(
+            src_ref=whole.at[0],
+            dst_ref=whole.at[step],
+            send_sem=share_sem.at[step - 1],
+            recv_sem=join_sem.at[step - 1],
+            device_id={"kv": peer},
+            device_id_type=MESH,
+        )
+        share.start()
+        shares.append(share)
+    for step in range(n):
+        if step:
+            shares[step - 1].wait_recv()
+        owner = lax.rem(me + n - step, n)
+        place = pl.ds(pl.multiple_of(owner * rows, rows), rows)
+        middle_rows = whole[step]
+        middle_ref[place, :] = middle_rows
+        values = middle_rows.astype(jnp.float32)
+        mean_square = jnp.mean(values * values, axis=-1, keepdims=True)
+        normed_ref[place, :] = (
+            values * lax.rsqrt(mean_square + EPSILON) * gain_ref[...]
+        ).astype(jnp.bfloat16)
+    for copy in copies + shares:
+        copy.wait_send()
+
+
+def sum_middle(n, partial_out, tokens, mlp_gain):
+    rows, width = tokens.shape
+    piece = rows // n
+    whole_shape = jax.ShapeDtypeStruct((rows, width), jnp.bfloat16)
+    return pl.pallas_call(
+        functools.partial(middle_kernel, n),
+        name="sum_middle",
+        out_shape=(whole_shape, whole_shape),
+        in_specs=[VMEM_SPEC] * 3,
+        out_specs=(VMEM_SPEC, VMEM_SPEC),
+        scratch_shapes=[
+            pltpu.VMEM((n - 1, piece, width), jnp.bfloat16),
+            pltpu.VMEM((piece, width), jnp.float32),
+            pltpu.VMEM((n, piece, width), jnp.bfloat16),
+        ]
+        + [pltpu.SemaphoreType.DMA((n - 1,))] * 4,
+        compiler_params=pltpu.CompilerParams(collective_id=0, has_side_effects=True),
+    )(partial_out.reshape(n, piece, width), tokens, mlp_gain.reshape(1, width))
+
+
+def scatter_kernel(n, piece_ref, out_ref, landed, send_sem, recv_sem):
+    me = lax.axis_index("kv")
+    greet(n, me)
+    copies = exchange(n, me, piece_ref, landed, send_sem, recv_sem)
+    out_ref[...] = piece_ref[me].astype(jnp.float32)
+    for step in range(1, n):
+        copies[step - 1].wait_recv()
+        out_ref[...] += landed[step - 1].astype(jnp.float32)
+    for copy in copies:
+        copy.wait_send()
+
+
+def sum_scatter(n, pieces):
+    shape = pieces.shape[1:]
+    return pl.pallas_call(
+        functools.partial(scatter_kernel, n),
+        name="sum_scatter",
+        out_shape=jax.ShapeDtypeStruct(shape, jnp.float32),
+        in_specs=[VMEM_SPEC],
+        out_specs=VMEM_SPEC,
+        scratch_shapes=[pltpu.VMEM((n - 1,) + shape, jnp.bfloat16)]
+        + [pltpu.SemaphoreType.DMA((n - 1,))] * 2,
+        compiler_params=pltpu.CompilerParams(collective_id=1, has_side_effects=True),
+    )(pieces)
 
 
 def shards(
@@ -205,16 +326,14 @@
     )
     projected_out = jnp.dot(attended, w_out, preferred_element_type=jnp.float32)
     partial_out, w_pair = lax.optimization_barrier((projected_out.astype(jnp.bfloat16), w_pair))
-    summed = lax.psum(partial_out, "kv").astype(jnp.float32)
-    middle = (tokens.astype(jnp.float32) + summed).astype(jnp.bfloat16)
-    normed_mid = rms_scale(middle, mlp_gain)
+    middle, normed_mid = sum_middle(groups, partial_out, tokens, mlp_gain)
     paired = jnp.dot(normed_mid, w_pair, preferred_element_type=jnp.float32)
     hidden_width = w_pair.shape[1] // 2
     hidden = (jax.nn.silu(paired[:, :hidden_width]) * paired[:, hidden_width:]).astype(jnp.bfloat16)
-    down_part = jnp.dot(hidden, w_down, preferred_element_type=jnp.float32)
-    reduced = lax.psum_scatter(
-        down_part.astype(jnp.bfloat16), "kv", scatter_dimension=1, tiled=True
-    ).astype(jnp.float32)
+    down_part = lax.dot_general(
+        w_down, hidden, (((0,), (1,)), ((), ())), preferred_element_type=jnp.float32
+    ).astype(jnp.bfloat16)
+    reduced = sum_scatter(groups, down_part.reshape(groups, -1, new_rows)).T
     out_width = reduced.shape[1]
     residual = lax.dynamic_slice_in_dim(middle, kv_index * out_width, out_width, 1).astype(
         jnp.float32

time: 390 us -> 313 us (0.80)
  waiting for transfers between devices: 217 us -> 35.8 us
  Pallas kernels: 0 us -> 104 us
  local copies, waits for them, and re-layouts: 25.4 us -> 30.3 us
    psum x1 -> x0, waiting for transfers between devices: 124 us -> none  [shards(): summed = lax.psum(partial_out, 'kv').astype(jnp.float32)]
    pallas_call x0 -> x2, Pallas kernels: none -> 104 us  [the longest x1 69.2 us: sum_middle(): pl.pallas_call(functools.partial(middle_kernel, n), name='sum_middle', ou...]
    unnamed x5 -> x2, waiting for transfers between devices: 61.9 us -> 0.03 us
    pallas_call x0 -> x1, local copies, waits for them, and re-layouts: none -> 4.44 us  [sum_middle(): pl.pallas_call(functools.partial(middle_kernel, n), name='sum_middle', ou...]
    unnamed x23 -> x20, local copies, waits for them, and re-layouts: 4.46 us -> 0.05 us
    convert_element_type x0 -> x1, local copies, waits for them, and re-layouts: none -> 4.39 us  [shards(): down_part = lax.dot_general(w_down, hidden, (((0,), (1,)), ((), ())), pre...]
    all_to_all x1, waiting for transfers between devices: 7.16 us -> 11.3 us  [shards(): lax.all_to_all(outgoing, 'blk', split_axis=1, concat_axis=1, tiled=True)]
  transfers between devices with their start and end apart: 5 -> 3, of which waited for: 4 -> 2; matrix products, arithmetic and copies ran while one was open for 23% -> 27% of each run, Pallas kernels for 0% -> 0%
where the time goes in v2:
time: 313 us; the launch traced here: 312 us
  Pallas kernels  104 us (33%)
  matrix products  56.7 us (18%)
  other arithmetic  41.6 us (13%)
  waiting for transfers between devices  35.8 us (11%)
  local copies, waits for them, and re-layouts  30.3 us (10%)
  blocking collectives  19.9 us (6%)
  between operations  13.8 us (4%)
  starting transfers between devices  8.63 us (3%)
    pallas_call x1, Pallas kernels, sum_middle(): pl.pallas_call(functools.partial(middle_kernel, n), name='sum_middle', ou...  69.2 us
    pallas_call x1, Pallas kernels, sum_scatter(): pl.pallas_call(functools.partial(scatter_kernel, n), name='sum_scatter',...  35.2 us
    all_gather x1, waiting for transfers between devices, shards(): w_qkv = lax.all_gather(mine[:, :attn_width], 'blk', axis=0, tiled=True)  24.5 us
    all_to_all x1, blocking collectives, shards(): mine = lax.all_to_all(packed, 'kv', split_axis=0, concat_axis=0, tiled=True)  19.9 us
    dot_general x8, matrix products, prefix_step(): jnp.einsum('gnqst,sgdt->gnqd', weights, value_part, preferred_element_typ...  18.6 us
    dot_general x8, matrix products, prefix_step(): jnp.einsum('qgnd,sgdt->gnqst', grouped_q, key_part, preferred_element_typ...  14.8 us
    all_to_all x1, waiting for transfers between devices, shards(): lax.all_to_all(outgoing, 'blk', split_axis=1, concat_axis=1, tiled=True)  11.3 us
    reduce_sum x9, other arithmetic, partial_block(): return (row_max, jnp.sum(weights, axis=-1), weights.astype(jnp.bfloat16))  9.39 us
  transfers between devices with their start and end apart: 3, of which 2 were waited for; matrix products, arithmetic and copies ran while one was open for 27% of the time, Pallas kernels for 0%

profile of v2, /device:TPU:1, one launch (start us, length us, event | category | flops | bytes accessed | tf_op | source)
XLA Modules:
  0.0 311.8 jit_solution(6787470470676666848)
XLA Ops:
  17.6 19.9 %all_to_all.10 = bf16[8,20,2208]{2,1,0:T(8,128)(2,1)} all-to-all(bf16[8,20,2208]{2,1,0:T(8,128)(2,1)S(1)} %concatenate.33), channel_id=1, replica_groups=mesh['blk'=16,'kv'=8] {'kv'}, dimensions={0} | all-to-all | bytes 1413120 | tf_op jit(solution)/shard_map/all_to_all | solution.py:232
  43.0 8.6 %all-to-all-start.1 = ((bf16[2,32,1,80,128]{4,3,0,2,1:T(8,128)(2,1)}), bf16[2,32,1,80,128]{4,3,0,2,1:T(8,128)(2,1)S(1)}, u32[]{:S(2)}, u32[]{:S(2)}) async-start(bf16[2,32,1,80,128]{4,3,0,2,1:T(8,128)(2,1)} %fusion.60), calls=%async_computation.1 | async-start | bytes 2621440 | tf_op jit(solution)/shard_map/all_to_all | solution.py:287
  56.9 2.3 fusion.44
  60.1 2.2 slice.65
  62.3 11.3 %all-to-all-done.1 = bf16[2,32,1,80,128]{4,3,0,2,1:T(8,128)(2,1)S(1)} async-done(((bf16[2,32,1,80,128]{4,3,0,2,1:T(8,128)(2,1)}), bf16[2,32,1,80,128]{4,3,0,2,1:T(8,128)(2,1)S(1)}, u32[]{:S(2)}, u32[]{:S(2)}) %all-to-all-start.1) | async-done | bytes 1310752 | tf_op jit(solution)/shard_map/all_to_all | solution.py:287
  74.7 24.5 %all-gather.3.cloned.1.call-done = bf16[2560,480]{1,0:T(8,128)(2,1)} async-done(((bf16[160,480]{1,0:T(8,128)(2,1)}), bf16[2560,480]{1,0:T(8,128)(2,1)}) %all-gather.3.cloned.1.call-update) | async-done | bytes 2457616 | tf_op jit(solution)/shard_map/all_gather | solution.py:234
  99.2 4.1 %fusion.51 = f32[512,480]{0,1:T(8,128)S(1)} fusion(bf16[2560,480]{1,0:T(8,128)(2,1)} %all-gather.3.cloned.1.call-done, bf16[512,2560]{1,0:T(8,128)(2,1)} %token_ref.1, f32[2560]{0:T(1024)S(1)} %copy-done.7, f32[512]{0:T(512)S(1)} %add_rsqrt_fusion), kind=kOutput, calls=%fused_computation.60 | convolution fusion | flops 1263534080 | bytes 6074368 | tf_op jit(solution)/shard_map/dot_general | solution.py:250
  104.8 2.2 fusion.61
  108.1 64.4 %while.16 = (s32[]{:T(128)}, f32[1,4,512]{2,1,0:T(4,128)S(1)}, f32[1,4,512]{2,1,0:T(4,128)S(1)}, f32[1,4,512,80]{2,3,1,0:T(8,128)}, pred[8,4]{1,0:T(8,128)(4,1)S...) while((s32[]{:T(128)}, f32[1,4,512]{2,1,0:T(4,128)S(1)}, ...), condition=%wide.region_14.15_spmd.clone.clone, body=%wide.region_11.14_spmd.clone.clone.sunk | while | flops 351253504 | bytes 20842768 | solution.py:319
  113.1 2.3 fusion.129
  121.2 2.3 fusion.129
  129.2 2.3 fusion.129
  137.2 2.3 fusion.129
  145.2 2.3 fusion.129
  153.3 2.3 fusion.129
  161.3 2.3 fusion.129
  169.3 2.3 fusion.129
  173.7 3.0 convolution_convert_fusion.1
  176.7 69.2 %sum_middle.1 = (bf16[512,2560]{1,0:T(8,128)(2,1)}, bf16[512,2560]{1,0:T(8,128)(2,1)}) custom-call(bf16[8,64,2560]{2,1,0:T(8,128)(2,1)} %bitcast.213, bf16[512,2560]{1,0:T(8,128)(2,1)} %token_ref.1, f32[1,2560]{1,0:T(1,128)} %reshape.452.gain_ref), custom_call_target="tpu_custom_call" | custom-call | tf_op jit(solution)/shard_map/sum_middle/pallas_call | solution.py:168
  245.9 4.4 %copy.48 = bf16[512,2560]{0,1:T(8,128)(2,1)} copy(bf16[512,2560]{1,0:T(8,128)(2,1)} %get-tuple-element.75) | data formatting | bytes 5242880 | tf_op jit(solution)/shard_map/sum_middle/pallas_call | solution.py:168
  250.3 8.5 %fusion.105 = f32[512,1728]{0,1:T(8,128)S(1)} fusion(bf16[512,2560]{1,0:T(8,128)(2,1)} %get-tuple-element.76, bf16[2560,1728]{1,0:T(8,128)(2,1)} %all-gather.5.cloned.1.call-done), kind=kOutput, calls=%fused_computation.151 | convolution fusion | flops 4529848320 | bytes 15007744 | tf_op jit(solution)/shard_map/dot_general | solution.py:330
  258.9 4.5 %fusion.47 = bf16[2560,512]{0,1:T(8,128)(2,1)} fusion(bf16[864,2560]{1,0:T(8,128)(2,1)S(1)} %bitcast.225, f32[512,1728]{0,1:T(8,128)S(1)} %fusion.105), kind=kOutput, calls=%fused_computation.56 | convolution fusion | flops 2268889088 | bytes 10584064 | tf_op jit(solution)/shard_map/dot_general | solution.py:333
  263.4 4.4 %copy.49 = bf16[2560,512]{1,0:T(8,128)(2,1)} copy(bf16[2560,512]{0,1:T(8,128)(2,1)} %fusion.47) | data formatting | bytes 5242880 | tf_op jit(solution)/shard_map/convert_element_type | solution.py:335
  267.8 35.2 %sum_scatter.1 = f32[320,512]{1,0:T(8,128)} custom-call(bf16[8,320,512]{2,1,0:T(8,128)(2,1)} %bitcast.211), custom_call_target="tpu_custom_call" | custom-call | tf_op jit(solution)/shard_map/sum_scatter/pallas_call | solution.py:198
  (204 shorter events, 74.4 us)
Async XLA Ops:
  6.5 167.1 %copy-start = (bf16[320,2560]{1,0:T(8,128)(2,1)S(1)}, bf16[320,2560]{1,0:T(8,128)(2,1)}, u32[]{:S(2)}) copy-start(bf16[320,2560]{1,0:T(8,128)(2,1)} %param.24) | copy-start | bytes 4915204
  6.5 92.7 %all-gather.3.cloned.1.call-start = ((), (), s32[]{:S(2)}) async-start(), calls=%async_computation.2 | async-start | bytes 2785280 | tf_op jit(solution)/shard_map/all_gather | solution.py:234
  12.0 27.8 %copy-start.6 = (s32[128]{0:T(128)S(1)}, s32[128]{0:T(128)}, u32[]{:S(2)}) copy-start(s32[128]{0:T(128)} %param.27) | copy-start | bytes 1540
  13.1 27.6 %copy-start.1 = (bf16[2,8,1,80,128]{4,3,2,1,0:T(8,128)(2,1)S(1)}, bf16[2,8,1,80,128]{4,3,2,1,0:T(8,128)(2,1)}, u32[]{:S(2)}) copy-start(bf16[2,8,1,80,128]{4,3,2,1,0:T(8,128)(2,1)} %param.26) | copy-start | bytes 983044
  39.0 1.7 copy-start.2
  39.7 11.9 %copy-start.8 = (s32[16]{0:T(128)S(1)}, s32[16]{0:T(128)}, u32[]{:S(2)}) copy-start(s32[16]{0:T(128)} %param.29) | copy-start | bytes 196
  39.7 12.6 %copy-start.9 = (s32[16]{0:T(128)S(1)}, s32[16]{0:T(128)}, u32[]{:S(2)}) copy-start(s32[16]{0:T(128)} %param.28) | copy-start | bytes 196
  40.0 14.9 %copy-start.5 = (f32[2560]{0:T(1024)S(1)}, f32[2560]{0:T(1024)}, u32[]{:S(2)}) copy-start(f32[2560]{0:T(1024)} %param.18) | copy-start | bytes 30724
  43.0 30.5 %all-to-all-start.1 = ((bf16[2,32,1,80,128]{4,3,0,2,1:T(8,128)(2,1)}), bf16[2,32,1,80,128]{4,3,0,2,1:T(8,128)(2,1)S(1)}, u32[]{:S(2)}, u32[]{:S(2)}) async-start(bf16[2,32,1,80,128]{4,3,0,2,1:T(8,128)(2,1)} %fusion.60), calls=%async_computation.1 | async-start | bytes 2621440 | tf_op jit(solution)/shard_map/all_to_all | solution.py:287
  51.6 47.6 %copy-start.7 = (f32[2560]{0:T(1024)S(1)}, f32[2560]{0:T(1024)}, u32[]{:S(2)}) copy-start(f32[2560]{0:T(1024)} %param.17) | copy-start | bytes 30724
  51.6 125.1 %all-gather.5.cloned.1.call-start = ((), (), s32[]{:S(2)}) async-start(), calls=%async_computation.3 | async-start | bytes 9748480 | tf_op jit(solution)/shard_map/all_gather | solution.py:235
  110.1 3.0 copy-start.3
  115.5 0.9 copy-start.4
  118.2 3.0 copy-start.3
  126.2 3.0 copy-start.3
  131.5 0.9 copy-start.4
  134.2 3.0 copy-start.3
  139.6 0.9 copy-start.4
  142.3 3.0 copy-start.3
  150.3 3.0 copy-start.3
  158.3 3.0 copy-start.3
  166.3 3.0 copy-start.3
  245.9 13.0 %slice-start = ((s8[4423680]{0:T(1024)(128)(4,1)}), s8[229376]{0:T(1024)(128)(4,1)S(1)}, s32[]{:S(2)}) async-start(s8[4423680]{0:T(1024)(128)(4,1)} %bitcast.224), calls=%async_computation.4 | async-start | bytes 458752
  250.3 8.5 %slice-start.1 = ((s8[4423680]{0:T(1024)(128)(4,1)}), s8[4194304]{0:T(1024)(128)(4,1)S(1)}, s32[]{:S(2)}) async-start(s8[4423680]{0:T(1024)(128)(4,1)} %bitcast.224), calls=%async_computation.5 | async-start | bytes 8388608
  (5 other events, 4.3 us)
Sparse Core Ops, SparseCore 0:
  39.9 59.2 all-gather.2
  101.6 74.8 all-gather.4

commit v3 on v2

--- a/solution.py
+++ b/solution.py
@@ -57,27 +57,6 @@
     return (global_rank, local_rank)
 
 
-def visible(query_pos, key_pos):
-    distance = query_pos - key_pos
-    return (distance >= 0) & ((distance < WINDOW) | (key_pos < SINKS))
-
-
-def partial_block(scores, seen_mask):
-    masked = jnp.where(seen_mask, scores, FLOOR_SCORE)
-    row_max = jnp.max(masked, axis=-1)
-    weights = jnp.where(seen_mask, jnp.exp(masked - row_max[..., None]), 0.0)
-    return (row_max, jnp.sum(weights, axis=-1), weights.astype(jnp.bfloat16))
-
-
-def combine(first_part, second_part):
-    maxima = jnp.maximum(first_part[0], second_part[0])
-    scale_first = jnp.exp(first_part[0] - maxima)
-    scale_second = jnp.exp(second_part[0] - maxima)
-    totals = first_part[1] * scale_first + second_part[1] * scale_second
-    outputs = first_part[2] * scale_first[..., None] + second_part[2] * scale_second[..., None]
-    return (maxima, totals, outputs)
-
-
 def pack_groups(matrices, groups):
     rows = matrices[0].shape[0]
     pieces = [
@@ -91,6 +70,149 @@
 
 MESH = pl.DeviceIdType.MESH
 VMEM_SPEC = pl.BlockSpec(memory_space=pltpu.VMEM)
+
+
+LIFT = 1.0 / math.sqrt(HD) * math.log2(math.e)
+
+
+def attention_kernel(
+    scalars, query_ref, own_key_ref, own_value_ref, blocks_ref, out_ref,
+    keys, values, score_a, score_b, row_max, summed,
+):
+    slots, block = blocks_ref.shape[0], blocks_ref.shape[3]
+    rows = query_ref.shape[2]
+    depth = keys.shape[1]
+    wide = values.shape[0]
+    chunk = rows
+    per_chunk = chunk // block
+    chunks = slots // per_chunk
+    before, live_rows = scalars[2 * slots], scalars[2 * slots + 1]
+
+    def padded_key(part, limit):
+        spots = lax.broadcasted_iota(jnp.int32, (depth - HD, block), 1)
+        lines = lax.broadcasted_iota(jnp.int32, (depth - HD, block), 0)
+        bias = jnp.where((lines == 0) & (spots >= limit), FLOOR_SCORE, 0.0)
+        return jnp.concatenate([part.astype(jnp.float32), bias], axis=0).T.astype(jnp.bfloat16)
+
+    @pl.when(pl.program_id(0) == 0)
+    def _():
+        ones = jnp.ones((wide - HD, block), jnp.bfloat16)
+
+        def place(slot, carry):
+            limit = jnp.where(
+                scalars[slots + slot] > 0, before - scalars[slot] * block, 0
+            )
+            spot = pl.multiple_of(slot * block, block)
+            keys[pl.ds(spot, block), :] = padded_key(blocks_ref[slot, 0], limit)
+            values[:, pl.ds(spot, block)] = jnp.concatenate([blocks_ref[slot, 1], ones], axis=0)
+            return carry
+
+        lax.fori_loop(0, slots, place, 0)
+        for part in range(rows // block):
+            near = slice(part * block, (part + 1) * block)
+            far = slice(slots * block + part * block, slots * block + (part + 1) * block)
+            keys[far, :] = padded_key(own_key_ref[:, near], live_rows - part * block)
+            values[:, far] = jnp.concatenate([own_value_ref[:, near], ones], axis=0)
+
+    query = jnp.concatenate(
+        [
+            query_ref[0].astype(jnp.float32),
+            jnp.ones((16, rows), jnp.float32),
+            jnp.zeros((depth - HD - 16, rows), jnp.float32),
+        ],
+        axis=0,
+    ).astype(jnp.bfloat16)
+
+    def score(index, into):
+        spot = pl.multiple_of(index * chunk, chunk)
+        into[...] = jnp.dot(keys[pl.ds(spot, chunk), :], query, preferred_element_type=jnp.float32)
+
+    def window(index, into):
+        near = before + rows - WINDOW
+        needed = False
+        for part in range(per_chunk):
+            needed |= scalars[index * per_chunk + part] * block < near
+
+        @pl.when(needed)
+        def _():
+            for part in range(per_chunk):
+                lines = slice(part * block, (part + 1) * block)
+                place = scalars[index * per_chunk + part] * block + lax.broadcasted_iota(
+                    jnp.int32, (block, rows), 0
+                )
+                away = before - place + lax.broadcasted_iota(jnp.int32, (block, rows), 1)
+                seen = (away < WINDOW) | (place < SINKS)
+                into[lines, :] = jnp.where(seen, into[lines, :], FLOOR_SCORE)
+
+    def absorb(index, held):
+        spot = pl.multiple_of(index * chunk, chunk)
+        now = held[...]
+        largest = jnp.maximum(row_max[...], jnp.max(now, axis=0, keepdims=True))
+        fade = jnp.exp2((row_max[...] - largest) * LIFT)
+        weights = jnp.exp2((now - largest) * LIFT).astype(jnp.bfloat16)
+        row_max[...] = largest
+        summed[...] = summed[...] * fade + jnp.dot(
+            values[:, pl.ds(spot, chunk)], weights, preferred_element_type=jnp.float32
+        )
+
+    score(chunks, score_b)
+    causal = lax.broadcasted_iota(jnp.int32, (rows, rows), 0) <= lax.broadcasted_iota(
+        jnp.int32, (rows, rows), 1
+    )
+    score_b[...] = jnp.where(causal, score_b[...], FLOOR_SCORE)
+    row_max[...] = jnp.full_like(row_max, FLOOR_SCORE)
+    summed[...] = jnp.zeros_like(summed)
+    score(0, score_a)
+    absorb(chunks, score_b)
+    window(0, score_a)
+
+    def pair(step, carry):
+        first = step * 2
+        score(first + 1, score_b)
+        absorb(first, score_a)
+        window(first + 1, score_b)
+        later = lax.rem(first + 2, chunks)
+        score(later, score_a)
+        absorb(first + 1, score_b)
+        window(later, score_a)
+        return carry
+
+    lax.fori_loop(0, chunks // 2, pair, 0)
+    out_ref[0] = (summed[:HD, :] / summed[HD : HD + 1, :]).astype(jnp.bfloat16)
+
+
+def attend(scalars, query, own_key, own_value, blocks):
+    heads, width, rows = query.shape
+    slots, block = blocks.shape[0], blocks.shape[3]
+    span = slots * block + rows
+    whole = pl.BlockSpec(memory_space=pltpu.VMEM)
+    return pl.pallas_call(
+        attention_kernel,
+        name="attend",
+        grid=(heads,),
+        out_shape=jax.ShapeDtypeStruct((heads, width, rows), jnp.bfloat16),
+        in_specs=[
+            pl.BlockSpec(memory_space=pltpu.SMEM),
+            pl.BlockSpec((1, width, rows), lambda head: (head, 0, 0)),
+            whole,
+            whole,
+            whole,
+        ],
+        out_specs=pl.BlockSpec((1, width, rows), lambda head: (head, 0, 0)),
+        scratch_shapes=[
+            pltpu.VMEM((span, 128), jnp.bfloat16),
+            pltpu.VMEM((96, span), jnp.bfloat16),
+            pltpu.VMEM((rows, rows), jnp.float32),
+            pltpu.VMEM((rows, rows), jnp.float32),
+            pltpu.VMEM((1, rows), jnp.float32),
+            pltpu.VMEM((96, rows), jnp.float32),
+        ],
+        cost_estimate=pl.CostEstimate(
+            flops=4 * heads * rows * span * 128,
+            bytes_accessed=span * 4 * width,
+            transcendentals=heads * rows * span,
+        ),
+    )(scalars, query, own_key, own_value, blocks)
 
 
 def greet(n, me):
@@ -168,6 +290,7 @@
     return pl.pallas_call(
         functools.partial(middle_kernel, n),
         name="sum_middle",
+        cost_estimate=pl.CostEstimate(flops=0, bytes_accessed=200_000_000, transcendentals=0),
         out_shape=(whole_shape, whole_shape),
         in_specs=[VMEM_SPEC] * 3,
         out_specs=(VMEM_SPEC, VMEM_SPEC),
@@ -236,16 +359,13 @@
     query_width = w_query.shape[1] // groups
     key_width = w_key.shape[1] // groups
     kv_local = key_width // HD
-    per_group = HEADS // KV_HEADS
     new_rows = tokens.shape[0]
     prompts = prefix_len.shape[0]
     slots = cache.shape[1]
-    score_scale = 1.0 / math.sqrt(HD)
     prefix_here = prefix_len[blk_index]
     live_count = new_len[blk_index]
     row_ids = jnp.arange(new_rows, dtype=jnp.int32)
     positions = prefix_here + row_ids
-    offsets = jnp.arange(BLOCK, dtype=jnp.int32)
     normed = rms_scale(tokens, attn_gain)
     projected = jnp.dot(normed, w_qkv, preferred_element_type=jnp.float32)
     queries = rotate(projected[:, :query_width].reshape(new_rows, -1, HD), positions).astype(
@@ -258,17 +378,6 @@
     value_new = (
         projected[:, query_width + key_width :].reshape(new_rows, kv_local, HD).astype(jnp.bfloat16)
     )
-    grouped_q = queries.reshape(new_rows, kv_local, per_group, HD)
-    own_scores = (
-        jnp.einsum("qgnd,kgd->gnqk", grouped_q, key_new, preferred_element_type=jnp.float32)
-        * score_scale
-    )
-    own_mask = (row_ids[None, :] < live_count) & visible(positions[:, None], positions[None, :])
-    own_max, own_sum, own_weights = partial_block(own_scores, own_mask)
-    own_out = jnp.einsum(
-        "gnqk,kgd->gnqd", own_weights, value_new, preferred_element_type=jnp.float32
-    )
-    running = (own_max, own_sum, own_out)
     global_rank, local_rank = slot_ranks(slot_prompt, prompts, slots)
     own_prompts = lax.dynamic_slice_in_dim(slot_prompt, blk_index * slots, slots)
     own_ranks = lax.dynamic_slice_in_dim(local_rank, blk_index * slots, slots)
@@ -291,41 +400,21 @@
     received = (landing[None, :] == buffer_ids[:, None]) & for_me[None, :]
     block_number = jnp.sum(jnp.where(received, global_rank[None, :], 0), axis=1)
     block_live = jnp.any(received, axis=1)
-    total_slots = prompts * CAP
-    group_slots = min(total_slots, max(1, 512 // BLOCK))
-    step_count = total_slots // group_slots
-    key_blocks = arrived[0].reshape(step_count, group_slots, kv_local, HD, BLOCK)
-    value_blocks = arrived[1].reshape(step_count, group_slots, kv_local, HD, BLOCK)
-    numbers = block_number.reshape(step_count, group_slots)
-    live_flags = block_live.reshape(step_count, group_slots)
-
-    def prefix_step(running_state, inputs):
-        key_part, value_part, number_part, flag_part = inputs
-        scores = (
-            jnp.einsum("qgnd,sgdt->gnqst", grouped_q, key_part, preferred_element_type=jnp.float32)
-            * score_scale
-        )
-        scores = scores.reshape(kv_local, per_group, new_rows, group_slots * BLOCK)
-        key_pos = number_part[:, None] * BLOCK + offsets[None, :]
-        key_live = (flag_part[:, None] & (key_pos < prefix_here)).reshape(-1)
-        seen_mask = key_live[None, :] & visible(positions[:, None], key_pos.reshape(-1)[None, :])
-        block_max, block_sum, weights = partial_block(scores, seen_mask)
-        weights = weights.reshape(kv_local, per_group, new_rows, group_slots, BLOCK)
-        block_out = jnp.einsum(
-            "gnqst,sgdt->gnqd", weights, value_part, preferred_element_type=jnp.float32
-        )
-        return (combine(running_state, (block_max, block_sum, block_out)), None)
-
-    running = lax.scan(prefix_step, running, (key_blocks, value_blocks, numbers, live_flags))[0]
-    totals = running[1]
-    outputs = running[2]
-    attended = (
-        jnp.transpose(outputs / totals[..., None], (2, 0, 1, 3))
-        .reshape(new_rows, -1)
-        .astype(jnp.bfloat16)
-    )
-    projected_out = jnp.dot(attended, w_out, preferred_element_type=jnp.float32)
-    partial_out, w_pair = lax.optimization_barrier((projected_out.astype(jnp.bfloat16), w_pair))
+    blocks = jnp.transpose(arrived, (1, 2, 0, 3, 4)).reshape(prompts * CAP, 2, HD, BLOCK)
+    scalars = jnp.concatenate(
+        [block_number, block_live.astype(jnp.int32), jnp.stack([prefix_here, live_count])]
+    )
+    attended = attend(
+        scalars,
+        jnp.transpose(queries, (1, 2, 0)),
+        key_new.reshape(new_rows, HD).T,
+        value_new.reshape(new_rows, HD).T,
+        blocks,
+    ).reshape(-1, new_rows)
+    projected_out = lax.dot_general(
+        attended, w_out, (((0,), (0,)), ((), ())), preferred_element_type=jnp.float32
+    )
+    partial_out = projected_out.astype(jnp.bfloat16)
     middle, normed_mid = sum_middle(groups, partial_out, tokens, mlp_gain)
     paired = jnp.dot(normed_mid, w_pair, preferred_element_type=jnp.float32)
     hidden_width = w_pair.shape[1] // 2

time: 313 us -> 289 us (0.923)
  Pallas kernels: 104 us -> 149 us
  matrix products: 56.7 us -> 21.3 us
  other arithmetic: 41.6 us -> 16.5 us
  local copies, waits for them, and re-layouts: 30.3 us -> 20.4 us
    pallas_call x1 -> x2, Pallas kernels: 69.2 us -> 113 us  [the longest x1 91.8 us: sum_middle(): pl.pallas_call(functools.partial(middle_kernel, n), name='sum_middle', co...]
    dot_general x19 -> x1, matrix products: 39.6 us -> 4.02 us  [shards(): lax.dot_general(attended, w_out, (((0,), (0,)), ((), ())), preferred_elem...]
    all_gather x1, waiting for transfers between devices: 24.5 us -> 38.3 us  [shards(): w_qkv = lax.all_gather(mine[:, :attn_width], 'blk', axis=0, tiled=True)]
    all_to_all x1, waiting for transfers between devices: 11.3 us -> 0.01 us  [shards(): lax.all_to_all(outgoing, 'blk', split_axis=1, concat_axis=1, tiled=True)]
    and x17 -> x0, other arithmetic: 9.42 us -> none  [the longest x8 5.65 us: prefix_step(): key_live = (flag_part[:, None] & (key_pos < prefix_here)).reshape(-1)]
    reduce_sum x9 -> x0, other arithmetic: 9.39 us -> none  [partial_block(): return (row_max, jnp.sum(weights, axis=-1), weights.astype(jnp.bfloat16))]
    while x40 -> x0, local copies, waits for them, and re-layouts: 6.81 us -> none
    add x17 -> x0, other arithmetic: 6.29 us -> none  [the longest x9 5.72 us: shards(): positions = prefix_here + row_ids]
  transfers between devices with their start and end apart: 3 -> 3, of which waited for: 2 -> 1; matrix products, arithmetic and copies ran while one was open for 27% -> 10% of each run, Pallas kernels for 0% -> 39%
where the time goes in v3:
time: 289 us; the launch traced here: 288 us
  Pallas kernels  149 us (52%)
  waiting for transfers between devices  38.4 us (13%)
  matrix products  21.3 us (7%)
  local copies, waits for them, and re-layouts  20.4 us (7%)
  blocking collectives  20 us (7%)
  other arithmetic  16.5 us (6%)
  between operations  13.7 us (5%)
  starting transfers between devices  8.76 us (3%)
    pallas_call x1, Pallas kernels, sum_middle(): pl.pallas_call(functools.partial(middle_kernel, n), name='sum_middle', co...  91.8 us
    all_gather x1, waiting for transfers between devices, shards(): w_qkv = lax.all_gather(mine[:, :attn_width], 'blk', axis=0, tiled=True)  38.3 us
    pallas_call x1, Pallas kernels, sum_scatter(): pl.pallas_call(functools.partial(scatter_kernel, n), name='sum_scatter',...  35.4 us
    pallas_call x1, Pallas kernels, attend(): pl.pallas_call(attention_kernel, name='attend', grid=(heads,), out_shape=...  21.6 us
    all_to_all x1, blocking collectives, shards(): mine = lax.all_to_all(packed, 'kv', split_axis=0, concat_axis=0, tiled=True)  20 us
    all_to_all x1, starting transfers between devices, shards(): lax.all_to_all(outgoing, 'blk', split_axis=1, concat_axis=1, tiled=True)  8.72 us
    dot_general x1, matrix products, shards(): paired = jnp.dot(normed_mid, w_pair, preferred_element_type=jnp.float32)  8.49 us
  transfers between devices with their start and end apart: 3, of which 1 were waited for; matrix products, arithmetic and copies ran while one was open for 10% of the time, Pallas kernels for 39%

profile of v3, /device:TPU:1, one launch (start us, length us, event | category | flops | bytes accessed | tf_op | source)
XLA Modules:
  0.0 287.9 jit_solution(2685260101930407376)
XLA Ops:
  6.5 1.0 convert_element_type.69
  7.6 0.8 convert_element_type.70
  8.6 1.0 convert_element_type.68
  10.4 1.1 convert_element_type.71
  12.7 1.5 concatenate.22
  14.3 20.0 %all_to_all.10 = bf16[8,20,2208]{2,1,0:T(8,128)(2,1)} all-to-all(bf16[8,20,2208]{2,1,0:T(8,128)(2,1)S(1)} %concatenate.22), channel_id=1, replica_groups=mesh['blk'=16,'kv'=8] {'kv'}, dimensions={0} | all-to-all | bytes 1413120 | tf_op jit(solution)/shard_map/all_to_all | solution.py:355
  34.3 1.5 reshape.253
  36.6 1.0 slice.55
  39.5 1.4 fusion.9
  40.9 8.7 %all-to-all-start.1 = ((bf16[2,32,1,80,128]{4,3,0,2,1:T(8,128)(2,1)}), bf16[2,32,1,80,128]{4,3,0,2,1:T(8,128)(2,1)S(1)}, u32[]{:S(2)}, u32[]{:S(2)}) async-start(bf16[2,32,1,80,128]{4,3,0,2,1:T(8,128)(2,1)} %fusion.9), calls=%async_computation.1 | async-start | bytes 2621440 | tf_op jit(solution)/shard_map/all_to_all | solution.py:396
  52.8 1.8 pad_add_fusion.scalars
  55.3 2.3 fusion
  58.0 38.3 %all-gather.3.cloned.1.call-done = bf16[2560,480]{1,0:T(8,128)(2,1)} async-done(((bf16[160,480]{1,0:T(8,128)(2,1)}), bf16[2560,480]{1,0:T(8,128)(2,1)}) %all-gather.3.cloned.1.call-update) | async-done | bytes 2457616 | tf_op jit(solution)/shard_map/all_gather | solution.py:357
  96.3 4.1 %fusion.4 = f32[512,480]{0,1:T(8,128)S(1)} fusion(bf16[2560,480]{1,0:T(8,128)(2,1)} %all-gather.3.cloned.1.call-done, bf16[512,2560]{1,0:T(8,128)(2,1)} %token_ref.1, f32[2560]{0:T(1024)S(1)} %copy-done.6, f32[512]{0:T(512)S(1)} %add_rsqrt_fusion), kind=kOutput, calls=%fused_computation.9 | convolution fusion | flops 1263534080 | bytes 6074368 | tf_op jit(solution)/shard_map/dot_general | solution.py:370
  103.0 1.1 copy-done.2
  104.1 21.6 %attend.1 = bf16[4,80,512]{2,1,0:T(8,128)(2,1)} custom-call(s32[66]{0:T(128)} %pad_add_fusion.scalars, bf16[4,80,512]{2,1,0:T(8,128)(2,1)} %maximum_bitcast_fusion.query_ref, bf16[80,512]{1,0:T(8,128)(2,1)} %maximum_bitcast_fusion.1.own_key_ref, bf16[80,512]{1,0:T(8,128)(2,1)} %fusion.22.own_value_ref, bf16[32,2,80,128]{3,2,1,0:T(8,128)(2,1)} %bitcast.63), custom_call_target="tpu_custom_call" | custom-call | flops 4831838208 | bytes 1474560 | tf_op jit(solution)/shard_map/attend/pallas_call | solution.py:189
  125.7 4.0 %convolution_convert_fusion.1 = bf16[512,2560]{1,0:T(8,128)(2,1)} fusion(bf16[320,512]{1,0:T(8,128)(2,1)} %bitcast.67, bf16[320,2560]{1,0:T(8,128)(2,1)S(1)} %copy-done), kind=kOutput, calls=%fused_computation.7 | convolution fusion | flops 840171520 | bytes 4587520 | tf_op jit(solution)/shard_map/dot_general | solution.py:414
  129.8 91.8 %sum_middle.1 = (bf16[512,2560]{1,0:T(8,128)(2,1)}, bf16[512,2560]{1,0:T(8,128)(2,1)}) custom-call(bf16[8,64,2560]{2,1,0:T(8,128)(2,1)} %bitcast.61, bf16[512,2560]{1,0:T(8,128)(2,1)} %token_ref.1, f32[1,2560]{1,0:T(1,128)} %reshape.259.gain_ref), custom_call_target="tpu_custom_call" | custom-call | bytes 200000000 | tf_op jit(solution)/shard_map/sum_middle/pallas_call | solution.py:290
  221.6 4.5 %copy.38 = bf16[512,2560]{0,1:T(8,128)(2,1)} copy(bf16[512,2560]{1,0:T(8,128)(2,1)} %get-tuple-element.7) | data formatting | bytes 5242880 | tf_op jit(solution)/shard_map/sum_middle/pallas_call | solution.py:290
  226.0 8.5 %fusion.34 = f32[512,1728]{0,1:T(8,128)S(1)} fusion(bf16[512,2560]{1,0:T(8,128)(2,1)} %get-tuple-element.8, bf16[2560,1728]{1,0:T(8,128)(2,1)} %all-gather.5.cloned.1.call-done), kind=kOutput, calls=%fused_computation.78 | convolution fusion | flops 4529848320 | bytes 15007744 | tf_op jit(solution)/shard_map/dot_general | solution.py:419
  234.5 4.7 %fusion.3 = bf16[2560,512]{0,1:T(8,128)(2,1)} fusion(bf16[864,2560]{1,0:T(8,128)(2,1)S(1)} %bitcast.66, f32[512,1728]{0,1:T(8,128)S(1)} %fusion.34), kind=kOutput, calls=%fused_computation.8 | convolution fusion | flops 2268889088 | bytes 10584064 | tf_op jit(solution)/shard_map/dot_general | solution.py:422
  239.3 4.4 %copy.39 = bf16[2560,512]{1,0:T(8,128)(2,1)} copy(bf16[2560,512]{0,1:T(8,128)(2,1)} %fusion.3) | data formatting | bytes 5242880 | tf_op jit(solution)/shard_map/convert_element_type | solution.py:424
  243.7 35.4 %sum_scatter.1 = f32[320,512]{1,0:T(8,128)} custom-call(bf16[8,320,512]{2,1,0:T(8,128)(2,1)} %bitcast.59), custom_call_target="tpu_custom_call" | custom-call | tf_op jit(solution)/shard_map/sum_scatter/pallas_call | solution.py:321
  279.0 2.0 fusion.13
  (73 shorter events, 11.6 us)
Async XLA Ops:
  6.5 119.2 %copy-start = (bf16[320,2560]{1,0:T(8,128)(2,1)S(1)}, bf16[320,2560]{1,0:T(8,128)(2,1)}, u32[]{:S(2)}) copy-start(bf16[320,2560]{1,0:T(8,128)(2,1)} %param.22) | copy-start | bytes 4915204
  6.5 5.5 %copy-start.3 = (f32[20,6912]{1,0:T(8,128)S(1)}, f32[20,6912]{1,0:T(8,128)}, u32[]{:S(2)}) copy-start(f32[20,6912]{1,0:T(8,128)} %param.21) | copy-start | bytes 1658884
  6.5 89.8 %all-gather.3.cloned.1.call-start = ((), (), s32[]{:S(2)}) async-start(), calls=%async_computation.2 | async-start | bytes 2785280 | tf_op jit(solution)/shard_map/all_gather | solution.py:357
  14.2 23.4 %copy-start.5 = (s32[128]{0:T(128)S(1)}, s32[128]{0:T(128)}, u32[]{:S(2)}) copy-start(s32[128]{0:T(128)} %param.25) | copy-start | bytes 1540
  14.3 24.3 %copy-start.1 = (bf16[2,8,1,80,128]{4,3,2,1,0:T(8,128)(2,1)S(1)}, bf16[2,8,1,80,128]{4,3,2,1,0:T(8,128)(2,1)}, u32[]{:S(2)}) copy-start(bf16[2,8,1,80,128]{4,3,2,1,0:T(8,128)(2,1)} %param.24) | copy-start | bytes 983044
  36.5 189.5 %all-gather.5.cloned.1.call-start = ((), (), s32[]{:S(2)}) async-start(), calls=%async_computation.3 | async-start | bytes 9748480 | tf_op jit(solution)/shard_map/all_gather | solution.py:358
  39.5 10.1 %copy-start.7 = (s32[16]{0:T(128)S(1)}, s32[16]{0:T(128)}, u32[]{:S(2)}) copy-start(s32[16]{0:T(128)} %param.27) | copy-start | bytes 196
  39.5 10.7 %copy-start.8 = (s32[16]{0:T(128)S(1)}, s32[16]{0:T(128)}, u32[]{:S(2)}) copy-start(s32[16]{0:T(128)} %param.26) | copy-start | bytes 196
  39.5 11.3 %copy-start.4 = (f32[2560]{0:T(1024)S(1)}, f32[2560]{0:T(1024)}, u32[]{:S(2)}) copy-start(f32[2560]{0:T(1024)} %param.16) | copy-start | bytes 30724
  40.9 55.4 %copy-start.6 = (f32[2560]{0:T(1024)S(1)}, f32[2560]{0:T(1024)}, u32[]{:S(2)}) copy-start(f32[2560]{0:T(1024)} %param.15) | copy-start | bytes 30724
  40.9 62.1 %all-to-all-start.1 = ((bf16[2,32,1,80,128]{4,3,0,2,1:T(8,128)(2,1)}), bf16[2,32,1,80,128]{4,3,0,2,1:T(8,128)(2,1)S(1)}, u32[]{:S(2)}, u32[]{:S(2)}) async-start(bf16[2,32,1,80,128]{4,3,0,2,1:T(8,128)(2,1)} %fusion.9), calls=%async_computation.1 | async-start | bytes 2621440 | tf_op jit(solution)/shard_map/all_to_all | solution.py:396
  103.0 1.1 copy-start.2
  221.5 13.0 %slice-start = ((s8[4423680]{0:T(1024)(128)(4,1)}), s8[229376]{0:T(1024)(128)(4,1)S(1)}, s32[]{:S(2)}) async-start(s8[4423680]{0:T(1024)(128)(4,1)} %bitcast.65), calls=%async_computation.4 | async-start | bytes 458752
  226.0 8.5 %slice-start.1 = ((s8[4423680]{0:T(1024)(128)(4,1)}), s8[4194304]{0:T(1024)(128)(4,1)S(1)}, s32[]{:S(2)}) async-start(s8[4423680]{0:T(1024)(128)(4,1)} %bitcast.65), calls=%async_computation.5 | async-start | bytes 8388608
Sparse Core Ops, SparseCore 0:
  36.6 59.6 all-gather.2
  98.7 96.9 all-gather.4

commit v4 on v3

--- a/solution.py
+++ b/solution.py
@@ -70,6 +70,156 @@
 
 MESH = pl.DeviceIdType.MESH
 VMEM_SPEC = pl.BlockSpec(memory_space=pltpu.VMEM)
+
+
+def fan_out(step_count, make):
+    copies = [make(step) for step in range(1, step_count)]
+    for copy in copies:
+        copy.start()
+    return copies
+
+
+def regroup_kernel(
+    n_kv, n_blk, first_ref, second_ref, cache_ref, first_out, second_out, cache_out,
+    first_in, second_in, cache_in, whole, stage_a, stage_b,
+    first_send, first_recv, second_send, second_recv, cache_send, cache_recv, send, recv,
+):
+    me_kv, me = lax.axis_index("kv"), lax.axis_index("blk")
+    rows = first_ref.shape[1]
+    half, line, core = lax.div(me, 8), lax.rem(lax.div(me, 2), 4), lax.rem(me, 2)
+
+    barrier = pltpu.get_barrier_semaphore()
+    for axis, count, mine in (("kv", n_kv, me_kv), ("blk", n_blk, me)):
+        for step in range(1, count):
+            pl.semaphore_signal(
+                barrier, inc=1, device_id={axis: lax.rem(mine + step, count)}, device_id_type=MESH
+            )
+    pl.semaphore_wait(barrier, n_kv + n_blk - 2)
+
+    def swap(source, landing, sent, got):
+        def make(step):
+            peer = lax.rem(me_kv + step, n_kv)
+            return pltpu.make_async_remote_copy(
+                src_ref=source.at[peer],
+                dst_ref=landing.at[me_kv],
+                send_sem=sent.at[step - 1],
+                recv_sem=got.at[step - 1],
+                device_id={"kv": peer},
+                device_id_type=MESH,
+            )
+
+        return fan_out(n_kv, make)
+
+    def deal(step):
+        peer = lax.rem(me + step, n_blk)
+        return pltpu.make_async_remote_copy(
+            src_ref=cache_ref.at[peer],
+            dst_ref=cache_in.at[step - 1],
+            send_sem=cache_send.at[step - 1],
+            recv_sem=cache_recv.at[step - 1],
+            device_id={"blk": peer},
+            device_id_type=MESH,
+        )
+
+    firsts = swap(first_ref, first_in, first_send, first_recv)
+    seconds = swap(second_ref, second_in, second_send, second_recv)
+    deals = fan_out(n_blk, deal)
+
+    first_in[me_kv] = first_ref[me_kv]
+    for copy in firsts:
+        copy.wait_recv()
+    for group in range(n_kv):
+        stage_a[group * rows : (group + 1) * rows, :] = first_in[group].astype(jnp.float32)
+    whole[0] = stage_a[...].astype(jnp.bfloat16)
+
+    passed = {}
+
+    def pass_on(held, peer, slot):
+        copy = pltpu.make_async_remote_copy(
+            src_ref=whole.at[held],
+            dst_ref=whole.at[slot],
+            send_sem=send.at[slot - 1],
+            recv_sem=recv.at[slot - 1],
+            device_id={"blk": peer},
+            device_id_type=MESH,
+        )
+        copy.start()
+        passed[slot] = copy
+
+    def along(step):
+        return half * 8 + lax.rem(line + step, 4) * 2 + core
+
+    across = lax.rem(me + 8, n_blk)
+    sibling = me + 1 - 2 * core
+    pass_on(0, across, 8)
+    for step in (1, 3, 2):
+        pass_on(0, along(step), 2 * step)
+    pass_on(0, sibling, 1)
+    passed[8].wait_recv()
+    for step in (1, 3, 2):
+        pass_on(8, along(step), 8 + 2 * step)
+    pass_on(8, sibling, 9)
+
+    second_in[me_kv] = second_ref[me_kv]
+    for copy in seconds:
+        copy.wait_recv()
+    for group in range(n_kv):
+        stage_b[group * rows : (group + 1) * rows, :] = second_in[group].astype(jnp.float32)
+    second_out[...] = stage_b[...].astype(jnp.bfloat16)
+
+    for base in (0, 8):
+        for step in (1, 3, 2):
+            slot = base + 2 * step
+            passed[slot].wait_recv()
+            pass_on(slot, sibling, slot + 1)
+    for base in (0, 8):
+        for step in range(4):
+            for other in range(2):
+                slot = base + 2 * step + other
+                if other:
+                    passed[slot].wait_recv()
+                owner = (
+                    lax.rem(half + base // 8, 2) * 8
+                    + lax.rem(line + 4 - step, 4) * 2
+                    + lax.rem(core + other, 2)
+                )
+                first_out[owner] = whole[slot]
+    cache_out[me] = cache_ref[me]
+    for step in range(1, n_blk):
+        deals[step - 1].wait_recv()
+        cache_out[lax.rem(me + n_blk - step, n_blk)] = cache_in[step - 1]
+    for copy in firsts + seconds + deals + list(passed.values()):
+        copy.wait_send()
+
+
+def regroup(n_kv, n_blk, first, second, cached):
+    rows = first.shape[1]
+    tall = n_kv * rows
+    first_width, second_width = first.shape[2], second.shape[2]
+    half = jnp.bfloat16
+    dma = pltpu.SemaphoreType.DMA
+    return pl.pallas_call(
+        functools.partial(regroup_kernel, n_kv, n_blk),
+        name="regroup",
+        out_shape=(
+            jax.ShapeDtypeStruct((n_blk, tall, first_width), half),
+            jax.ShapeDtypeStruct((tall, second_width), half),
+            jax.ShapeDtypeStruct(cached.shape, half),
+        ),
+        in_specs=[VMEM_SPEC] * 3,
+        out_specs=(VMEM_SPEC,) * 3,
+        scratch_shapes=[
+            pltpu.VMEM(first.shape, half),
+            pltpu.VMEM(second.shape, half),
+            pltpu.VMEM((n_blk - 1,) + cached.shape[1:], half),
+            pltpu.VMEM((n_blk, tall, first_width), half),
+            pltpu.VMEM((tall, first_width), jnp.float32),
+            pltpu.VMEM((tall, second_width), jnp.float32),
+        ]
+        + [dma((n_kv - 1,))] * 4
+        + [dma((n_blk - 1,))] * 4,
+        compiler_params=pltpu.CompilerParams(collective_id=2, has_side_effects=True),
+    )(first, second, cached)
 
 
 LIFT = 1.0 / math.sqrt(HD) * math.log2(math.e)
@@ -350,12 +500,6 @@
     n_blocks = lax.axis_size("blk")
     blk_index = lax.axis_index("blk")
     kv_index = lax.axis_index("kv")
-    packed = pack_groups((w_query, w_key, w_value, w_gate, w_up), groups)
-    attn_width = (w_query.shape[1] + w_key.shape[1] + w_value.shape[1]) // groups
-    mine = lax.all_to_all(packed, "kv", split_axis=0, concat_axis=0, tiled=True)
-    mine = mine.reshape(-1, mine.shape[-1])
-    w_qkv = lax.all_gather(mine[:, :attn_width], "blk", axis=0, tiled=True)
-    w_pair = lax.all_gather(mine[:, attn_width:], "blk", axis=0, tiled=True)
     query_width = w_query.shape[1] // groups
     key_width = w_key.shape[1] // groups
     kv_local = key_width // HD
@@ -366,18 +510,6 @@
     live_count = new_len[blk_index]
     row_ids = jnp.arange(new_rows, dtype=jnp.int32)
     positions = prefix_here + row_ids
-    normed = rms_scale(tokens, attn_gain)
-    projected = jnp.dot(normed, w_qkv, preferred_element_type=jnp.float32)
-    queries = rotate(projected[:, :query_width].reshape(new_rows, -1, HD), positions).astype(
-        jnp.bfloat16
-    )
-    key_new = rotate(
-        projected[:, query_width : query_width + key_width].reshape(new_rows, kv_local, HD),
-        positions,
-    ).astype(jnp.bfloat16)
-    value_new = (
-        projected[:, query_width + key_width :].reshape(new_rows, kv_local, HD).astype(jnp.bfloat16)
-    )
     global_rank, local_rank = slot_ranks(slot_prompt, prompts, slots)
     own_prompts = lax.dynamic_slice_in_dim(slot_prompt, blk_index * slots, slots)
     own_ranks = lax.dynamic_slice_in_dim(local_rank, blk_index * slots, slots)
@@ -387,20 +519,36 @@
     source_slot = jnp.sum(
         jnp.where(matches, jnp.arange(slots, dtype=jnp.int32)[None, :], 0), axis=1
     )
-    filled = jnp.any(matches, axis=1)
-    outgoing = jnp.where(
-        filled[None, :, None, None, None],
-        jnp.take(cache, source_slot, axis=1),
-        jnp.zeros((), cache.dtype),
-    )
-    arrived = lax.all_to_all(outgoing, "blk", split_axis=1, concat_axis=1, tiled=True)
+    by_slot = jnp.transpose(cache.reshape(2, slots, HD, BLOCK), (1, 0, 2, 3))
+    outgoing = jnp.take(by_slot, source_slot, axis=0, mode="clip").reshape(prompts, CAP, 2, HD, BLOCK)
+    w_first, w_second, arrived = regroup(
+        groups,
+        n_blocks,
+        pack_groups((w_query, w_key, w_value), groups),
+        pack_groups((w_gate, w_up), groups),
+        outgoing,
+    )
+    w_qkv = w_first.reshape(-1, w_first.shape[2])
+    w_pair = lax.all_gather(w_second, "blk", axis=0, tiled=True)
+    normed = rms_scale(tokens, attn_gain)
+    projected = jnp.dot(normed, w_qkv, preferred_element_type=jnp.float32)
+    queries = rotate(projected[:, :query_width].reshape(new_rows, -1, HD), positions).astype(
+        jnp.bfloat16
+    )
+    key_new = rotate(
+        projected[:, query_width : query_width + key_width].reshape(new_rows, kv_local, HD),
+        positions,
+    ).astype(jnp.bfloat16)
+    value_new = (
+        projected[:, query_width + key_width :].reshape(new_rows, kv_local, HD).astype(jnp.bfloat16)
+    )
     slot_ids = jnp.arange(prompts * slots, dtype=jnp.int32)
     landing = slot_ids // slots * CAP + local_rank
     for_me = slot_prompt == blk_index
     received = (landing[None, :] == buffer_ids[:, None]) & for_me[None, :]
     block_number = jnp.sum(jnp.where(received, global_rank[None, :], 0), axis=1)
     block_live = jnp.any(received, axis=1)
-    blocks = jnp.transpose(arrived, (1, 2, 0, 3, 4)).reshape(prompts * CAP, 2, HD, BLOCK)
+    blocks = arrived.reshape(prompts * CAP, 2, HD, BLOCK)
     scalars = jnp.concatenate(
         [block_number, block_live.astype(jnp.int32), jnp.stack([prefix_here, live_count])]
     )

time: 289 us -> 264 us (0.913)
  Pallas kernels: 149 us -> 193 us
  waiting for transfers between devices: 38.4 us -> 0.04 us
  blocking collectives: 20 us -> 0 us
  starting transfers between devices: 8.76 us -> 0.01 us
  local copies, waits for them, and re-layouts: 20.4 us -> 15.7 us
    pallas_call x0 -> x1, Pallas kernels: none -> 52.4 us  [regroup(): pl.pallas_call(functools.partial(regroup_kernel, n_kv, n_blk), name='regr...]
    all_gather x2 -> x1, waiting for transfers between devices: 38.3 us -> 0.02 us  [shards(): w_pair = lax.all_gather(w_second, 'blk', axis=0, tiled=True)]
    all_to_all x1 -> x0, blocking collectives: 20 us -> none  [shards(): mine = lax.all_to_all(packed, 'kv', split_axis=0, concat_axis=0, tiled=True)]
    all_to_all x1 -> x0, starting transfers between devices: 8.72 us -> none  [shards(): lax.all_to_all(outgoing, 'blk', split_axis=1, concat_axis=1, tiled=True)]
    pallas_call x1, Pallas kernels: 91.8 us -> 84.2 us  [sum_middle(): pl.pallas_call(functools.partial(middle_kernel, n), name='sum_middle', co...]
  transfers between devices with their start and end apart: 3 -> 1, of which waited for: 1 -> 0; matrix products, arithmetic and copies ran while one was open for 10% -> 9% of each run, Pallas kernels for 39% -> 40%
where the time goes in v4:
time: 264 us; the launch traced here: 263 us
  Pallas kernels  193 us (73%)
  matrix products  22.4 us (8%)
  other arithmetic  17.6 us (7%)
  local copies, waits for them, and re-layouts  15.7 us (6%)
  between operations  13.6 us (5%)
    pallas_call x1, Pallas kernels, sum_middle(): pl.pallas_call(functools.partial(middle_kernel, n), name='sum_middle', co...  84.2 us
    pallas_call x1, Pallas kernels, regroup(): pl.pallas_call(functools.partial(regroup_kernel, n_kv, n_blk), name='regr...  52.4 us
    pallas_call x1, Pallas kernels, sum_scatter(): pl.pallas_call(functools.partial(scatter_kernel, n), name='sum_scatter',...  35 us
    pallas_call x1, Pallas kernels, attend(): pl.pallas_call(attention_kernel, name='attend', grid=(heads,), out_shape=...  21.6 us
    dot_general x1, matrix products, shards(): paired = jnp.dot(normed_mid, w_pair, preferred_element_type=jnp.float32)  8.37 us
    dot_general x1, matrix products, shards(): lax.dot_general(w_down, hidden, (((0,), (1,)), ((), ())), preferred_eleme...  6.66 us
  transfers between devices with their start and end apart: 1, of which 0 were waited for; matrix products, arithmetic and copies ran while one was open for 9% of the time, Pallas kernels for 40%

profile of v4, /device:TPU:1, one launch (start us, length us, event | category | flops | bytes accessed | tf_op | source)
XLA Modules:
  0.0 262.6 jit_solution(4253985318809963725)
XLA Ops:
  6.5 0.9 eq.55
  7.4 0.8 convert_element_type.69
  8.4 0.8 convert_element_type.70
  10.0 0.7 dynamic-slice_add_fusion
  10.8 1.0 convert_element_type.68
  12.0 1.1 convert_element_type.71
  14.3 1.1 pad_maximum_fusion.second_ref
  15.4 1.8 gather_fusion
  17.2 0.8 pad_maximum_fusion.1.first_ref
  18.0 52.4 %regroup.1 = (bf16[16,160,480]{2,1,0:T(8,128)(2,1)}, bf16[160,1728]{1,0:T(8,128)(2,1)}, bf16[16,2,2,80,128]{4,3,2,1,0:T(8,128)(2,1)}) custom-call(bf16[8,20,480]{2,1,0:T(8,128)(2,1)} %pad_maximum_fusion.1.first_ref, bf16[8,20,1728]{2,1,0:T(8,128)(2,1)} %pad_maximum_fusion.second_ref, bf16[16,2,2,80,128]{4,3,2,1,0:T(8,128)(2,1)} %bitcast.50), custom_call_target="tpu_custom_call" | custom-call | tf_op jit(solution)/shard_map/regroup/pallas_call | solution.py:201
  72.7 2.5 fusion
  75.2 3.3 %fusion.4 = f32[512,480]{0,1:T(8,128)S(1)} fusion(bf16[2560,480]{1,0:T(8,128)(2,1)} %bitcast.55, bf16[512,2560]{1,0:T(8,128)(2,1)S(1)} %copy-done.1, f32[2560]{0:T(1024)S(1)} %copy-done.6, f32[512]{0:T(512)S(1)} %add_rsqrt_fusion), kind=kOutput, calls=%fused_computation.9 | convolution fusion | flops 1263534080 | bytes 6074368 | tf_op jit(solution)/shard_map/dot_general | solution.py:534
  78.9 1.9 pad_add_fusion.scalars
  80.8 0.7 add_convert_fusion.1
  82.9 0.8 maximum_bitcast_fusion.query_ref
  84.3 21.6 %attend.1 = bf16[4,80,512]{2,1,0:T(8,128)(2,1)} custom-call(s32[66]{0:T(128)} %pad_add_fusion.scalars, bf16[4,80,512]{2,1,0:T(8,128)(2,1)} %maximum_bitcast_fusion.query_ref, bf16[80,512]{1,0:T(8,128)(2,1)} %maximum_bitcast_fusion.1.own_key_ref, bf16[80,512]{1,0:T(8,128)(2,1)} %fusion.21.own_value_ref, bf16[32,2,80,128]{3,2,1,0:T(8,128)(2,1)} %bitcast.56), custom_call_target="tpu_custom_call" | custom-call | flops 4831838208 | bytes 1474560 | tf_op jit(solution)/shard_map/attend/pallas_call | solution.py:339
  106.0 4.0 %convolution_convert_fusion.1 = bf16[512,2560]{1,0:T(8,128)(2,1)} fusion(bf16[320,512]{1,0:T(8,128)(2,1)} %bitcast.57, bf16[320,2560]{1,0:T(8,128)(2,1)S(1)} %copy-done), kind=kOutput, calls=%fused_computation.7 | convolution fusion | flops 840171520 | bytes 4587520 | tf_op jit(solution)/shard_map/dot_general | solution.py:562
  110.0 84.2 %sum_middle.1 = (bf16[512,2560]{1,0:T(8,128)(2,1)}, bf16[512,2560]{1,0:T(8,128)(2,1)}) custom-call(bf16[8,64,2560]{2,1,0:T(8,128)(2,1)} %bitcast.52, bf16[512,2560]{1,0:T(8,128)(2,1)} %token_ref.1, f32[1,2560]{1,0:T(1,128)} %reshape.234.gain_ref), custom_call_target="tpu_custom_call" | custom-call | bytes 200000000 | tf_op jit(solution)/shard_map/sum_middle/pallas_call | solution.py:440
  194.2 4.4 %copy.29 = bf16[512,2560]{0,1:T(8,128)(2,1)} copy(bf16[512,2560]{1,0:T(8,128)(2,1)} %get-tuple-element.12) | data formatting | bytes 5242880 | tf_op jit(solution)/shard_map/sum_middle/pallas_call | solution.py:440
  199.3 8.4 %fusion.31 = f32[512,1728]{0,1:T(8,128)S(1)} fusion(bf16[512,2560]{1,0:T(8,128)(2,1)} %get-tuple-element.13, bf16[2560,1728]{1,0:T(8,128)(2,1)} %all-gather.2.cloned.1.call-done), kind=kOutput, calls=%fused_computation.73 | convolution fusion | flops 4529848320 | bytes 15007744 | tf_op jit(solution)/shard_map/dot_general | solution.py:567
  207.7 6.7 %fusion.3 = bf16[2560,512]{0,1:T(8,128)(2,1)} fusion(bf16[864,2560]{1,0:T(8,128)(2,1)} %param.23, f32[512,1728]{0,1:T(8,128)S(1)} %fusion.31), kind=kOutput, calls=%fused_computation.8 | convolution fusion | flops 2268889088 | bytes 10584064 | tf_op jit(solution)/shard_map/dot_general | solution.py:570
  214.4 4.4 %copy.30 = bf16[2560,512]{1,0:T(8,128)(2,1)} copy(bf16[2560,512]{0,1:T(8,128)(2,1)} %fusion.3) | data formatting | bytes 5242880 | tf_op jit(solution)/shard_map/convert_element_type | solution.py:572
  218.7 35.0 %sum_scatter.1 = f32[320,512]{1,0:T(8,128)} custom-call(bf16[8,320,512]{2,1,0:T(8,128)(2,1)} %bitcast.49), custom_call_target="tpu_custom_call" | custom-call | tf_op jit(solution)/shard_map/sum_scatter/pallas_call | solution.py:471
  253.7 2.0 fusion.12
  (57 shorter events, 7.8 us)
Async XLA Ops:
  6.5 99.4 %copy-start = (bf16[320,2560]{1,0:T(8,128)(2,1)S(1)}, bf16[320,2560]{1,0:T(8,128)(2,1)}, u32[]{:S(2)}) copy-start(bf16[320,2560]{1,0:T(8,128)(2,1)} %param.22) | copy-start | bytes 4915204
  6.5 7.1 %copy-start.3 = (f32[20,6912]{1,0:T(8,128)S(1)}, f32[20,6912]{1,0:T(8,128)}, u32[]{:S(2)}) copy-start(f32[20,6912]{1,0:T(8,128)} %param.21) | copy-start | bytes 1658884
  6.5 192.8 %all-gather.2.cloned.1.call-start = ((), (), s32[]{:S(2)}) async-start(), calls=%async_computation | async-start | bytes 9748480 | tf_op jit(solution)/shard_map/all_gather | solution.py:532
  13.1 2.3 copy-start.2
  15.4 55.0 %copy-start.7 = (s32[16]{0:T(128)S(1)}, s32[16]{0:T(128)}, u32[]{:S(2)}) copy-start(s32[16]{0:T(128)} %param.27) | copy-start | bytes 196
  15.4 55.7 %copy-start.8 = (s32[16]{0:T(128)S(1)}, s32[16]{0:T(128)}, u32[]{:S(2)}) copy-start(s32[16]{0:T(128)} %param.26) | copy-start | bytes 196
  15.4 56.2 %copy-start.4 = (f32[2560]{0:T(1024)S(1)}, f32[2560]{0:T(1024)}, u32[]{:S(2)}) copy-start(f32[2560]{0:T(1024)} %param.16) | copy-start | bytes 30724
  15.4 56.8 %copy-start.5 = (s32[128]{0:T(128)S(1)}, s32[128]{0:T(128)}, u32[]{:S(2)}) copy-start(s32[128]{0:T(128)} %param.25) | copy-start | bytes 1540
  18.0 57.2 %copy-start.6 = (f32[2560]{0:T(1024)S(1)}, f32[2560]{0:T(1024)}, u32[]{:S(2)}) copy-start(f32[2560]{0:T(1024)} %param.15) | copy-start | bytes 30724
  72.7 2.5 copy-start.1
Sparse Core Ops, SparseCore 0:
  70.5 89.6 all-gather.1

commit v5 on v4

--- a/solution.py
+++ b/solution.py
@@ -454,30 +454,135 @@
     )(partial_out.reshape(n, piece, width), tokens, mlp_gain.reshape(1, width))
 
 
-def scatter_kernel(n, piece_ref, out_ref, landed, send_sem, recv_sem):
+def hidden_kernel(
+    n, normed_ref, middle_hbm, pair_hbm, down_hbm, out_ref, pair, down, hidden, terms, landed,
+    window, turned, pair_sem, down_sem, window_sem, send_sem, recv_sem,
+):
     me = lax.axis_index("kv")
-    greet(n, me)
-    copies = exchange(n, me, piece_ref, landed, send_sem, recv_sem)
-    out_ref[...] = piece_ref[me].astype(jnp.float32)
+    rows, width = normed_ref.shape
+    halves, part = terms.shape[0], terms.shape[2]
+    piece = width // n
+    tiles = pair.shape[1] // 256
+    units = down.shape[0]
+    barrier = pltpu.get_barrier_semaphore()
     for step in range(1, n):
-        copies[step - 1].wait_recv()
-        out_ref[...] += landed[step - 1].astype(jnp.float32)
+        peer = lax.rem(me + step, n)
+        pl.semaphore_signal(barrier, inc=1, device_id={"kv": peer}, device_id_type=MESH)
+
+    def bring(tile):
+        lanes = pl.ds(pl.multiple_of(tile * 256, 256), 256)
+        return pltpu.make_async_copy(pair_hbm.at[:, lanes], pair.at[:, lanes], pair_sem.at[tile])
+
+    for tile in range(tiles):
+        bring(tile).start()
+    fetch = pltpu.make_async_copy(down_hbm, down, down_sem)
+    fetch.start()
+    left = lax.div(me * piece, 128) * 128
+    view = pltpu.make_async_copy(
+        middle_hbm.at[:, pl.ds(pl.multiple_of(left, 128), window.shape[1])], window, window_sem
+    )
+    view.start()
+
+    copies = []
+    for half in range(halves):
+        lines = slice(half * part, (half + 1) * part)
+
+        @pl.loop(0, tiles)
+        def _(tile):
+            if half == 0:
+                bring(tile).wait()
+            lanes = pl.ds(pl.multiple_of(tile * 256, 256), 256)
+            both = jnp.dot(normed_ref[lines, :], pair[:, lanes], preferred_element_type=jnp.float32)
+            gate, up = both[:, :128], both[:, 128:]
+            hidden[:, pl.ds(pl.multiple_of(tile * 128, 128), 128)] = (
+                gate / (1.0 + jnp.exp(-gate)) * up
+            ).astype(jnp.bfloat16)
+
+        if half == 0:
+            fetch.wait()
+
+        @pl.loop(0, width // 512)
+        def _(tile):
+            spot = pl.ds(pl.multiple_of(tile * 512, 512), 512)
+            term = jnp.dot(
+                hidden[:, :units], down[:, spot], preferred_element_type=jnp.float32
+            )
+            terms[half, spot, :] = term.T.astype(jnp.bfloat16)
+
+        if half == 0:
+            pl.semaphore_wait(barrier, n - 1)
+        for step in range(1, n):
+            peer = lax.rem(me + step, n)
+            copy = pltpu.make_async_remote_copy(
+                src_ref=terms.at[half, pl.ds(pl.multiple_of(peer * piece, piece), piece)],
+                dst_ref=landed.at[half, step - 1],
+                send_sem=send_sem.at[half, step - 1],
+                recv_sem=recv_sem.at[half, step - 1],
+                device_id={"kv": peer},
+                device_id_type=MESH,
+            )
+            copy.start()
+            copies.append(copy)
+    view.wait()
+    turned[...] = window[...].astype(jnp.float32).T
+    residual = pl.ds(pl.multiple_of(me * piece - left, 64), piece)
+    for half in range(halves):
+        lines = slice(half * part, (half + 1) * part)
+        own = pl.ds(pl.multiple_of(me * piece, piece), piece)
+        out_ref[:, lines] = turned[residual, lines] + terms[half, own, :].astype(jnp.float32)
+        for step in range(1, n):
+            copies[half * (n - 1) + step - 1].wait_recv()
+            out_ref[:, lines] += landed[half, step - 1].astype(jnp.float32)
     for copy in copies:
         copy.wait_send()
 
 
-def sum_scatter(n, pieces):
-    shape = pieces.shape[1:]
+def feed_forward(n, normed_mid, middle, w_pair, w_down):
+    rows, width = normed_mid.shape
+    halves = 2
+    part = rows // halves
+    piece = width // n
+    half = jnp.bfloat16
+    dma = pltpu.SemaphoreType.DMA
+    any_spec = pl.BlockSpec(memory_space=pl.ANY)
     return pl.pallas_call(
-        functools.partial(scatter_kernel, n),
-        name="sum_scatter",
-        out_shape=jax.ShapeDtypeStruct(shape, jnp.float32),
-        in_specs=[VMEM_SPEC],
+        functools.partial(hidden_kernel, n),
+        name="feed_forward",
+        out_shape=jax.ShapeDtypeStruct((piece, rows), jnp.float32),
+        in_specs=[VMEM_SPEC, any_spec, any_spec, any_spec],
         out_specs=VMEM_SPEC,
-        scratch_shapes=[pltpu.VMEM((n - 1,) + shape, jnp.bfloat16)]
-        + [pltpu.SemaphoreType.DMA((n - 1,))] * 2,
-        compiler_params=pltpu.CompilerParams(collective_id=1, has_side_effects=True),
-    )(pieces)
+        scratch_shapes=[
+            pltpu.VMEM(w_pair.shape, half),
+            pltpu.VMEM(w_down.shape, half),
+            pltpu.VMEM((part, w_pair.shape[1] // 2), half),
+            pltpu.VMEM((halves, width, part), half),
+            pltpu.VMEM((halves, n - 1, piece, part), half),
+            pltpu.VMEM((rows, piece + 64), half),
+            pltpu.VMEM((piece + 64, rows), jnp.float32),
+            dma((w_pair.shape[1] // 256,)),
+            dma,
+            dma,
+            dma((halves, n - 1)),
+            dma((halves, n - 1)),
+        ],
+        compiler_params=pltpu.CompilerParams(
+            collective_id=1, has_side_effects=True, vmem_limit_bytes=56 * 1024 * 1024
+        ),
+    )(normed_mid, middle, w_pair, w_down)
+
+
+def pack_pairs(first, second, groups):
+    rows, columns = first.shape
+    units = columns // groups
+    padded = -(-units // 128) * 128
+    tiles = [
+        jnp.pad(
+            matrix.astype(jnp.bfloat16).reshape(rows, groups, units),
+            ((0, 0), (0, 0), (0, padded - units)),
+        ).reshape(rows, groups, -1, 1, 128)
+        for matrix in (first, second)
+    ]
+    return jnp.transpose(jnp.concatenate(tiles, axis=3), (1, 0, 2, 3, 4)).reshape(groups, rows, -1)
 
 
 def shards(
@@ -525,7 +630,7 @@
         groups,
         n_blocks,
         pack_groups((w_query, w_key, w_value), groups),
-        pack_groups((w_gate, w_up), groups),
+        pack_pairs(w_gate, w_up, groups),
         outgoing,
     )
     w_qkv = w_first.reshape(-1, w_first.shape[2])
@@ -564,18 +669,8 @@
     )
     partial_out = projected_out.astype(jnp.bfloat16)
     middle, normed_mid = sum_middle(groups, partial_out, tokens, mlp_gain)
-    paired = jnp.dot(normed_mid, w_pair, preferred_element_type=jnp.float32)
-    hidden_width = w_pair.shape[1] // 2
-    hidden = (jax.nn.silu(paired[:, :hidden_width]) * paired[:, hidden_width:]).astype(jnp.bfloat16)
-    down_part = lax.dot_general(
-        w_down, hidden, (((0,), (1,)), ((), ())), preferred_element_type=jnp.float32
-    ).astype(jnp.bfloat16)
-    reduced = sum_scatter(groups, down_part.reshape(groups, -1, new_rows)).T
-    out_width = reduced.shape[1]
-    residual = lax.dynamic_slice_in_dim(middle, kv_index * out_width, out_width, 1).astype(
-        jnp.float32
-    )
-    mixed = jnp.where((row_ids < live_count)[:, None], residual + reduced, 0.0)
+    summed = feed_forward(groups, normed_mid, middle, w_pair, w_down).T
+    mixed = jnp.where((row_ids < live_count)[:, None], summed, 0.0)
     return mixed.astype(jnp.bfloat16)
 
 

time: 264 us -> 244 us (0.924)
  matrix products: 22.4 us -> 7.32 us
  local copies, waits for them, and re-layouts: 15.7 us -> 7.81 us
  Pallas kernels: 193 us -> 200 us
    dot_general x2 -> x0, matrix products: 15 us -> none  [the longest x1 8.37 us: shards(): paired = jnp.dot(normed_mid, w_pair, preferred_element_type=jnp.float32)]
    pallas_call x1, Pallas kernels: 35 us -> 40.9 us  [feed_forward(): pl.pallas_call(functools.partial(hidden_kernel, n), name='feed_forward',...]
    pallas_call x1 -> x0, local copies, waits for them, and re-layouts: 4.4 us -> none  [sum_middle(): pl.pallas_call(functools.partial(middle_kernel, n), name='sum_middle', co...]
    convert_element_type x1 -> x0, local copies, waits for them, and re-layouts: 4.39 us -> none  [shards(): down_part = lax.dot_general(w_down, hidden, (((0,), (1,)), ((), ())), pre...]
    convert_element_type x5 -> x3, other arithmetic: 3.8 us -> 0.03 us  [pack_groups(): matrix.astype(jnp.bfloat16).reshape(rows, groups, matrix.shape[1] // groups)]
  transfers between devices with their start and end apart: 1 -> 1, of which waited for: 0 -> 0; matrix products, arithmetic and copies ran while one was open for 9% -> 8% of each run, Pallas kernels for 40% -> 44%
where the time goes in v5:
time: 244 us
  Pallas kernels  200 us (82%)
  other arithmetic  15 us (6%)
  between operations  13.7 us (6%)
  local copies, waits for them, and re-layouts  7.81 us (3%)
  matrix products  7.32 us (3%)
    pallas_call x1, Pallas kernels, sum_middle(): pl.pallas_call(functools.partial(middle_kernel, n), name='sum_middle', co...  84.7 us
    pallas_call x1, Pallas kernels, regroup(): pl.pallas_call(functools.partial(regroup_kernel, n_kv, n_blk), name='regr...  52.4 us
    pallas_call x1, Pallas kernels, feed_forward(): pl.pallas_call(functools.partial(hidden_kernel, n), name='feed_forward',...  40.9 us
    pallas_call x1, Pallas kernels, attend(): pl.pallas_call(attention_kernel, name='attend', grid=(heads,), out_shape=...  21.7 us
  transfers between devices with their start and end apart: 1, of which 0 were waited for; matrix products, arithmetic and copies ran while one was open for 8% of the time, Pallas kernels for 44%

profile of v5, /device:TPU:1, one launch (start us, length us, event | category | flops | bytes accessed | tf_op | source)
XLA Modules:
  0.0 243.5 jit_solution(14016132603793537563)
XLA Ops:
  6.5 0.9 eq.55
  8.1 0.7 dynamic-slice_add_fusion
  8.9 1.1 convert_element_type.65
  10.6 1.2 convert_element_type.66
  12.5 1.0 copy.24.second_ref
  13.9 1.8 gather_fusion
  15.7 0.8 pad_maximum_fusion.1.first_ref
  16.5 52.4 %regroup.1 = (bf16[16,160,480]{2,1,0:T(8,128)(2,1)}, bf16[160,1792]{1,0:T(8,128)(2,1)}, bf16[16,2,2,80,128]{4,3,2,1,0:T(8,128)(2,1)}) custom-call(bf16[8,20,480]{2,1,0:T(8,128)(2,1)} %pad_maximum_fusion.1.first_ref, bf16[8,20,1792]{2,1,0:T(8,128)(2,1)} %copy.24.second_ref, bf16[16,2,2,80,128]{4,3,2,1,0:T(8,128)(2,1)} %bitcast.42), custom_call_target="tpu_custom_call" | custom-call | tf_op jit(solution)/shard_map/regroup/pallas_call | solution.py:201
  68.9 2.5 %fusion = f32[512]{0:T(512)S(1)} fusion(bf16[512,2560]{1,0:T(8,128)(2,1)} %token_ref.1), kind=kLoop, calls=%fused_computation.3 | loop fusion | flops 3931648 | bytes 2623488 | tf_op jit(solution)/shard_map/reduce_sum | solution.py:27
  71.5 3.3 %fusion.3 = f32[512,480]{0,1:T(8,128)S(1)} fusion(bf16[2560,480]{1,0:T(8,128)(2,1)} %bitcast.48, bf16[512,2560]{1,0:T(8,128)(2,1)S(1)} %copy-done.1, f32[2560]{0:T(1024)S(1)} %copy-done.8, f32[512]{0:T(512)S(1)} %add_rsqrt_fusion), kind=kOutput, calls=%fused_computation.7 | convolution fusion | flops 1263534080 | bytes 6074368 | tf_op jit(solution)/shard_map/dot_general | solution.py:639
  74.9 0.6 dynamic_slice.13
  75.5 0.6 dynamic_slice.12
  76.6 0.6 reshape.243.gain_ref
  77.5 1.9 pad_add_fusion.scalars
  79.3 0.7 add_convert_fusion.1
  80.4 0.6 maximum_bitcast_fusion.1.own_key_ref
  81.5 0.8 maximum_bitcast_fusion.query_ref
  82.3 0.6 fusion.16.own_value_ref
  82.9 21.7 %attend.1 = bf16[4,80,512]{2,1,0:T(8,128)(2,1)} custom-call(s32[66]{0:T(128)} %pad_add_fusion.scalars, bf16[4,80,512]{2,1,0:T(8,128)(2,1)} %maximum_bitcast_fusion.query_ref, bf16[80,512]{1,0:T(8,128)(2,1)} %maximum_bitcast_fusion.1.own_key_ref, bf16[80,512]{1,0:T(8,128)(2,1)} %fusion.16.own_value_ref, bf16[32,2,80,128]{3,2,1,0:T(8,128)(2,1)} %bitcast.49), custom_call_target="tpu_custom_call" | custom-call | flops 4831838208 | bytes 1474560 | tf_op jit(solution)/shard_map/attend/pallas_call | solution.py:339
  104.6 4.0 %convolution_convert_fusion = bf16[512,2560]{1,0:T(8,128)(2,1)} fusion(bf16[320,512]{1,0:T(8,128)(2,1)} %bitcast.50, bf16[320,2560]{1,0:T(8,128)(2,1)S(1)} %copy-done), kind=kOutput, calls=%fused_computation.6 | convolution fusion | flops 840171520 | bytes 4587520 | tf_op jit(solution)/shard_map/dot_general | solution.py:667
  108.6 84.7 %sum_middle.1 = (bf16[512,2560]{1,0:T(8,128)(2,1)}, bf16[512,2560]{1,0:T(8,128)(2,1)}) custom-call(bf16[8,64,2560]{2,1,0:T(8,128)(2,1)} %bitcast.44, bf16[512,2560]{1,0:T(8,128)(2,1)} %token_ref.1, f32[1,2560]{1,0:T(1,128)} %reshape.243.gain_ref), custom_call_target="tpu_custom_call" | custom-call | bytes 200000000 | tf_op jit(solution)/shard_map/sum_middle/pallas_call | solution.py:440
  193.2 0.6 iota_compare_fusion.4
  193.9 40.9 %feed_forward.1 = f32[320,512]{1,0:T(8,128)} custom-call(bf16[512,2560]{1,0:T(8,128)(2,1)} %get-tuple-element.12.normed_ref, bf16[512,2560]{1,0:T(8,128)(2,1)} %get-tuple-element.13.middle_hbm, bf16[2560,1792]{1,0:T(8,128)(2,1)} %all-gather.2.cloned.1.call-done.pair_hbm, bf16[864,2560]{1,0:T(8,128)(2,1)} %down_hbm.1), custom_call_target="tpu_custom_call" | custom-call | tf_op jit(solution)/shard_map/feed_forward/pallas_call | solution.py:548
  234.8 1.9 fusion.7
  (58 shorter events, 4.1 us)
Async XLA Ops:
  6.5 98.0 %copy-start = (bf16[320,2560]{1,0:T(8,128)(2,1)S(1)}, bf16[320,2560]{1,0:T(8,128)(2,1)}, u32[]{:S(2)}) copy-start(bf16[320,2560]{1,0:T(8,128)(2,1)} %param.22) | copy-start | bytes 4915204
  6.5 187.3 %all-gather.2.cloned.1.call-start = ((), (), s32[]{:S(2)}) async-start(), calls=%async_computation | async-start | bytes 9748480 | tf_op jit(solution)/shard_map/all_gather | solution.py:637
  10.6 2.9 %copy-start.4 = (f32[20,640]{1,0:T(8,128)S(1)}, f32[20,640]{1,0:T(8,128)}, u32[]{:S(2)}) copy-start(f32[20,640]{1,0:T(8,128)} %param.18) | copy-start | bytes 153604
  10.6 3.0 %copy-start.5 = (f32[20,640]{1,0:T(8,128)S(1)}, f32[20,640]{1,0:T(8,128)}, u32[]{:S(2)}) copy-start(f32[20,640]{1,0:T(8,128)} %param.19) | copy-start | bytes 153604
  10.6 3.1 %copy-start.3 = (f32[20,2560]{1,0:T(8,128)S(1)}, f32[20,2560]{1,0:T(8,128)}, u32[]{:S(2)}) copy-start(f32[20,2560]{1,0:T(8,128)} %param.17) | copy-start | bytes 614404
  11.8 2.1 copy-start.2
  16.5 54.9 %copy-start.8 = (f32[2560]{0:T(1024)S(1)}, f32[2560]{0:T(1024)}, u32[]{:S(2)}) copy-start(f32[2560]{0:T(1024)} %param.15) | copy-start | bytes 30724
  68.9 2.5 %copy-start.1 = (bf16[512,2560]{1,0:T(8,128)(2,1)S(1)}, bf16[512,2560]{1,0:T(8,128)(2,1)}, u32[]{:S(2)}) copy-start(bf16[512,2560]{1,0:T(8,128)(2,1)} %token_ref.1) | copy-start | bytes 7864324
  71.5 3.4 %copy-start.9 = (s32[16]{0:T(128)S(1)}, s32[16]{0:T(128)}, u32[]{:S(2)}) copy-start(s32[16]{0:T(128)} %param.26) | copy-start | bytes 196
  71.5 4.0 %copy-start.10 = (s32[16]{0:T(128)S(1)}, s32[16]{0:T(128)}, u32[]{:S(2)}) copy-start(s32[16]{0:T(128)} %param.27) | copy-start | bytes 196
  71.5 4.7 %copy-start.7 = (s32[128]{0:T(128)S(1)}, s32[128]{0:T(128)}, u32[]{:S(2)}) copy-start(s32[128]{0:T(128)} %param.25) | copy-start | bytes 1540
  71.5 5.1 %copy-start.6 = (f32[2560]{0:T(1024)S(1)}, f32[2560]{0:T(1024)}, u32[]{:S(2)}) copy-start(f32[2560]{0:T(1024)} %param.16) | copy-start | bytes 30724
Sparse Core Ops, SparseCore 0:
  69.1 89.2 all-gather.1

commit v6 on v5

--- a/solution.py
+++ b/solution.py
@@ -122,9 +122,6 @@
         )
 
     firsts = swap(first_ref, first_in, first_send, first_recv)
-    seconds = swap(second_ref, second_in, second_send, second_recv)
-    deals = fan_out(n_blk, deal)
-
     first_in[me_kv] = first_ref[me_kv]
     for copy in firsts:
         copy.wait_recv()
@@ -155,23 +152,24 @@
     for step in (1, 3, 2):
         pass_on(0, along(step), 2 * step)
     pass_on(0, sibling, 1)
+    seconds = swap(second_ref, second_in, second_send, second_recv)
     passed[8].wait_recv()
     for step in (1, 3, 2):
         pass_on(8, along(step), 8 + 2 * step)
     pass_on(8, sibling, 9)
-
+    deals = fan_out(n_blk, deal)
+
+    for base in (0, 8):
+        for step in (1, 3, 2):
+            slot = base + 2 * step
+            passed[slot].wait_recv()
+            pass_on(slot, sibling, slot + 1)
     second_in[me_kv] = second_ref[me_kv]
     for copy in seconds:
         copy.wait_recv()
     for group in range(n_kv):
         stage_b[group * rows : (group + 1) * rows, :] = second_in[group].astype(jnp.float32)
     second_out[...] = stage_b[...].astype(jnp.bfloat16)
-
-    for base in (0, 8):
-        for step in (1, 3, 2):
-            slot = base + 2 * step
-            passed[slot].wait_recv()
-            pass_on(slot, sibling, slot + 1)
     for base in (0, 8):
         for step in range(4):
             for other in range(2):

time: 244 us -> 240 us (0.984)
  Pallas kernels: 200 us -> 196 us
where the time goes in v6:
time: 240 us
  Pallas kernels  196 us (82%)
  other arithmetic  15 us (6%)
  between operations  13.7 us (6%)
  local copies, waits for them, and re-layouts  7.81 us (3%)
  matrix products  7.32 us (3%)
    pallas_call x1, Pallas kernels, sum_middle(): pl.pallas_call(functools.partial(middle_kernel, n), name='sum_middle', co...  83.2 us
    pallas_call x1, Pallas kernels, regroup(): pl.pallas_call(functools.partial(regroup_kernel, n_kv, n_blk), name='regr...  50.3 us
    pallas_call x1, Pallas kernels, feed_forward(): pl.pallas_call(functools.partial(hidden_kernel, n), name='feed_forward',...  40.8 us
    pallas_call x1, Pallas kernels, attend(): pl.pallas_call(attention_kernel, name='attend', grid=(heads,), out_shape=...  21.6 us
  transfers between devices with their start and end apart: 1, of which 0 were waited for; matrix products, arithmetic and copies ran while one was open for 8% of the time, Pallas kernels for 44%

profile of v6, /device:TPU:1, one launch (start us, length us, event | category | flops | bytes accessed | tf_op | source)
XLA Modules:
  0.0 239.8 jit_solution(14043575033132506534)
XLA Ops:
  6.5 0.9 eq.55
  8.1 0.7 dynamic-slice_add_fusion
  8.9 1.1 convert_element_type.65
  10.6 1.2 convert_element_type.66
  12.5 1.0 copy.24.second_ref
  13.9 1.8 gather_fusion
  15.7 0.8 pad_maximum_fusion.1.first_ref
  16.5 50.3 %regroup.1 = (bf16[16,160,480]{2,1,0:T(8,128)(2,1)}, bf16[160,1792]{1,0:T(8,128)(2,1)}, bf16[16,2,2,80,128]{4,3,2,1,0:T(8,128)(2,1)}) custom-call(bf16[8,20,480]{2,1,0:T(8,128)(2,1)} %pad_maximum_fusion.1.first_ref, bf16[8,20,1792]{2,1,0:T(8,128)(2,1)} %copy.24.second_ref, bf16[16,2,2,80,128]{4,3,2,1,0:T(8,128)(2,1)} %bitcast.42), custom_call_target="tpu_custom_call" | custom-call | tf_op jit(solution)/shard_map/regroup/pallas_call | solution.py:199
  66.9 2.5 %fusion = f32[512]{0:T(512)S(1)} fusion(bf16[512,2560]{1,0:T(8,128)(2,1)} %token_ref.1), kind=kLoop, calls=%fused_computation.3 | loop fusion | flops 3931648 | bytes 2623488 | tf_op jit(solution)/shard_map/reduce_sum | solution.py:27
  69.4 3.3 %fusion.3 = f32[512,480]{0,1:T(8,128)S(1)} fusion(bf16[2560,480]{1,0:T(8,128)(2,1)} %bitcast.48, bf16[512,2560]{1,0:T(8,128)(2,1)S(1)} %copy-done.1, f32[2560]{0:T(1024)S(1)} %copy-done.8, f32[512]{0:T(512)S(1)} %add_rsqrt_fusion), kind=kOutput, calls=%fused_computation.7 | convolution fusion | flops 1263534080 | bytes 6074368 | tf_op jit(solution)/shard_map/dot_general | solution.py:637
  72.9 0.6 dynamic_slice.13
  73.4 0.6 dynamic_slice.12
  74.5 0.6 reshape.243.gain_ref
  75.4 1.9 pad_add_fusion.scalars
  77.3 0.6 add_convert_fusion.1
  78.3 0.6 maximum_bitcast_fusion.1.own_key_ref
  79.5 0.8 maximum_bitcast_fusion.query_ref
  80.2 0.6 fusion.16.own_value_ref
  80.9 21.6 %attend.1 = bf16[4,80,512]{2,1,0:T(8,128)(2,1)} custom-call(s32[66]{0:T(128)} %pad_add_fusion.scalars, bf16[4,80,512]{2,1,0:T(8,128)(2,1)} %maximum_bitcast_fusion.query_ref, bf16[80,512]{1,0:T(8,128)(2,1)} %maximum_bitcast_fusion.1.own_key_ref, bf16[80,512]{1,0:T(8,128)(2,1)} %fusion.16.own_value_ref, bf16[32,2,80,128]{3,2,1,0:T(8,128)(2,1)} %bitcast.49), custom_call_target="tpu_custom_call" | custom-call | flops 4831838208 | bytes 1474560 | tf_op jit(solution)/shard_map/attend/pallas_call | solution.py:337
  102.5 4.0 %convolution_convert_fusion = bf16[512,2560]{1,0:T(8,128)(2,1)} fusion(bf16[320,512]{1,0:T(8,128)(2,1)} %bitcast.50, bf16[320,2560]{1,0:T(8,128)(2,1)S(1)} %copy-done), kind=kOutput, calls=%fused_computation.6 | convolution fusion | flops 840171520 | bytes 4587520 | tf_op jit(solution)/shard_map/dot_general | solution.py:665
  106.5 83.2 %sum_middle.1 = (bf16[512,2560]{1,0:T(8,128)(2,1)}, bf16[512,2560]{1,0:T(8,128)(2,1)}) custom-call(bf16[8,64,2560]{2,1,0:T(8,128)(2,1)} %bitcast.44, bf16[512,2560]{1,0:T(8,128)(2,1)} %token_ref.1, f32[1,2560]{1,0:T(1,128)} %reshape.243.gain_ref), custom_call_target="tpu_custom_call" | custom-call | bytes 200000000 | tf_op jit(solution)/shard_map/sum_middle/pallas_call | solution.py:438
  189.6 0.6 iota_compare_fusion.4
  190.3 40.8 %feed_forward.1 = f32[320,512]{1,0:T(8,128)} custom-call(bf16[512,2560]{1,0:T(8,128)(2,1)} %get-tuple-element.12.normed_ref, bf16[512,2560]{1,0:T(8,128)(2,1)} %get-tuple-element.13.middle_hbm, bf16[2560,1792]{1,0:T(8,128)(2,1)} %all-gather.2.cloned.1.call-done.pair_hbm, bf16[864,2560]{1,0:T(8,128)(2,1)} %down_hbm.1), custom_call_target="tpu_custom_call" | custom-call | tf_op jit(solution)/shard_map/feed_forward/pallas_call | solution.py:546
  231.1 1.9 fusion.7
  (58 shorter events, 4.1 us)
Async XLA Ops:
  6.5 96.0 %copy-start = (bf16[320,2560]{1,0:T(8,128)(2,1)S(1)}, bf16[320,2560]{1,0:T(8,128)(2,1)}, u32[]{:S(2)}) copy-start(bf16[320,2560]{1,0:T(8,128)(2,1)} %param.22) | copy-start | bytes 4915204
  6.5 183.7 %all-gather.2.cloned.1.call-start = ((), (), s32[]{:S(2)}) async-start(), calls=%async_computation | async-start | bytes 9748480 | tf_op jit(solution)/shard_map/all_gather | solution.py:635
  10.6 2.9 %copy-start.4 = (f32[20,640]{1,0:T(8,128)S(1)}, f32[20,640]{1,0:T(8,128)}, u32[]{:S(2)}) copy-start(f32[20,640]{1,0:T(8,128)} %param.18) | copy-start | bytes 153604
  10.6 3.0 %copy-start.5 = (f32[20,640]{1,0:T(8,128)S(1)}, f32[20,640]{1,0:T(8,128)}, u32[]{:S(2)}) copy-start(f32[20,640]{1,0:T(8,128)} %param.19) | copy-start | bytes 153604
  10.6 3.1 %copy-start.3 = (f32[20,2560]{1,0:T(8,128)S(1)}, f32[20,2560]{1,0:T(8,128)}, u32[]{:S(2)}) copy-start(f32[20,2560]{1,0:T(8,128)} %param.17) | copy-start | bytes 614404
  11.8 2.1 copy-start.2
  16.5 52.8 %copy-start.8 = (f32[2560]{0:T(1024)S(1)}, f32[2560]{0:T(1024)}, u32[]{:S(2)}) copy-start(f32[2560]{0:T(1024)} %param.15) | copy-start | bytes 30724
  66.9 2.5 %copy-start.1 = (bf16[512,2560]{1,0:T(8,128)(2,1)S(1)}, bf16[512,2560]{1,0:T(8,128)(2,1)}, u32[]{:S(2)}) copy-start(bf16[512,2560]{1,0:T(8,128)(2,1)} %token_ref.1) | copy-start | bytes 7864324
  69.4 3.4 %copy-start.9 = (s32[16]{0:T(128)S(1)}, s32[16]{0:T(128)}, u32[]{:S(2)}) copy-start(s32[16]{0:T(128)} %param.26) | copy-start | bytes 196
  69.4 4.0 %copy-start.10 = (s32[16]{0:T(128)S(1)}, s32[16]{0:T(128)}, u32[]{:S(2)}) copy-start(s32[16]{0:T(128)} %param.27) | copy-start | bytes 196
  69.4 4.7 %copy-start.7 = (s32[128]{0:T(128)S(1)}, s32[128]{0:T(128)}, u32[]{:S(2)}) copy-start(s32[128]{0:T(128)} %param.25) | copy-start | bytes 1540
  69.4 5.1 %copy-start.6 = (f32[2560]{0:T(1024)S(1)}, f32[2560]{0:T(1024)}, u32[]{:S(2)}) copy-start(f32[2560]{0:T(1024)} %param.16) | copy-start | bytes 30724
Sparse Core Ops, SparseCore 0:
  67.0 89.6 all-gather.1

commit v7 on v6

--- a/solution.py
+++ b/solution.py
@@ -363,72 +363,203 @@
     )(scalars, query, own_key, own_value, blocks)
 
 
-def greet(n, me):
+def hail(n, me):
     barrier = pltpu.get_barrier_semaphore()
     for step in range(1, n):
         peer = lax.rem(me + step, n)
         pl.semaphore_signal(barrier, inc=1, device_id={"kv": peer}, device_id_type=MESH)
-    pl.semaphore_wait(barrier, n - 1)
-
-
-def exchange(n, me, piece_ref, landed, send_sem, recv_sem):
-    copies = []
-    for step in range(1, n):
-        peer = lax.rem(me + step, n)
+    return barrier
+
+
+class Links:
+    def __init__(self, send, recv):
+        self.send, self.recv, self.started = send, recv, []
+
+    def go(self, source, target, peer, index):
         copy = pltpu.make_async_remote_copy(
-            src_ref=piece_ref.at[peer],
-            dst_ref=landed.at[step - 1],
-            send_sem=send_sem.at[step - 1],
-            recv_sem=recv_sem.at[step - 1],
+            src_ref=source,
+            dst_ref=target,
+            send_sem=self.send.at[index],
+            recv_sem=self.recv.at[index],
             device_id={"kv": peer},
             device_id_type=MESH,
         )
         copy.start()
-        copies.append(copy)
-    return copies
+        self.started.append(copy)
+        return copy
+
+    def close(self):
+        for copy in self.started:
+            copy.wait_send()
+
+
+def z_steps(lines):
+    return sorted(range(1, lines), key=lambda step: min(step, lines - step))
+
+
+def as_float(ref):
+    return ref[...].astype(jnp.float32)
+
+
+class Scatter(Links):
+    def __init__(self, n, me, view, landings, send, recv):
+        super().__init__(send, recv)
+        self.land_a, self.land_b, self.stage_a, self.stage_b, self.got_a, self.got_b = landings
+        self.lines, self.me, self.view = n // 2, me, view
+        self.z, self.y = lax.div(me, 2), lax.rem(me, 2)
+        self.partner = 2 * self.z + 1 - self.y
+        self.steps = z_steps(self.lines)
+
+    def line(self, step):
+        return 2 * lax.rem(self.z + step, self.lines)
+
+    def open(self):
+        lines = self.lines
+        self.along = [
+            self.go(
+                self.view(self.line(step) + side, 0),
+                self.land_a.at[step - 1, side],
+                self.line(step) + self.y,
+                2 * (step - 1) + side,
+            )
+            for step in self.steps
+            for side in range(2)
+        ]
+        self.across = {
+            step: self.go(
+                self.view(self.line(step) + 1 - self.y, 1),
+                self.land_b.at[step],
+                self.partner,
+                2 * (lines - 1) + step,
+            )
+            for step in self.steps + [0]
+        }
+
+    def forward(self):
+        lines = self.lines
+        self.last_b = []
+        for step in self.steps:
+            self.across[step].wait_recv()
+            self.stage_b[step - 1] = (
+                as_float(self.view(self.line(step) + self.y, 1)) + as_float(self.land_b.at[step])
+            ).astype(jnp.bfloat16)
+            self.last_b.append(
+                self.go(
+                    self.stage_b.at[step - 1],
+                    self.got_b.at[step - 1],
+                    self.line(step) + self.y,
+                    3 * lines - 2 + step - 1,
+                )
+            )
+        for copy in self.along:
+            copy.wait_recv()
+        self.stage_a[...] = self.gathered(1 - self.y).astype(jnp.bfloat16)
+        self.last_a = self.go(self.stage_a, self.got_a, self.partner, 4 * lines - 3)
+
+    def gathered(self, side):
+        total = as_float(self.view(2 * self.z + side, 0))
+        for step in range(self.lines - 1):
+            total += as_float(self.land_a.at[step, side])
+        return total
+
+    def finish_a(self):
+        self.last_a.wait_recv()
+        return self.gathered(self.y) + as_float(self.got_a)
+
+    def finish_b(self):
+        self.across[0].wait_recv()
+        total = as_float(self.view(self.me, 1)) + as_float(self.land_b.at[0])
+        for copy in self.last_b:
+            copy.wait_recv()
+        for step in range(self.lines - 1):
+            total += as_float(self.got_b.at[step])
+        return total
+
+
+def scatter_scratch(n, shape, copies=1):
+    lines = n // 2
+    sizes = [(lines - 1, 2), (lines,), (), (lines - 1,), (), (lines - 1,)]
+    lead = () if copies == 1 else (copies,)
+    return [pltpu.VMEM(lead + size + shape, jnp.bfloat16) for size in sizes] + [
+        pltpu.SemaphoreType.DMA(lead + (4 * lines - 2,))
+    ] * 2
 
 
 def middle_kernel(
-    n, piece_ref, token_ref, gain_ref, middle_ref, normed_ref, landed, total, whole,
-    send_sem, recv_sem, share_sem, join_sem,
+    n, piece_ref, token_ref, gain_ref, middle_ref, normed_ref,
+    land_a, land_b, stage_a, stage_b, got_a, got_b, send, recv, whole, share, join,
 ):
     me = lax.axis_index("kv")
-    rows = piece_ref.shape[1]
-    greet(n, me)
-    copies = exchange(n, me, piece_ref, landed, send_sem, recv_sem)
-    own = pl.ds(pl.multiple_of(me * rows, rows), rows)
-    total[...] = token_ref[own, :].astype(jnp.float32) + piece_ref[me].astype(jnp.float32)
-    for step in range(1, n):
-        copies[step - 1].wait_recv()
-        total[...] += landed[step - 1].astype(jnp.float32)
-    whole[0] = total[...].astype(jnp.bfloat16)
-    shares = []
-    for step in range(1, n):
-        peer = lax.rem(me + step, n)
-        share = pltpu.make_async_remote_copy(
-            src_ref=whole.at[0],
-            dst_ref=whole.at[step],
-            send_sem=share_sem.at[step - 1],
-            recv_sem=join_sem.at[step - 1],
-            device_id={"kv": peer},
-            device_id_type=MESH,
-        )
-        share.start()
-        shares.append(share)
-    for step in range(n):
-        if step:
-            shares[step - 1].wait_recv()
-        owner = lax.rem(me + n - step, n)
-        place = pl.ds(pl.multiple_of(owner * rows, rows), rows)
-        middle_rows = whole[step]
+    part = piece_ref.shape[2]
+    lines = n // 2
+    barrier = hail(n, me)
+    terms = Scatter(
+        n, me, lambda k, h: piece_ref.at[k, h],
+        (land_a, land_b, stage_a, stage_b, got_a, got_b), send, recv,
+    )
+    links = Links(share, join)
+    pl.semaphore_wait(barrier, n - 1)
+    terms.open()
+    terms.forward()
+
+    def rows_of(step, side, half):
+        owner = 2 * lax.rem(terms.z + lines - step, lines) + lax.rem(terms.y + side, 2)
+        return pl.ds(pl.multiple_of((owner * 2 + half) * part, part), part)
+
+    def index_of(step, side, half):
+        return (step * 2 + side) * 2 + half - 2
+
+    came = {}
+
+    def spread(held, slot, peer):
+        came[slot] = links.go(whole.at[held], whole.at[slot], peer, index_of(*slot))
+
+    def settle(slot):
+        place = rows_of(*slot)
+        middle_rows = whole[slot]
         middle_ref[place, :] = middle_rows
         values = middle_rows.astype(jnp.float32)
         mean_square = jnp.mean(values * values, axis=-1, keepdims=True)
         normed_ref[place, :] = (
             values * lax.rsqrt(mean_square + EPSILON) * gain_ref[...]
         ).astype(jnp.bfloat16)
-    for copy in copies + shares:
-        copy.wait_send()
+
+    def peer_at(step):
+        return terms.line(step) + terms.y
+
+    own_a = token_ref[rows_of(0, 0, 0), :].astype(jnp.float32)
+    whole[0, 0, 0] = (own_a + terms.finish_a()).astype(jnp.bfloat16)
+    for step in terms.steps:
+        spread((0, 0, 0), (step, 0, 0), peer_at(step))
+    spread((0, 0, 0), (0, 1, 0), terms.partner)
+    own_b = token_ref[rows_of(0, 0, 1), :].astype(jnp.float32)
+    whole[0, 0, 1] = (own_b + terms.finish_b()).astype(jnp.bfloat16)
+    spread((0, 0, 1), (0, 1, 1), terms.partner)
+    for step in terms.steps:
+        spread((0, 0, 1), (step, 0, 1), peer_at(step))
+    settle((0, 0, 0))
+    settle((0, 0, 1))
+    for step in terms.steps:
+        came[step, 0, 0].wait_recv()
+        spread((step, 0, 0), (step, 1, 0), terms.partner)
+        if step == terms.steps[0]:
+            came[0, 1, 1].wait_recv()
+            for far in terms.steps:
+                spread((0, 1, 1), (far, 1, 1), peer_at(far))
+    settle((0, 1, 1))
+    for step in terms.steps:
+        settle((step, 0, 0))
+    came[0, 1, 0].wait_recv()
+    settle((0, 1, 0))
+    for step, side, half in (
+        [(step, 0, 1) for step in terms.steps]
+        + [(step, 1, 0) for step in terms.steps]
+        + [(step, 1, 1) for step in terms.steps]
+    ):
+        came[step, side, half].wait_recv()
+        settle((step, side, half))
+    terms.close()
+    links.close()
 
 
 def sum_middle(n, partial_out, tokens, mlp_gain):
@@ -442,19 +573,17 @@
         out_shape=(whole_shape, whole_shape),
         in_specs=[VMEM_SPEC] * 3,
         out_specs=(VMEM_SPEC, VMEM_SPEC),
-        scratch_shapes=[
-            pltpu.VMEM((n - 1, piece, width), jnp.bfloat16),
-            pltpu.VMEM((piece, width), jnp.float32),
-            pltpu.VMEM((n, piece, width), jnp.bfloat16),
-        ]
-        + [pltpu.SemaphoreType.DMA((n - 1,))] * 4,
+        scratch_shapes=scatter_scratch(n, (piece // 2, width))
+        + [pltpu.VMEM((n // 2, 2, 2, piece // 2, width), jnp.bfloat16)]
+        + [pltpu.SemaphoreType.DMA((2 * n - 2,))] * 2,
         compiler_params=pltpu.CompilerParams(collective_id=0, has_side_effects=True),
-    )(partial_out.reshape(n, piece, width), tokens, mlp_gain.reshape(1, width))
+    )(partial_out.reshape(n, 2, piece // 2, width), tokens, mlp_gain.reshape(1, width))
 
 
 def hidden_kernel(
-    n, normed_ref, middle_hbm, pair_hbm, down_hbm, out_ref, pair, down, hidden, terms, landed,
-    window, turned, pair_sem, down_sem, window_sem, send_sem, recv_sem,
+    n, normed_ref, middle_hbm, pair_hbm, down_hbm, out_ref, pair, down, hidden, terms,
+    window, turned, pair_sem, down_sem, window_sem,
+    land_a, land_b, stage_a, stage_b, got_a, got_b, send, recv,
 ):
     me = lax.axis_index("kv")
     rows, width = normed_ref.shape
@@ -462,10 +591,7 @@
     piece = width // n
     tiles = pair.shape[1] // 256
     units = down.shape[0]
-    barrier = pltpu.get_barrier_semaphore()
-    for step in range(1, n):
-        peer = lax.rem(me + step, n)
-        pl.semaphore_signal(barrier, inc=1, device_id={"kv": peer}, device_id_type=MESH)
+    barrier = hail(n, me)
 
     def bring(tile):
         lanes = pl.ds(pl.multiple_of(tile * 256, 256), 256)
@@ -481,7 +607,15 @@
     )
     view.start()
 
-    copies = []
+    def exchange(half):
+        def term(owner, side):
+            start = pl.multiple_of(owner * piece + side * (piece // 2), piece // 2)
+            return terms.at[half, pl.ds(start, piece // 2)]
+
+        landings = [ref.at[half] for ref in (land_a, land_b, stage_a, stage_b, got_a, got_b)]
+        return Scatter(n, me, term, landings, send.at[half], recv.at[half])
+
+    sums = [exchange(half) for half in range(halves)]
     for half in range(halves):
         lines = slice(half * part, (half + 1) * part)
 
@@ -509,30 +643,20 @@
 
         if half == 0:
             pl.semaphore_wait(barrier, n - 1)
-        for step in range(1, n):
-            peer = lax.rem(me + step, n)
-            copy = pltpu.make_async_remote_copy(
-                src_ref=terms.at[half, pl.ds(pl.multiple_of(peer * piece, piece), piece)],
-                dst_ref=landed.at[half, step - 1],
-                send_sem=send_sem.at[half, step - 1],
-                recv_sem=recv_sem.at[half, step - 1],
-                device_id={"kv": peer},
-                device_id_type=MESH,
-            )
-            copy.start()
-            copies.append(copy)
+        sums[half].open()
     view.wait()
     turned[...] = window[...].astype(jnp.float32).T
-    residual = pl.ds(pl.multiple_of(me * piece - left, 64), piece)
+    for half in range(halves):
+        sums[half].forward()
+    shift = me * piece - left
     for half in range(halves):
         lines = slice(half * part, (half + 1) * part)
-        own = pl.ds(pl.multiple_of(me * piece, piece), piece)
-        out_ref[:, lines] = turned[residual, lines] + terms[half, own, :].astype(jnp.float32)
-        for step in range(1, n):
-            copies[half * (n - 1) + step - 1].wait_recv()
-            out_ref[:, lines] += landed[half, step - 1].astype(jnp.float32)
-    for copy in copies:
-        copy.wait_send()
+        for side, finish in enumerate((sums[half].finish_a, sums[half].finish_b)):
+            residual = pl.ds(pl.multiple_of(shift + side * (piece // 2), 32), piece // 2)
+            place = slice(side * (piece // 2), (side + 1) * (piece // 2))
+            out_ref[place, lines] = turned[residual, lines] + finish()
+    for half in range(halves):
+        sums[half].close()
 
 
 def feed_forward(n, normed_mid, middle, w_pair, w_down):
@@ -554,15 +678,13 @@
             pltpu.VMEM(w_down.shape, half),
             pltpu.VMEM((part, w_pair.shape[1] // 2), half),
             pltpu.VMEM((halves, width, part), half),
-            pltpu.VMEM((halves, n - 1, piece, part), half),
             pltpu.VMEM((rows, piece + 64), half),
             pltpu.VMEM((piece + 64, rows), jnp.float32),
             dma((w_pair.shape[1] // 256,)),
             dma,
             dma,
-            dma((halves, n - 1)),
-            dma((halves, n - 1)),
-        ],
+        ]
+        + scatter_scratch(n, (piece // 2, part), halves),
         compiler_params=pltpu.CompilerParams(
             collective_id=1, has_side_effects=True, vmem_limit_bytes=56 * 1024 * 1024
         ),

time: 240 us -> 215 us (0.90)
  Pallas kernels: 196 us -> 171 us
    pallas_call x1, Pallas kernels: 83.2 us -> 65.4 us  [sum_middle(): pl.pallas_call(functools.partial(middle_kernel, n), name='sum_middle', co...]
    pallas_call x1, Pallas kernels: 40.8 us -> 33.7 us  [feed_forward(): pl.pallas_call(functools.partial(hidden_kernel, n), name='feed_forward',...]
  transfers between devices with their start and end apart: 1 -> 1, of which waited for: 0 -> 0; matrix products, arithmetic and copies ran while one was open for 8% -> 9% of each run, Pallas kernels for 44% -> 40%
where the time goes in v7:
time: 215 us
  Pallas kernels  171 us (80%)
  other arithmetic  15 us (7%)
  between operations  13.7 us (6%)
  local copies, waits for them, and re-layouts  7.81 us (4%)
  matrix products  7.32 us (3%)
    pallas_call x1, Pallas kernels, sum_middle(): pl.pallas_call(functools.partial(middle_kernel, n), name='sum_middle', co...  65.4 us
    pallas_call x1, Pallas kernels, regroup(): pl.pallas_call(functools.partial(regroup_kernel, n_kv, n_blk), name='regr...  50.3 us
    pallas_call x1, Pallas kernels, feed_forward(): pl.pallas_call(functools.partial(hidden_kernel, n), name='feed_forward',...  33.7 us
    pallas_call x1, Pallas kernels, attend(): pl.pallas_call(attention_kernel, name='attend', grid=(heads,), out_shape=...  21.6 us
  transfers between devices with their start and end apart: 1, of which 0 were waited for; matrix products, arithmetic and copies ran while one was open for 9% of the time, Pallas kernels for 40%

profile of v7, /device:TPU:1, one launch (start us, length us, event | category | flops | bytes accessed | tf_op | source)
XLA Modules:
  0.0 215.0 jit_solution(2686772521466755046)
XLA Ops:
  6.5 0.9 eq.55
  8.1 0.7 dynamic-slice_add_fusion
  8.9 1.1 convert_element_type.65
  10.6 1.2 convert_element_type.66
  12.5 1.0 copy.24.second_ref
  13.9 1.8 gather_fusion
  15.7 0.8 pad_maximum_fusion.1.first_ref
  16.5 50.3 %regroup.1 = (bf16[16,160,480]{2,1,0:T(8,128)(2,1)}, bf16[160,1792]{1,0:T(8,128)(2,1)}, bf16[16,2,2,80,128]{4,3,2,1,0:T(8,128)(2,1)}) custom-call(bf16[8,20,480]{2,1,0:T(8,128)(2,1)} %pad_maximum_fusion.1.first_ref, bf16[8,20,1792]{2,1,0:T(8,128)(2,1)} %copy.24.second_ref, bf16[16,2,2,80,128]{4,3,2,1,0:T(8,128)(2,1)} %bitcast.42), custom_call_target="tpu_custom_call" | custom-call | tf_op jit(solution)/shard_map/regroup/pallas_call | solution.py:199
  66.9 2.5 %fusion = f32[512]{0:T(512)S(1)} fusion(bf16[512,2560]{1,0:T(8,128)(2,1)} %token_ref.1), kind=kLoop, calls=%fused_computation.3 | loop fusion | flops 3931648 | bytes 2623488 | tf_op jit(solution)/shard_map/reduce_sum | solution.py:27
  69.4 3.3 %fusion.3 = f32[512,480]{0,1:T(8,128)S(1)} fusion(bf16[2560,480]{1,0:T(8,128)(2,1)} %bitcast.48, bf16[512,2560]{1,0:T(8,128)(2,1)S(1)} %copy-done.1, f32[2560]{0:T(1024)S(1)} %copy-done.8, f32[512]{0:T(512)S(1)} %add_rsqrt_fusion), kind=kOutput, calls=%fused_computation.7 | convolution fusion | flops 1263534080 | bytes 6074368 | tf_op jit(solution)/shard_map/dot_general | solution.py:759
  72.9 0.6 dynamic_slice.13
  73.5 0.6 dynamic_slice.12
  74.5 0.6 reshape.243.gain_ref
  75.4 1.9 pad_add_fusion.scalars
  77.3 0.6 add_convert_fusion.1
  78.4 0.6 maximum_bitcast_fusion.1.own_key_ref
  79.5 0.8 maximum_bitcast_fusion.query_ref
  80.2 0.6 fusion.16.own_value_ref
  80.9 21.6 %attend.1 = bf16[4,80,512]{2,1,0:T(8,128)(2,1)} custom-call(s32[66]{0:T(128)} %pad_add_fusion.scalars, bf16[4,80,512]{2,1,0:T(8,128)(2,1)} %maximum_bitcast_fusion.query_ref, bf16[80,512]{1,0:T(8,128)(2,1)} %maximum_bitcast_fusion.1.own_key_ref, bf16[80,512]{1,0:T(8,128)(2,1)} %fusion.16.own_value_ref, bf16[32,2,80,128]{3,2,1,0:T(8,128)(2,1)} %bitcast.49), custom_call_target="tpu_custom_call" | custom-call | flops 4831838208 | bytes 1474560 | tf_op jit(solution)/shard_map/attend/pallas_call | solution.py:337
  102.5 4.0 %convolution_convert_fusion = bf16[512,2560]{1,0:T(8,128)(2,1)} fusion(bf16[320,512]{1,0:T(8,128)(2,1)} %bitcast.50, bf16[320,2560]{1,0:T(8,128)(2,1)S(1)} %copy-done), kind=kOutput, calls=%fused_computation.6 | convolution fusion | flops 840171520 | bytes 4587520 | tf_op jit(solution)/shard_map/dot_general | solution.py:787
  106.5 65.4 %sum_middle.1 = (bf16[512,2560]{1,0:T(8,128)(2,1)}, bf16[512,2560]{1,0:T(8,128)(2,1)}) custom-call(bf16[8,2,32,2560]{3,2,1,0:T(8,128)(2,1)} %bitcast.44, bf16[512,2560]{1,0:T(8,128)(2,1)} %token_ref.1, f32[1,2560]{1,0:T(1,128)} %reshape.243.gain_ref), custom_call_target="tpu_custom_call" | custom-call | bytes 200000000 | tf_op jit(solution)/shard_map/sum_middle/pallas_call | solution.py:569
  171.9 0.6 iota_compare_fusion.4
  172.6 33.7 %feed_forward.1 = f32[320,512]{1,0:T(8,128)} custom-call(bf16[512,2560]{1,0:T(8,128)(2,1)} %get-tuple-element.12.normed_ref, bf16[512,2560]{1,0:T(8,128)(2,1)} %get-tuple-element.13.middle_hbm, bf16[2560,1792]{1,0:T(8,128)(2,1)} %all-gather.2.cloned.1.call-done.pair_hbm, bf16[864,2560]{1,0:T(8,128)(2,1)} %down_hbm.1), custom_call_target="tpu_custom_call" | custom-call | tf_op jit(solution)/shard_map/feed_forward/pallas_call | solution.py:670
  206.3 1.9 fusion.7
  (58 shorter events, 4.1 us)
Async XLA Ops:
  6.5 96.0 %copy-start = (bf16[320,2560]{1,0:T(8,128)(2,1)S(1)}, bf16[320,2560]{1,0:T(8,128)(2,1)}, u32[]{:S(2)}) copy-start(bf16[320,2560]{1,0:T(8,128)(2,1)} %param.22) | copy-start | bytes 4915204
  6.5 166.0 %all-gather.2.cloned.1.call-start = ((), (), s32[]{:S(2)}) async-start(), calls=%async_computation | async-start | bytes 9748480 | tf_op jit(solution)/shard_map/all_gather | solution.py:757
  10.6 2.9 %copy-start.4 = (f32[20,640]{1,0:T(8,128)S(1)}, f32[20,640]{1,0:T(8,128)}, u32[]{:S(2)}) copy-start(f32[20,640]{1,0:T(8,128)} %param.18) | copy-start | bytes 153604
  10.6 3.0 %copy-start.5 = (f32[20,640]{1,0:T(8,128)S(1)}, f32[20,640]{1,0:T(8,128)}, u32[]{:S(2)}) copy-start(f32[20,640]{1,0:T(8,128)} %param.19) | copy-start | bytes 153604
  10.6 3.1 %copy-start.3 = (f32[20,2560]{1,0:T(8,128)S(1)}, f32[20,2560]{1,0:T(8,128)}, u32[]{:S(2)}) copy-start(f32[20,2560]{1,0:T(8,128)} %param.17) | copy-start | bytes 614404
  11.8 2.1 copy-start.2
  16.5 52.9 %copy-start.8 = (f32[2560]{0:T(1024)S(1)}, f32[2560]{0:T(1024)}, u32[]{:S(2)}) copy-start(f32[2560]{0:T(1024)} %param.15) | copy-start | bytes 30724
  66.9 2.5 %copy-start.1 = (bf16[512,2560]{1,0:T(8,128)(2,1)S(1)}, bf16[512,2560]{1,0:T(8,128)(2,1)}, u32[]{:S(2)}) copy-start(bf16[512,2560]{1,0:T(8,128)(2,1)} %token_ref.1) | copy-start | bytes 7864324
  69.4 3.4 %copy-start.9 = (s32[16]{0:T(128)S(1)}, s32[16]{0:T(128)}, u32[]{:S(2)}) copy-start(s32[16]{0:T(128)} %param.26) | copy-start | bytes 196
  69.4 4.0 %copy-start.10 = (s32[16]{0:T(128)S(1)}, s32[16]{0:T(128)}, u32[]{:S(2)}) copy-start(s32[16]{0:T(128)} %param.27) | copy-start | bytes 196
  69.4 4.7 %copy-start.7 = (s32[128]{0:T(128)S(1)}, s32[128]{0:T(128)}, u32[]{:S(2)}) copy-start(s32[128]{0:T(128)} %param.25) | copy-start | bytes 1540
  69.4 5.1 %copy-start.6 = (f32[2560]{0:T(1024)S(1)}, f32[2560]{0:T(1024)}, u32[]{:S(2)}) copy-start(f32[2560]{0:T(1024)} %param.16) | copy-start | bytes 30724
Sparse Core Ops, SparseCore 0:
  67.0 89.6 all-gather.1

commit v8 on v7

--- a/solution.py
+++ b/solution.py
@@ -80,9 +80,11 @@
 
 
 def regroup_kernel(
-    n_kv, n_blk, first_ref, second_ref, cache_ref, first_out, second_out, cache_out,
-    first_in, second_in, cache_in, whole, stage_a, stage_b,
+    n_kv, n_blk, first_ref, second_ref, cache_ref, extra_ref, token_ref, gain_ref,
+    projected_ref, second_out, cache_out,
+    first_in, second_in, cache_in, whole, extra, normed, weights, stage_a, stage_b,
     first_send, first_recv, second_send, second_recv, cache_send, cache_recv, send, recv,
+    extra_send, extra_recv,
 ):
     me_kv, me = lax.axis_index("kv"), lax.axis_index("blk")
     rows = first_ref.shape[1]
@@ -129,7 +131,21 @@
         stage_a[group * rows : (group + 1) * rows, :] = first_in[group].astype(jnp.float32)
     whole[0] = stage_a[...].astype(jnp.bfloat16)
 
-    passed = {}
+    extra[0] = extra_ref[...]
+
+    passed, passed_extra = {}, {}
+
+    def pass_extra(held, peer, slot):
+        copy = pltpu.make_async_remote_copy(
+            src_ref=extra.at[held],
+            dst_ref=extra.at[slot],
+            send_sem=extra_send.at[slot - 1],
+            recv_sem=extra_recv.at[slot - 1],
+            device_id={"blk": peer},
+            device_id_type=MESH,
+        )
+        copy.start()
+        passed_extra[slot] = copy
 
     def pass_on(held, peer, slot):
         copy = pltpu.make_async_remote_copy(
@@ -153,11 +169,25 @@
         pass_on(0, along(step), 2 * step)
     pass_on(0, sibling, 1)
     seconds = swap(second_ref, second_in, second_send, second_recv)
+
+    @pl.loop(0, token_ref.shape[0] // 64)
+    def _(part):
+        lines = pl.ds(pl.multiple_of(part * 64, 64), 64)
+        values = token_ref[lines, :].astype(jnp.float32)
+        mean_square = jnp.mean(values * values, axis=-1, keepdims=True)
+        normed[lines, :] = (
+            values * lax.rsqrt(mean_square + EPSILON) * gain_ref[...]
+        ).astype(jnp.bfloat16)
+
     passed[8].wait_recv()
     for step in (1, 3, 2):
         pass_on(8, along(step), 8 + 2 * step)
     pass_on(8, sibling, 9)
     deals = fan_out(n_blk, deal)
+    pass_extra(0, across, 8)
+    for step in (1, 3, 2):
+        pass_extra(0, along(step), 2 * step)
+    pass_extra(0, sibling, 1)
 
     for base in (0, 8):
         for step in (1, 3, 2):
@@ -170,54 +200,87 @@
     for group in range(n_kv):
         stage_b[group * rows : (group + 1) * rows, :] = second_in[group].astype(jnp.float32)
     second_out[...] = stage_b[...].astype(jnp.bfloat16)
+    passed_extra[8].wait_recv()
+    for step in (1, 3, 2):
+        pass_extra(8, along(step), 8 + 2 * step)
+    pass_extra(8, sibling, 9)
+
+    def owner_of(base, step, other):
+        return (
+            lax.rem(half + base // 8, 2) * 8
+            + lax.rem(line + 4 - step, 4) * 2
+            + lax.rem(core + other, 2)
+        )
+
+    tall = whole.shape[1]
     for base in (0, 8):
         for step in range(4):
             for other in range(2):
                 slot = base + 2 * step + other
                 if other:
                     passed[slot].wait_recv()
-                owner = (
-                    lax.rem(half + base // 8, 2) * 8
-                    + lax.rem(line + 4 - step, 4) * 2
-                    + lax.rem(core + other, 2)
-                )
-                first_out[owner] = whole[slot]
-    cache_out[me] = cache_ref[me]
+                place = pl.multiple_of(owner_of(base, step, other) * tall, tall)
+                weights[pl.ds(place, tall), :] = whole[slot]
+
+    @pl.loop(0, normed.shape[0] // 128)
+    def _(part):
+        lines = pl.ds(pl.multiple_of(part * 128, 128), 128)
+        projected_ref[lines, :] = jnp.dot(
+            normed[lines, :], weights[...], preferred_element_type=jnp.float32
+        )
+
+    for base in (0, 8):
+        for step in (1, 3, 2):
+            slot = base + 2 * step
+            passed_extra[slot].wait_recv()
+            pass_extra(slot, sibling, slot + 1)
+    for base in (0, 8):
+        for step in range(4):
+            for other in range(2):
+                slot = base + 2 * step + other
+                if other:
+                    passed_extra[slot].wait_recv()
+                cache_out[owner_of(base, step, other), 1] = extra[slot]
+    cache_out[me, 0] = cache_ref[me]
     for step in range(1, n_blk):
         deals[step - 1].wait_recv()
-        cache_out[lax.rem(me + n_blk - step, n_blk)] = cache_in[step - 1]
-    for copy in firsts + seconds + deals + list(passed.values()):
+        cache_out[lax.rem(me + n_blk - step, n_blk), 0] = cache_in[step - 1]
+    for copy in firsts + seconds + deals + [*passed.values(), *passed_extra.values()]:
         copy.wait_send()
 
 
-def regroup(n_kv, n_blk, first, second, cached):
+def regroup(n_kv, n_blk, first, second, cached, extra, tokens, gain):
     rows = first.shape[1]
     tall = n_kv * rows
     first_width, second_width = first.shape[2], second.shape[2]
     half = jnp.bfloat16
     dma = pltpu.SemaphoreType.DMA
+    blocks = (n_blk, 2) + cached.shape[1:]
     return pl.pallas_call(
         functools.partial(regroup_kernel, n_kv, n_blk),
         name="regroup",
         out_shape=(
-            jax.ShapeDtypeStruct((n_blk, tall, first_width), half),
+            jax.ShapeDtypeStruct((tokens.shape[0], first_width), jnp.float32),
             jax.ShapeDtypeStruct((tall, second_width), half),
-            jax.ShapeDtypeStruct(cached.shape, half),
+            jax.ShapeDtypeStruct(blocks, half),
         ),
-        in_specs=[VMEM_SPEC] * 3,
+        in_specs=[VMEM_SPEC] * 6,
         out_specs=(VMEM_SPEC,) * 3,
         scratch_shapes=[
             pltpu.VMEM(first.shape, half),
             pltpu.VMEM(second.shape, half),
             pltpu.VMEM((n_blk - 1,) + cached.shape[1:], half),
             pltpu.VMEM((n_blk, tall, first_width), half),
+            pltpu.VMEM((n_blk,) + extra.shape, half),
+            pltpu.VMEM(tokens.shape, half),
+            pltpu.VMEM((n_blk * tall, first_width), half),
             pltpu.VMEM((tall, first_width), jnp.float32),
             pltpu.VMEM((tall, second_width), jnp.float32),
         ]
         + [dma((n_kv - 1,))] * 4
-        + [dma((n_blk - 1,))] * 4,
+        + [dma((n_blk - 1,))] * 6,
         compiler_params=pltpu.CompilerParams(collective_id=2, has_side_effects=True),
-    )(first, second, cached)
+    )(first, second, cached, extra, tokens, gain.reshape(1, -1))
 
 
 LIFT = 1.0 / math.sqrt(HD) * math.log2(math.e)
@@ -738,25 +801,28 @@
     global_rank, local_rank = slot_ranks(slot_prompt, prompts, slots)
     own_prompts = lax.dynamic_slice_in_dim(slot_prompt, blk_index * slots, slots)
     own_ranks = lax.dynamic_slice_in_dim(local_rank, blk_index * slots, slots)
-    placed = own_prompts * CAP + own_ranks
     buffer_ids = jnp.arange(prompts * CAP, dtype=jnp.int32)
-    matches = placed[None, :] == buffer_ids[:, None]
-    source_slot = jnp.sum(
-        jnp.where(matches, jnp.arange(slots, dtype=jnp.int32)[None, :], 0), axis=1
-    )
+    own_slots = jnp.arange(slots, dtype=jnp.int32)
+    wanted = jnp.arange(prompts + 1, dtype=jnp.int32)[:, None]
+    matches = jnp.where(
+        wanted < prompts,
+        (own_prompts[None, :] == wanted) & (own_ranks[None, :] == 0),
+        own_ranks[None, :] == 1,
+    )
+    source_slot = jnp.sum(jnp.where(matches, own_slots[None, :], 0), axis=1)
     by_slot = jnp.transpose(cache.reshape(2, slots, HD, BLOCK), (1, 0, 2, 3))
-    outgoing = jnp.take(by_slot, source_slot, axis=0, mode="clip").reshape(prompts, CAP, 2, HD, BLOCK)
-    w_first, w_second, arrived = regroup(
+    outgoing = jnp.take(by_slot, source_slot, axis=0, mode="clip")
+    projected, w_second, arrived = regroup(
         groups,
         n_blocks,
         pack_groups((w_query, w_key, w_value), groups),
         pack_pairs(w_gate, w_up, groups),
-        outgoing,
-    )
-    w_qkv = w_first.reshape(-1, w_first.shape[2])
+        outgoing[:prompts],
+        outgoing[prompts],
+        tokens,
+        attn_gain,
+    )
     w_pair = lax.all_gather(w_second, "blk", axis=0, tiled=True)
-    normed = rms_scale(tokens, attn_gain)
-    projected = jnp.dot(normed, w_qkv, preferred_element_type=jnp.float32)
     queries = rotate(projected[:, :query_width].reshape(new_rows, -1, HD), positions).astype(
         jnp.bfloat16
     )

time: 215 us -> 211 us (0.981)
  local copies, waits for them, and re-layouts: 7.81 us -> 15.2 us
  other arithmetic: 15 us -> 10.9 us
  Pallas kernels: 171 us -> 167 us
  matrix products: 7.32 us -> 3.98 us
    pallas_call x1, Pallas kernels: 50.3 us -> 46.6 us  [regroup(): pl.pallas_call(functools.partial(regroup_kernel, n_kv, n_blk), name='regr...]
    dot_general x1 -> x0, matrix products: 3.34 us -> none  [shards(): projected = jnp.dot(normed, w_qkv, preferred_element_type=jnp.float32)]
    pallas_call x0 -> x1, local copies, waits for them, and re-layouts: none -> 2.59 us  [regroup(): pl.pallas_call(functools.partial(regroup_kernel, n_kv, n_blk), name='regr...]
    reduce_sum x2 -> x1, other arithmetic: 2.56 us -> 0.09 us  [shards(): source_slot = jnp.sum(jnp.where(matches, own_slots[None, :], 0), axis=1)]
  transfers between devices with their start and end apart: 1 -> 1, of which waited for: 0 -> 0; matrix products, arithmetic and copies ran while one was open for 9% -> 8% of each run, Pallas kernels for 40% -> 41%
where the time goes in v8:
time: 211 us
  Pallas kernels  167 us (79%)
  local copies, waits for them, and re-layouts  15.2 us (7%)
  between operations  13.7 us (6%)
  other arithmetic  10.9 us (5%)
  matrix products  3.98 us (2%)
    pallas_call x1, Pallas kernels, sum_middle(): pl.pallas_call(functools.partial(middle_kernel, n), name='sum_middle', co...  65.2 us
    pallas_call x1, Pallas kernels, regroup(): pl.pallas_call(functools.partial(regroup_kernel, n_kv, n_blk), name='regr...  46.6 us
    pallas_call x1, Pallas kernels, feed_forward(): pl.pallas_call(functools.partial(hidden_kernel, n), name='feed_forward',...  33.5 us
    pallas_call x1, Pallas kernels, attend(): pl.pallas_call(attention_kernel, name='attend', grid=(heads,), out_shape=...  21.6 us
  transfers between devices with their start and end apart: 1, of which 0 were waited for; matrix products, arithmetic and copies ran while one was open for 8% of the time, Pallas kernels for 41%

profile of v8, /device:TPU:1, one launch (start us, length us, event | category | flops | bytes accessed | tf_op | source)
XLA Modules:
  0.0 210.8 jit_solution(7026666010195793601)
XLA Ops:
  6.6 0.9 eq.63
  8.1 0.7 dynamic_slice.14
  9.0 1.7 gather_fusion
  10.7 0.9 slice.39.cache_ref
  11.6 0.6 slice_bitcast_fusion.1.extra_ref
  12.8 1.2 convert_element_type.58
  14.7 0.9 copy.30.second_ref
  16.1 0.6 reshape.233.gain_ref
  16.7 0.8 pad_maximum_fusion.1.first_ref
  17.5 46.6 %regroup.1 = (f32[512,480]{1,0:T(8,128)}, bf16[160,1792]{1,0:T(8,128)(2,1)}, bf16[16,2,2,80,128]{4,3,2,1,0:T(8,128)(2,1)}) custom-call(bf16[8,20,480]{2,1,0:T(8,128)(2,1)} %pad_maximum_fusion.1.first_ref, bf16[8,20,1792]{2,1,0:T(8,128)(2,1)} %copy.30.second_ref, bf16[16,2,80,128]{3,2,1,0:T(8,128)(2,1)} %slice.39.cache_ref, ...), custom_call_target="tpu_custom_call" | custom-call | tf_op jit(solution)/shard_map/regroup/pallas_call | solution.py:259
  64.2 2.6 %copy.32 = f32[512,480]{0,1:T(8,128)} copy(f32[512,480]{1,0:T(8,128)} %get-tuple-element.10) | data formatting | bytes 1966080 | tf_op jit(solution)/shard_map/regroup/pallas_call | solution.py:259
  67.8 0.6 dynamic_slice.12
  69.7 1.9 pad_add_fusion.scalars
  71.6 0.7 add_convert_fusion.1
  72.3 0.9 slice_bitcast_fusion
  73.6 0.6 maximum_bitcast_fusion.1.own_key_ref
  74.7 0.8 maximum_bitcast_fusion.query_ref
  75.5 1.6 fusion.9.own_value_ref
  77.0 21.6 %attend.1 = bf16[4,80,512]{2,1,0:T(8,128)(2,1)} custom-call(s32[66]{0:T(128)} %pad_add_fusion.scalars, bf16[4,80,512]{2,1,0:T(8,128)(2,1)} %maximum_bitcast_fusion.query_ref, bf16[80,512]{1,0:T(8,128)(2,1)} %maximum_bitcast_fusion.1.own_key_ref, bf16[80,512]{1,0:T(8,128)(2,1)} %fusion.9.own_value_ref, bf16[32,2,80,128]{3,2,1,0:T(8,128)(2,1)} %bitcast.46), custom_call_target="tpu_custom_call" | custom-call | flops 4831838208 | bytes 1474560 | tf_op jit(solution)/shard_map/attend/pallas_call | solution.py:400
  98.7 4.0 %convolution_convert_fusion = bf16[512,2560]{1,0:T(8,128)(2,1)} fusion(bf16[320,512]{1,0:T(8,128)(2,1)} %bitcast.47, bf16[320,2560]{1,0:T(8,128)(2,1)S(1)} %copy-done), kind=kOutput, calls=%fused_computation.1 | convolution fusion | flops 840171520 | bytes 4587520 | tf_op jit(solution)/shard_map/dot_general | solution.py:853
  102.7 65.2 %sum_middle.1 = (bf16[512,2560]{1,0:T(8,128)(2,1)}, bf16[512,2560]{1,0:T(8,128)(2,1)}) custom-call(bf16[8,2,32,2560]{3,2,1,0:T(8,128)(2,1)} %bitcast.41, bf16[512,2560]{1,0:T(8,128)(2,1)} %token_ref.3, f32[1,2560]{1,0:T(1,128)} %reshape.239.gain_ref), custom_call_target="tpu_custom_call" | custom-call | bytes 200000000 | tf_op jit(solution)/shard_map/sum_middle/pallas_call | solution.py:632
  167.9 0.7 iota_compare_fusion.4
  168.6 33.5 %feed_forward.1 = f32[320,512]{1,0:T(8,128)} custom-call(bf16[512,2560]{1,0:T(8,128)(2,1)} %get-tuple-element.12.normed_ref, bf16[512,2560]{1,0:T(8,128)(2,1)} %get-tuple-element.13.middle_hbm, bf16[2560,1792]{1,0:T(8,128)(2,1)} %all-gather.2.cloned.1.call-done.pair_hbm, bf16[864,2560]{1,0:T(8,128)(2,1)} %down_hbm.1), custom_call_target="tpu_custom_call" | custom-call | tf_op jit(solution)/shard_map/feed_forward/pallas_call | solution.py:733
  202.1 1.9 fusion
  (62 shorter events, 5.6 us)
Async XLA Ops:
  6.5 92.1 %copy-start = (bf16[320,2560]{1,0:T(8,128)(2,1)S(1)}, bf16[320,2560]{1,0:T(8,128)(2,1)}, u32[]{:S(2)}) copy-start(bf16[320,2560]{1,0:T(8,128)(2,1)} %param.22) | copy-start | bytes 4915204
  6.5 5.7 %copy-start.2 = (f32[20,6912]{1,0:T(8,128)S(1)}, f32[20,6912]{1,0:T(8,128)}, u32[]{:S(2)}) copy-start(f32[20,6912]{1,0:T(8,128)} %param.20) | copy-start | bytes 1658884
  6.5 162.1 %all-gather.2.cloned.1.call-start = ((), (), s32[]{:S(2)}) async-start(), calls=%async_computation | async-start | bytes 9748480 | tf_op jit(solution)/shard_map/all_gather | solution.py:825
  12.8 2.9 %copy-start.4 = (f32[20,640]{1,0:T(8,128)S(1)}, f32[20,640]{1,0:T(8,128)}, u32[]{:S(2)}) copy-start(f32[20,640]{1,0:T(8,128)} %param.18) | copy-start | bytes 153604
  12.8 3.0 %copy-start.5 = (f32[20,640]{1,0:T(8,128)S(1)}, f32[20,640]{1,0:T(8,128)}, u32[]{:S(2)}) copy-start(f32[20,640]{1,0:T(8,128)} %param.19) | copy-start | bytes 153604
  12.8 3.1 %copy-start.3 = (f32[20,2560]{1,0:T(8,128)S(1)}, f32[20,2560]{1,0:T(8,128)}, u32[]{:S(2)}) copy-start(f32[20,2560]{1,0:T(8,128)} %param.17) | copy-start | bytes 614404
  14.0 2.1 copy-start.6
  64.2 2.7 %copy-start.1 = (f32[512,480]{1,0:T(8,128)S(1)}, f32[512,480]{1,0:T(8,128)}, u32[]{:S(2)}) copy-start(f32[512,480]{1,0:T(8,128)} %get-tuple-element.10) | copy-start | bytes 2949124
  64.2 3.0 %copy-start.9 = (s32[16]{0:T(128)S(1)}, s32[16]{0:T(128)}, u32[]{:S(2)}) copy-start(s32[16]{0:T(128)} %param.26) | copy-start | bytes 196
  64.2 3.6 %copy-start.10 = (s32[16]{0:T(128)S(1)}, s32[16]{0:T(128)}, u32[]{:S(2)}) copy-start(s32[16]{0:T(128)} %param.27) | copy-start | bytes 196
  64.2 4.2 %copy-start.8 = (s32[128]{0:T(128)S(1)}, s32[128]{0:T(128)}, u32[]{:S(2)}) copy-start(s32[128]{0:T(128)} %param.25) | copy-start | bytes 1540
  64.2 4.6 %copy-start.7 = (f32[2560]{0:T(1024)S(1)}, f32[2560]{0:T(1024)}, u32[]{:S(2)}) copy-start(f32[2560]{0:T(1024)} %param.16) | copy-start | bytes 30724
Sparse Core Ops, SparseCore 0:
  64.3 88.0 all-gather.1

commit v9 on v8

--- a/solution.py
+++ b/solution.py
@@ -164,8 +164,27 @@
 
     across = lax.rem(me + 8, n_blk)
     sibling = me + 1 - 2 * core
+    near_rows = whole.shape[1] // 2
+    relayed = []
+
+    def relay(base):
+        for part, step in enumerate((1, 3)):
+            lines = pl.ds(part * near_rows, near_rows)
+            index = n_blk - 1 + base // 4 + part
+            passed[base + 2 * step].wait_recv()
+            copy = pltpu.make_async_remote_copy(
+                src_ref=whole.at[base + 2 * step, lines],
+                dst_ref=whole.at[base + 4, lines],
+                send_sem=send.at[index],
+                recv_sem=recv.at[index],
+                device_id={"blk": along(step)},
+                device_id_type=MESH,
+            )
+            copy.start()
+            relayed.append(copy)
+
     pass_on(0, across, 8)
-    for step in (1, 3, 2):
+    for step in (1, 3):
         pass_on(0, along(step), 2 * step)
     pass_on(0, sibling, 1)
     seconds = swap(second_ref, second_in, second_send, second_recv)
@@ -180,20 +199,25 @@
         ).astype(jnp.bfloat16)
 
     passed[8].wait_recv()
-    for step in (1, 3, 2):
+    for step in (1, 3):
         pass_on(8, along(step), 8 + 2 * step)
     pass_on(8, sibling, 9)
+    relay(0)
+    for step in (1, 3):
+        pass_on(2 * step, sibling, 2 * step + 1)
+    relay(8)
     deals = fan_out(n_blk, deal)
     pass_extra(0, across, 8)
     for step in (1, 3, 2):
         pass_extra(0, along(step), 2 * step)
     pass_extra(0, sibling, 1)
 
+    for step in (1, 3):
+        pass_on(8 + 2 * step, sibling, 9 + 2 * step)
     for base in (0, 8):
-        for step in (1, 3, 2):
-            slot = base + 2 * step
-            passed[slot].wait_recv()
-            pass_on(slot, sibling, slot + 1)
+        for copy in relayed[base // 4 : base // 4 + 2]:
+            copy.wait_recv()
+        pass_on(base + 4, sibling, base + 5)
     second_in[me_kv] = second_ref[me_kv]
     for copy in seconds:
         copy.wait_recv()
@@ -245,7 +269,7 @@
     for step in range(1, n_blk):
         deals[step - 1].wait_recv()
         cache_out[lax.rem(me + n_blk - step, n_blk), 0] = cache_in[step - 1]
-    for copy in firsts + seconds + deals + [*passed.values(), *passed_extra.values()]:
+    for copy in firsts + seconds + deals + [*passed.values(), *passed_extra.values()] + relayed:
         copy.wait_send()
 
 
@@ -278,7 +302,9 @@
             pltpu.VMEM((tall, second_width), jnp.float32),
         ]
         + [dma((n_kv - 1,))] * 4
-        + [dma((n_blk - 1,))] * 6,
+        + [dma((n_blk - 1,))] * 2
+        + [dma((n_blk + 3,))] * 2
+        + [dma((n_blk - 1,))] * 2,
         compiler_params=pltpu.CompilerParams(collective_id=2, has_side_effects=True),
     )(first, second, cached, extra, tokens, gain.reshape(1, -1))
 
@@ -575,7 +601,25 @@
     came = {}
 
     def spread(held, slot, peer):
-        came[slot] = links.go(whole.at[held], whole.at[slot], peer, index_of(*slot))
+        came[slot] = [links.go(whole.at[held], whole.at[slot], peer, index_of(*slot))]
+
+    def wait(slot):
+        for copy in came[slot]:
+            copy.wait_recv()
+
+    def relay(side, half):
+        came[2, side, half] = []
+        for quarter, step in enumerate((1, 3)):
+            held = pl.ds(quarter * (part // 2), part // 2)
+            wait((step, side, half))
+            came[2, side, half].append(
+                links.go(
+                    whole.at[step, side, half, held],
+                    whole.at[2, side, half, held],
+                    peer_at(step),
+                    index_of(2, side, half) if quarter == 0 else 2 * n - 2 + side + half,
+                )
+            )
 
     def settle(slot):
         place = rows_of(*slot)
@@ -592,35 +636,38 @@
 
     own_a = token_ref[rows_of(0, 0, 0), :].astype(jnp.float32)
     whole[0, 0, 0] = (own_a + terms.finish_a()).astype(jnp.bfloat16)
-    for step in terms.steps:
+    for step in (1, 3):
         spread((0, 0, 0), (step, 0, 0), peer_at(step))
     spread((0, 0, 0), (0, 1, 0), terms.partner)
     own_b = token_ref[rows_of(0, 0, 1), :].astype(jnp.float32)
     whole[0, 0, 1] = (own_b + terms.finish_b()).astype(jnp.bfloat16)
     spread((0, 0, 1), (0, 1, 1), terms.partner)
-    for step in terms.steps:
+    for step in (1, 3):
         spread((0, 0, 1), (step, 0, 1), peer_at(step))
     settle((0, 0, 0))
+    relay(0, 0)
+    for step in (1, 3):
+        spread((step, 0, 0), (step, 1, 0), terms.partner)
+    wait((0, 1, 1))
+    for step in (1, 3):
+        spread((0, 1, 1), (step, 1, 1), peer_at(step))
+    relay(0, 1)
+    wait((2, 0, 0))
+    spread((2, 0, 0), (2, 1, 0), terms.partner)
     settle((0, 0, 1))
-    for step in terms.steps:
-        came[step, 0, 0].wait_recv()
-        spread((step, 0, 0), (step, 1, 0), terms.partner)
-        if step == terms.steps[0]:
-            came[0, 1, 1].wait_recv()
-            for far in terms.steps:
-                spread((0, 1, 1), (far, 1, 1), peer_at(far))
     settle((0, 1, 1))
-    for step in terms.steps:
+    relay(1, 1)
+    for step in (1, 3, 2):
         settle((step, 0, 0))
-    came[0, 1, 0].wait_recv()
+    wait((0, 1, 0))
     settle((0, 1, 0))
-    for step, side, half in (
-        [(step, 0, 1) for step in terms.steps]
-        + [(step, 1, 0) for step in terms.steps]
-        + [(step, 1, 1) for step in terms.steps]
-    ):
-        came[step, side, half].wait_recv()
-        settle((step, side, half))
+    settle((1, 0, 1))
+    settle((3, 0, 1))
+    settle((1, 1, 1))
+    settle((3, 1, 1))
+    for slot in ((2, 0, 1), (1, 1, 0), (3, 1, 0), (2, 1, 1), (2, 1, 0)):
+        wait(slot)
+        settle(slot)
     terms.close()
     links.close()
 
@@ -638,7 +685,7 @@
         out_specs=(VMEM_SPEC, VMEM_SPEC),
         scratch_shapes=scatter_scratch(n, (piece // 2, width))
         + [pltpu.VMEM((n // 2, 2, 2, piece // 2, width), jnp.bfloat16)]
-        + [pltpu.SemaphoreType.DMA((2 * n - 2,))] * 2,
+        + [pltpu.SemaphoreType.DMA((2 * n + 1,))] * 2,
         compiler_params=pltpu.CompilerParams(collective_id=0, has_side_effects=True),
     )(partial_out.reshape(n, 2, piece // 2, width), tokens, mlp_gain.reshape(1, width))
 

time: 211 us -> 207 us (0.981)
  Pallas kernels: 167 us -> 162 us
    pallas_call x1, Pallas kernels: 65.2 us -> 61.2 us  [sum_middle(): pl.pallas_call(functools.partial(middle_kernel, n), name='sum_middle', co...]
    pallas_call x1, Pallas kernels: 46.6 us -> 44.3 us  [regroup(): pl.pallas_call(functools.partial(regroup_kernel, n_kv, n_blk), name='regr...]
  transfers between devices with their start and end apart: 1 -> 1, of which waited for: 0 -> 0; matrix products, arithmetic and copies ran while one was open for 8% -> 8% of each run, Pallas kernels for 41% -> 40%
where the time goes in v9:
time: 207 us; the launch traced here: 206 us
  Pallas kernels  162 us (78%)
  local copies, waits for them, and re-layouts  15.2 us (7%)
  between operations  13.7 us (7%)
  other arithmetic  10.9 us (5%)
  matrix products  3.98 us (2%)
    pallas_call x1, Pallas kernels, sum_middle(): pl.pallas_call(functools.partial(middle_kernel, n), name='sum_middle', co...  61.2 us
    pallas_call x1, Pallas kernels, regroup(): pl.pallas_call(functools.partial(regroup_kernel, n_kv, n_blk), name='regr...  44.3 us
    pallas_call x1, Pallas kernels, feed_forward(): pl.pallas_call(functools.partial(hidden_kernel, n), name='feed_forward',...  35.1 us
    pallas_call x1, Pallas kernels, attend(): pl.pallas_call(attention_kernel, name='attend', grid=(heads,), out_shape=...  21.6 us
  transfers between devices with their start and end apart: 1, of which 0 were waited for; matrix products, arithmetic and copies ran while one was open for 8% of the time, Pallas kernels for 40%

profile of v9, /device:TPU:1, one launch (start us, length us, event | category | flops | bytes accessed | tf_op | source)
XLA Modules:
  0.0 206.1 jit_solution(12810797445185767045)
XLA Ops:
  6.6 0.9 eq.63
  8.1 0.7 dynamic_slice.14
  9.0 1.7 gather_fusion
  10.7 0.9 slice.39.cache_ref
  11.6 0.6 slice_bitcast_fusion.1.extra_ref
  12.8 1.2 convert_element_type.58
  14.7 0.9 copy.30.second_ref
  16.1 0.6 reshape.233.gain_ref
  16.7 0.8 pad_maximum_fusion.1.first_ref
  17.5 44.3 %regroup.1 = (f32[512,480]{1,0:T(8,128)}, bf16[160,1792]{1,0:T(8,128)(2,1)}, bf16[16,2,2,80,128]{4,3,2,1,0:T(8,128)(2,1)}) custom-call(bf16[8,20,480]{2,1,0:T(8,128)(2,1)} %pad_maximum_fusion.1.first_ref, bf16[8,20,1792]{2,1,0:T(8,128)(2,1)} %copy.30.second_ref, bf16[16,2,80,128]{3,2,1,0:T(8,128)(2,1)} %slice.39.cache_ref, ...), custom_call_target="tpu_custom_call" | custom-call | tf_op jit(solution)/shard_map/regroup/pallas_call | solution.py:283
  61.9 2.6 %copy.32 = f32[512,480]{0,1:T(8,128)} copy(f32[512,480]{1,0:T(8,128)} %get-tuple-element.10) | data formatting | bytes 1966080 | tf_op jit(solution)/shard_map/regroup/pallas_call | solution.py:283
  65.5 0.6 dynamic_slice.12
  67.4 1.9 pad_add_fusion.scalars
  69.3 0.7 add_convert_fusion.1
  70.0 1.0 slice_bitcast_fusion
  71.3 0.6 maximum_bitcast_fusion.1.own_key_ref
  72.4 0.8 maximum_bitcast_fusion.query_ref
  73.2 1.6 fusion.9.own_value_ref
  74.7 21.6 %attend.1 = bf16[4,80,512]{2,1,0:T(8,128)(2,1)} custom-call(s32[66]{0:T(128)} %pad_add_fusion.scalars, bf16[4,80,512]{2,1,0:T(8,128)(2,1)} %maximum_bitcast_fusion.query_ref, bf16[80,512]{1,0:T(8,128)(2,1)} %maximum_bitcast_fusion.1.own_key_ref, bf16[80,512]{1,0:T(8,128)(2,1)} %fusion.9.own_value_ref, bf16[32,2,80,128]{3,2,1,0:T(8,128)(2,1)} %bitcast.46), custom_call_target="tpu_custom_call" | custom-call | flops 4831838208 | bytes 1474560 | tf_op jit(solution)/shard_map/attend/pallas_call | solution.py:426
  96.4 4.0 %convolution_convert_fusion = bf16[512,2560]{1,0:T(8,128)(2,1)} fusion(bf16[320,512]{1,0:T(8,128)(2,1)} %bitcast.47, bf16[320,2560]{1,0:T(8,128)(2,1)S(1)} %copy-done), kind=kOutput, calls=%fused_computation.1 | convolution fusion | flops 840171520 | bytes 4587520 | tf_op jit(solution)/shard_map/dot_general | solution.py:900
  100.4 61.2 %sum_middle.1 = (bf16[512,2560]{1,0:T(8,128)(2,1)}, bf16[512,2560]{1,0:T(8,128)(2,1)}) custom-call(bf16[8,2,32,2560]{3,2,1,0:T(8,128)(2,1)} %bitcast.41, bf16[512,2560]{1,0:T(8,128)(2,1)} %token_ref.3, f32[1,2560]{1,0:T(1,128)} %reshape.239.gain_ref), custom_call_target="tpu_custom_call" | custom-call | bytes 200000000 | tf_op jit(solution)/shard_map/sum_middle/pallas_call | solution.py:679
  161.6 0.7 iota_compare_fusion.4
  162.3 35.1 %feed_forward.1 = f32[320,512]{1,0:T(8,128)} custom-call(bf16[512,2560]{1,0:T(8,128)(2,1)} %get-tuple-element.12.normed_ref, bf16[512,2560]{1,0:T(8,128)(2,1)} %get-tuple-element.13.middle_hbm, bf16[2560,1792]{1,0:T(8,128)(2,1)} %all-gather.2.cloned.1.call-done.pair_hbm, bf16[864,2560]{1,0:T(8,128)(2,1)} %down_hbm.1), custom_call_target="tpu_custom_call" | custom-call | tf_op jit(solution)/shard_map/feed_forward/pallas_call | solution.py:780
  197.4 1.9 fusion
  (62 shorter events, 5.6 us)
Async XLA Ops:
  6.5 89.9 %copy-start = (bf16[320,2560]{1,0:T(8,128)(2,1)S(1)}, bf16[320,2560]{1,0:T(8,128)(2,1)}, u32[]{:S(2)}) copy-start(bf16[320,2560]{1,0:T(8,128)(2,1)} %param.22) | copy-start | bytes 4915204
  6.5 5.7 %copy-start.2 = (f32[20,6912]{1,0:T(8,128)S(1)}, f32[20,6912]{1,0:T(8,128)}, u32[]{:S(2)}) copy-start(f32[20,6912]{1,0:T(8,128)} %param.20) | copy-start | bytes 1658884
  6.5 155.8 %all-gather.2.cloned.1.call-start = ((), (), s32[]{:S(2)}) async-start(), calls=%async_computation | async-start | bytes 9748480 | tf_op jit(solution)/shard_map/all_gather | solution.py:872
  12.8 2.9 %copy-start.4 = (f32[20,640]{1,0:T(8,128)S(1)}, f32[20,640]{1,0:T(8,128)}, u32[]{:S(2)}) copy-start(f32[20,640]{1,0:T(8,128)} %param.18) | copy-start | bytes 153604
  12.8 3.0 %copy-start.5 = (f32[20,640]{1,0:T(8,128)S(1)}, f32[20,640]{1,0:T(8,128)}, u32[]{:S(2)}) copy-start(f32[20,640]{1,0:T(8,128)} %param.19) | copy-start | bytes 153604
  12.8 3.1 %copy-start.3 = (f32[20,2560]{1,0:T(8,128)S(1)}, f32[20,2560]{1,0:T(8,128)}, u32[]{:S(2)}) copy-start(f32[20,2560]{1,0:T(8,128)} %param.17) | copy-start | bytes 614404
  14.0 2.1 %copy-start.6 = (f32[2560]{0:T(1024)S(1)}, f32[2560]{0:T(1024)}, u32[]{:S(2)}) copy-start(f32[2560]{0:T(1024)} %param.15) | copy-start | bytes 30724
  61.9 2.7 %copy-start.1 = (f32[512,480]{1,0:T(8,128)S(1)}, f32[512,480]{1,0:T(8,128)}, u32[]{:S(2)}) copy-start(f32[512,480]{1,0:T(8,128)} %get-tuple-element.10) | copy-start | bytes 2949124
  61.9 3.0 %copy-start.9 = (s32[16]{0:T(128)S(1)}, s32[16]{0:T(128)}, u32[]{:S(2)}) copy-start(s32[16]{0:T(128)} %param.26) | copy-start | bytes 196
  61.9 3.6 %copy-start.10 = (s32[16]{0:T(128)S(1)}, s32[16]{0:T(128)}, u32[]{:S(2)}) copy-start(s32[16]{0:T(128)} %param.27) | copy-start | bytes 196
  61.9 4.2 %copy-start.8 = (s32[128]{0:T(128)S(1)}, s32[128]{0:T(128)}, u32[]{:S(2)}) copy-start(s32[128]{0:T(128)} %param.25) | copy-start | bytes 1540
  61.9 4.6 %copy-start.7 = (f32[2560]{0:T(1024)S(1)}, f32[2560]{0:T(1024)}, u32[]{:S(2)}) copy-start(f32[2560]{0:T(1024)} %param.16) | copy-start | bytes 30724
Sparse Core Ops, SparseCore 0:
  62.0 89.6 all-gather.1

commit v10 on v9

--- a/solution.py
+++ b/solution.py
@@ -20,41 +20,6 @@
 FLOOR_SCORE = -1e30
 EPSILON = 1e-05
 ROPE_BASE = 10000.0
-
-
-def rms_scale(row_data, gain_vec):
-    values = row_data.astype(jnp.float32)
-    mean_square = jnp.mean(values * values, axis=-1, keepdims=True)
-    return (values * lax.rsqrt(mean_square + EPSILON) * gain_vec).astype(jnp.bfloat16)
-
-
-def rotate(values, positions):
-    head_width = values.shape[-1]
-    half_width = head_width // 2
-    frequency = ROPE_BASE ** (-2.0 * jnp.arange(half_width, dtype=jnp.float32) / head_width)
-    angles = positions.astype(jnp.float32)[:, None] * frequency[None, :]
-    cosine = jnp.cos(angles)[:, None, :]
-    sine_wave = jnp.sin(angles)[:, None, :]
-    first_half = values[..., :half_width]
-    second_half = values[..., half_width:]
-    return jnp.concatenate(
-        [
-            first_half * cosine - second_half * sine_wave,
-            second_half * cosine + first_half * sine_wave,
-        ],
-        axis=-1,
-    )
-
-
-def slot_ranks(slot_prompt, prompts, slots):
-    onehot = (slot_prompt[:, None] == jnp.arange(prompts, dtype=jnp.int32)[None, :]).astype(
-        jnp.int32
-    )
-    running = jnp.cumsum(onehot, axis=0)
-    global_rank = jnp.sum(onehot * (running - 1), axis=1)
-    local_count = jnp.cumsum(onehot.reshape(-1, slots, prompts), axis=1).reshape(-1, prompts)
-    local_rank = jnp.sum(onehot * (local_count - 1), axis=1)
-    return (global_rank, local_rank)
 
 
 def pack_groups(matrices, groups):
@@ -249,9 +214,9 @@
     @pl.loop(0, normed.shape[0] // 128)
     def _(part):
         lines = pl.ds(pl.multiple_of(part * 128, 128), 128)
-        projected_ref[lines, :] = jnp.dot(
+        projected_ref[:, lines] = jnp.dot(
             normed[lines, :], weights[...], preferred_element_type=jnp.float32
-        )
+        ).T
 
     for base in (0, 8):
         for step in (1, 3, 2):
@@ -284,7 +249,7 @@
         functools.partial(regroup_kernel, n_kv, n_blk),
         name="regroup",
         out_shape=(
-            jax.ShapeDtypeStruct((tokens.shape[0], first_width), jnp.float32),
+            jax.ShapeDtypeStruct((first_width, tokens.shape[0]), jnp.float32),
             jax.ShapeDtypeStruct((tall, second_width), half),
             jax.ShapeDtypeStruct(blocks, half),
         ),
@@ -313,17 +278,28 @@
 
 
 def attention_kernel(
-    scalars, query_ref, own_key_ref, own_value_ref, blocks_ref, out_ref,
-    keys, values, score_a, score_b, row_max, summed,
+    prompt_ref, prefix_ref, new_ref, projected_ref, cosine_ref, sine_ref, blocks_ref, out_ref,
+    keys, values, score_a, score_b, row_max, summed, scalars,
 ):
+    me = lax.axis_index("blk")
     slots, block = blocks_ref.shape[0], blocks_ref.shape[3]
-    rows = query_ref.shape[2]
+    rows = projected_ref.shape[1]
+    heads = pl.num_programs(0)
     depth = keys.shape[1]
     wide = values.shape[0]
     chunk = rows
     per_chunk = chunk // block
     chunks = slots // per_chunk
-    before, live_rows = scalars[2 * slots], scalars[2 * slots + 1]
+    before, live_rows = prefix_ref[me], new_ref[me]
+
+    def rotated(index):
+        start = pl.multiple_of(index * HD, HD)
+        first = projected_ref[pl.ds(start, HD // 2), :]
+        second = projected_ref[pl.ds(start + HD // 2, HD // 2), :]
+        cosine, sine = cosine_ref[...], sine_ref[...]
+        return jnp.concatenate(
+            [first * cosine - second * sine, second * cosine + first * sine], axis=0
+        )
 
     def padded_key(part, limit):
         spots = lax.broadcasted_iota(jnp.int32, (depth - HD, block), 1)
@@ -334,6 +310,33 @@
     @pl.when(pl.program_id(0) == 0)
     def _():
         ones = jnp.ones((wide - HD, block), jnp.bfloat16)
+
+        def clear(spot, carry):
+            scalars[spot] = 0
+            return carry
+
+        lax.fori_loop(0, 2 * slots, clear, 0)
+        sources = slots // CAP
+        each = prompt_ref.shape[0] // sources
+
+        def find(source, count):
+            rank = jnp.int32(0)
+            for spot in range(each):
+                mine = prompt_ref[source * each + spot] == me
+                target = source * CAP + jnp.minimum(rank, CAP - 1)
+
+                @pl.when(mine)
+                def _(target=target, count=count):
+                    scalars[target] = count
+                    scalars[slots + target] = 1
+
+                rank = rank + mine.astype(jnp.int32)
+                count = count + mine.astype(jnp.int32)
+            return count
+
+        lax.fori_loop(0, sources, find, jnp.int32(0))
+        own_key = rotated(heads)
+        own_value = projected_ref[(heads + 1) * HD : (heads + 2) * HD, :].astype(jnp.bfloat16)
 
         def place(slot, carry):
             limit = jnp.where(
@@ -348,12 +351,12 @@
         for part in range(rows // block):
             near = slice(part * block, (part + 1) * block)
             far = slice(slots * block + part * block, slots * block + (part + 1) * block)
-            keys[far, :] = padded_key(own_key_ref[:, near], live_rows - part * block)
-            values[:, far] = jnp.concatenate([own_value_ref[:, near], ones], axis=0)
+            keys[far, :] = padded_key(own_key[:, near], live_rows - part * block)
+            values[:, far] = jnp.concatenate([own_value[:, near], ones], axis=0)
 
     query = jnp.concatenate(
         [
-            query_ref[0].astype(jnp.float32),
+            rotated(pl.program_id(0)),
             jnp.ones((16, rows), jnp.float32),
             jnp.zeros((depth - HD - 16, rows), jnp.float32),
         ],
@@ -418,23 +421,17 @@
     out_ref[0] = (summed[:HD, :] / summed[HD : HD + 1, :]).astype(jnp.bfloat16)
 
 
-def attend(scalars, query, own_key, own_value, blocks):
-    heads, width, rows = query.shape
-    slots, block = blocks.shape[0], blocks.shape[3]
+def attend(heads, slot_prompt, prefix_len, new_len, projected, cosine, sine, blocks):
+    rows = projected.shape[1]
+    slots, _, width, block = blocks.shape
     span = slots * block + rows
-    whole = pl.BlockSpec(memory_space=pltpu.VMEM)
+    smem = pl.BlockSpec(memory_space=pltpu.SMEM)
     return pl.pallas_call(
         attention_kernel,
         name="attend",
         grid=(heads,),
         out_shape=jax.ShapeDtypeStruct((heads, width, rows), jnp.bfloat16),
-        in_specs=[
-            pl.BlockSpec(memory_space=pltpu.SMEM),
-            pl.BlockSpec((1, width, rows), lambda head: (head, 0, 0)),
-            whole,
-            whole,
-            whole,
-        ],
+        in_specs=[smem, smem, smem] + [VMEM_SPEC] * 4,
         out_specs=pl.BlockSpec((1, width, rows), lambda head: (head, 0, 0)),
         scratch_shapes=[
             pltpu.VMEM((span, 128), jnp.bfloat16),
@@ -443,13 +440,14 @@
             pltpu.VMEM((rows, rows), jnp.float32),
             pltpu.VMEM((1, rows), jnp.float32),
             pltpu.VMEM((96, rows), jnp.float32),
+            pltpu.SMEM((2 * slots,), jnp.int32),
         ],
         cost_estimate=pl.CostEstimate(
             flops=4 * heads * rows * span * 128,
             bytes_accessed=span * 4 * width,
             transcendentals=heads * rows * span,
         ),
-    )(scalars, query, own_key, own_value, blocks)
+    )(slot_prompt, prefix_len, new_len, projected, cosine, sine, blocks)
 
 
 def hail(n, me):
@@ -834,21 +832,18 @@
     groups = lax.axis_size("kv")
     n_blocks = lax.axis_size("blk")
     blk_index = lax.axis_index("blk")
-    kv_index = lax.axis_index("kv")
-    query_width = w_query.shape[1] // groups
-    key_width = w_key.shape[1] // groups
-    kv_local = key_width // HD
     new_rows = tokens.shape[0]
     prompts = prefix_len.shape[0]
     slots = cache.shape[1]
-    prefix_here = prefix_len[blk_index]
-    live_count = new_len[blk_index]
     row_ids = jnp.arange(new_rows, dtype=jnp.int32)
-    positions = prefix_here + row_ids
-    global_rank, local_rank = slot_ranks(slot_prompt, prompts, slots)
+    frequency = ROPE_BASE ** (-2.0 * jnp.arange(HD // 2, dtype=jnp.float32) / HD)
+    positions = (prefix_len[blk_index] + row_ids).astype(jnp.float32)
+    angles = positions[None, :] * frequency[:, None]
     own_prompts = lax.dynamic_slice_in_dim(slot_prompt, blk_index * slots, slots)
-    own_ranks = lax.dynamic_slice_in_dim(local_rank, blk_index * slots, slots)
-    buffer_ids = jnp.arange(prompts * CAP, dtype=jnp.int32)
+    earlier = jnp.tri(slots, k=-1, dtype=jnp.bool_)
+    own_ranks = jnp.sum(
+        ((own_prompts[:, None] == own_prompts[None, :]) & earlier).astype(jnp.int32), axis=1
+    )
     own_slots = jnp.arange(slots, dtype=jnp.int32)
     wanted = jnp.arange(prompts + 1, dtype=jnp.int32)[:, None]
     matches = jnp.where(
@@ -870,32 +865,15 @@
         attn_gain,
     )
     w_pair = lax.all_gather(w_second, "blk", axis=0, tiled=True)
-    queries = rotate(projected[:, :query_width].reshape(new_rows, -1, HD), positions).astype(
-        jnp.bfloat16
-    )
-    key_new = rotate(
-        projected[:, query_width : query_width + key_width].reshape(new_rows, kv_local, HD),
-        positions,
-    ).astype(jnp.bfloat16)
-    value_new = (
-        projected[:, query_width + key_width :].reshape(new_rows, kv_local, HD).astype(jnp.bfloat16)
-    )
-    slot_ids = jnp.arange(prompts * slots, dtype=jnp.int32)
-    landing = slot_ids // slots * CAP + local_rank
-    for_me = slot_prompt == blk_index
-    received = (landing[None, :] == buffer_ids[:, None]) & for_me[None, :]
-    block_number = jnp.sum(jnp.where(received, global_rank[None, :], 0), axis=1)
-    block_live = jnp.any(received, axis=1)
-    blocks = arrived.reshape(prompts * CAP, 2, HD, BLOCK)
-    scalars = jnp.concatenate(
-        [block_number, block_live.astype(jnp.int32), jnp.stack([prefix_here, live_count])]
-    )
     attended = attend(
-        scalars,
-        jnp.transpose(queries, (1, 2, 0)),
-        key_new.reshape(new_rows, HD).T,
-        value_new.reshape(new_rows, HD).T,
-        blocks,
+        HEADS // groups,
+        slot_prompt,
+        prefix_len,
+        new_len,
+        projected,
+        jnp.cos(angles),
+        jnp.sin(angles),
+        arrived.reshape(prompts * CAP, 2, HD, BLOCK),
     ).reshape(-1, new_rows)
     projected_out = lax.dot_general(
         attended, w_out, (((0,), (0,)), ((), ())), preferred_element_type=jnp.float32
@@ -903,7 +881,7 @@
     partial_out = projected_out.astype(jnp.bfloat16)
     middle, normed_mid = sum_middle(groups, partial_out, tokens, mlp_gain)
     summed = feed_forward(groups, normed_mid, middle, w_pair, w_down).T
-    mixed = jnp.where((row_ids < live_count)[:, None], summed, 0.0)
+    mixed = jnp.where((row_ids < new_len[blk_index])[:, None], summed, 0.0)
     return mixed.astype(jnp.bfloat16)
 
 

time: 207 us -> 204 us (0.986)
  Pallas kernels: 162 us -> 170 us
  local copies, waits for them, and re-layouts: 15.2 us -> 8.99 us
  other arithmetic: 10.9 us -> 6.67 us
    pallas_call x1, Pallas kernels: 61.2 us -> 67.4 us  [sum_middle(): pl.pallas_call(functools.partial(middle_kernel, n), name='sum_middle', co...]
    pallas_call x1 -> x0, local copies, waits for them, and re-layouts: 2.59 us -> none  [regroup(): pl.pallas_call(functools.partial(regroup_kernel, n_kv, n_blk), name='regr...]
    concatenate x2 -> x0, other arithmetic: 2.26 us -> none  [the longest x1 1.88 us: shards(): jnp.concatenate([block_number, block_live.astype(jnp.int32), jnp.stack([p...]
  transfers between devices with their start and end apart: 1 -> 1, of which waited for: 0 -> 0; matrix products, arithmetic and copies ran while one was open for 8% -> 4% of each run, Pallas kernels for 40% -> 44%
where the time goes in v10:
time: 204 us
  Pallas kernels  170 us (83%)
  between operations  13.6 us (7%)
  local copies, waits for them, and re-layouts  8.99 us (4%)
  other arithmetic  6.67 us (3%)
  matrix products  4 us (2%)
    pallas_call x1, Pallas kernels, sum_middle(): pl.pallas_call(functools.partial(middle_kernel, n), name='sum_middle', co...  67.4 us
    pallas_call x1, Pallas kernels, regroup(): pl.pallas_call(functools.partial(regroup_kernel, n_kv, n_blk), name='regr...  44.3 us
    pallas_call x1, Pallas kernels, feed_forward(): pl.pallas_call(functools.partial(hidden_kernel, n), name='feed_forward',...  35.6 us
    pallas_call x1, Pallas kernels, attend(): pl.pallas_call(attention_kernel, name='attend', grid=(heads,), out_shape=...  22.9 us
  transfers between devices with their start and end apart: 1, of which 0 were waited for; matrix products, arithmetic and copies ran while one was open for 4% of the time, Pallas kernels for 44%

profile of v10, /device:TPU:1, one launch (start us, length us, event | category | flops | bytes accessed | tf_op | source)
XLA Modules:
  0.0 203.6 jit_solution(14800166284325462289)
XLA Ops:
  6.6 0.9 dynamic_slice.10
  7.4 0.2 convert_reduce_fusion
  7.7 1.7 gather_fusion
  9.4 0.9 slice.10.cache_ref
  10.3 0.6 slice_bitcast_fusion.extra_ref
  11.0 0.5 reshape.74
  11.5 1.2 convert_element_type.41
  12.7 0.5 reshape.76
  13.4 1.0 copy.24.second_ref
  14.7 0.1 reshape.71
  14.8 0.6 reshape.80.gain_ref
  15.5 0.8 pad_maximum_fusion.1.first_ref
  16.3 44.3 %regroup.1 = (f32[480,512]{1,0:T(8,128)}, bf16[160,1792]{1,0:T(8,128)(2,1)}, bf16[16,2,2,80,128]{4,3,2,1,0:T(8,128)(2,1)}) custom-call(bf16[8,20,480]{2,1,0:T(8,128)(2,1)} %pad_maximum_fusion.1.first_ref, bf16[8,20,1792]{2,1,0:T(8,128)(2,1)} %copy.24.second_ref, bf16[16,2,80,128]{3,2,1,0:T(8,128)(2,1)} %slice.10.cache_ref, ...), custom_call_target="tpu_custom_call" | custom-call | tf_op jit(solution)/shard_map/regroup/pallas_call | solution.py:248
  60.6 0.6 reshape.84.gain_ref
  61.2 0.6 dynamic_slice.11
  61.8 0.7 dynamic_slice.9
  62.5 0.7 add_convert_fusion
  63.1 1.0 multiply_sine_fusion
  64.2 22.9 %attend.1 = bf16[4,80,512]{2,1,0:T(8,128)(2,1)} custom-call(s32[128]{0:T(128)} %prompt_ref.1, s32[16]{0:T(128)} %prefix_ref.1, s32[16]{0:T(128)} %new_ref.1, f32[480,512]{1,0:T(8,128)} %get-tuple-element.10.projected_ref, f32[40,512]{1,0:T(8,128)} %get-tuple-element.16.cosine_ref, f32[40,512]{1,0:T(8,128)} %get-tuple-element.15.sine_ref, ...), custom_call_target="tpu_custom_call" | custom-call | flops 4831838208 | bytes 1474560 | tf_op jit(solution)/shard_map/attend/pallas_call | solution.py:429
  87.1 4.0 %convolution_convert_fusion = bf16[512,2560]{1,0:T(8,128)(2,1)} fusion(bf16[320,512]{1,0:T(8,128)(2,1)} %bitcast.33, bf16[320,2560]{1,0:T(8,128)(2,1)S(1)} %copy-done), kind=kOutput, calls=%fused_computation.1 | convolution fusion | flops 840171520 | bytes 4587520 | tf_op jit(solution)/shard_map/dot_general | solution.py:878
  91.1 67.4 %sum_middle.1 = (bf16[512,2560]{1,0:T(8,128)(2,1)}, bf16[512,2560]{1,0:T(8,128)(2,1)}) custom-call(bf16[8,2,32,2560]{3,2,1,0:T(8,128)(2,1)} %bitcast.28, bf16[512,2560]{1,0:T(8,128)(2,1)} %token_ref.3, f32[1,2560]{1,0:T(1,128)} %reshape.84.gain_ref), custom_call_target="tpu_custom_call" | custom-call | bytes 200000000 | tf_op jit(solution)/shard_map/sum_middle/pallas_call | solution.py:677
  158.5 0.7 iota_compare_fusion.2
  159.2 35.6 %feed_forward.1 = f32[320,512]{1,0:T(8,128)} custom-call(bf16[512,2560]{1,0:T(8,128)(2,1)} %get-tuple-element.12.normed_ref, bf16[512,2560]{1,0:T(8,128)(2,1)} %get-tuple-element.13.middle_hbm, bf16[2560,1792]{1,0:T(8,128)(2,1)} %all-gather.2.cloned.1.call-done.pair_hbm, bf16[864,2560]{1,0:T(8,128)(2,1)} %down_hbm.1), custom_call_target="tpu_custom_call" | custom-call | tf_op jit(solution)/shard_map/feed_forward/pallas_call | solution.py:778
  194.9 1.9 fusion
  (37 shorter events, 0.7 us)
Async XLA Ops:
  6.5 80.5 %copy-start = (bf16[320,2560]{1,0:T(8,128)(2,1)S(1)}, bf16[320,2560]{1,0:T(8,128)(2,1)}, u32[]{:S(2)}) copy-start(bf16[320,2560]{1,0:T(8,128)(2,1)} %param.22) | copy-start | bytes 4915204
  6.5 4.4 %copy-start.1 = (f32[20,6912]{1,0:T(8,128)S(1)}, f32[20,6912]{1,0:T(8,128)}, u32[]{:S(2)}) copy-start(f32[20,6912]{1,0:T(8,128)} %param.20) | copy-start | bytes 1658884
  6.5 152.7 %all-gather.2.cloned.1.call-start = ((), (), s32[]{:S(2)}) async-start(), calls=%async_computation | async-start | bytes 9748480 | tf_op jit(solution)/shard_map/all_gather | solution.py:867
  11.5 2.9 %copy-start.3 = (f32[20,640]{1,0:T(8,128)S(1)}, f32[20,640]{1,0:T(8,128)}, u32[]{:S(2)}) copy-start(f32[20,640]{1,0:T(8,128)} %param.18) | copy-start | bytes 153604
  11.5 3.0 %copy-start.4 = (f32[20,640]{1,0:T(8,128)S(1)}, f32[20,640]{1,0:T(8,128)}, u32[]{:S(2)}) copy-start(f32[20,640]{1,0:T(8,128)} %param.19) | copy-start | bytes 153604
  11.5 3.1 %copy-start.2 = (f32[20,2560]{1,0:T(8,128)S(1)}, f32[20,2560]{1,0:T(8,128)}, u32[]{:S(2)}) copy-start(f32[20,2560]{1,0:T(8,128)} %param.17) | copy-start | bytes 614404
  12.7 2.1 %copy-start.5 = (f32[2560]{0:T(1024)S(1)}, f32[2560]{0:T(1024)}, u32[]{:S(2)}) copy-start(f32[2560]{0:T(1024)} %param.15) | copy-start | bytes 30724
  15.5 45.1 %copy-start.6 = (f32[2560]{0:T(1024)S(1)}, f32[2560]{0:T(1024)}, u32[]{:S(2)}) copy-start(f32[2560]{0:T(1024)} %param.16) | copy-start | bytes 30724
  15.5 45.7 %copy-start.7 = (s32[16]{0:T(128)S(1)}, s32[16]{0:T(128)}, u32[]{:S(2)}) copy-start(s32[16]{0:T(128)} %prefix_ref.1) | copy-start | bytes 196
  15.5 46.3 %copy-start.8 = (s32[16]{0:T(128)S(1)}, s32[16]{0:T(128)}, u32[]{:S(2)}) copy-start(s32[16]{0:T(128)} %new_ref.1) | copy-start | bytes 196
Sparse Core Ops, SparseCore 0:
  60.7 96.1 all-gather.1

commit v11 on v10

--- a/solution.py
+++ b/solution.py
@@ -690,23 +690,43 @@
 
 def hidden_kernel(
     n, normed_ref, middle_hbm, pair_hbm, down_hbm, out_ref, pair, down, hidden, terms,
-    window, turned, pair_sem, down_sem, window_sem,
+    window, turned, pair_sem, swap_send, swap_recv, down_sem, window_sem,
     land_a, land_b, stage_a, stage_b, got_a, got_b, send, recv,
 ):
     me = lax.axis_index("kv")
     rows, width = normed_ref.shape
     halves, part = terms.shape[0], terms.shape[2]
     piece = width // n
-    tiles = pair.shape[1] // 256
+    tiles = pair.shape[3] // 256
+    blk = lax.axis_index("blk")
+    core = lax.rem(blk, 2)
+    sibling = blk + 1 - 2 * core
     units = down.shape[0]
     barrier = hail(n, me)
+    pl.semaphore_signal(barrier, inc=1, device_id={"blk": sibling}, device_id_type=MESH)
 
     def bring(tile):
         lanes = pl.ds(pl.multiple_of(tile * 256, 256), 256)
-        return pltpu.make_async_copy(pair_hbm.at[:, lanes], pair.at[:, lanes], pair_sem.at[tile])
+        return pltpu.make_async_copy(
+            pair_hbm.at[:, :, lanes], pair.at[:, core, :, lanes], pair_sem.at[tile]
+        )
+
+    def swap(tile):
+        lanes = pl.ds(pl.multiple_of(tile * 256, 256), 256)
+        return pltpu.make_async_remote_copy(
+            src_ref=pair_hbm.at[:, :, lanes],
+            dst_ref=pair.at[:, core, :, lanes],
+            send_sem=swap_send.at[tile],
+            recv_sem=swap_recv.at[tile],
+            device_id={"blk": sibling},
+            device_id_type=MESH,
+        )
 
     for tile in range(tiles):
         bring(tile).start()
+    pl.semaphore_wait(barrier, n)
+    for tile in range(tiles):
+        swap(tile).start()
     fetch = pltpu.make_async_copy(down_hbm, down, down_sem)
     fetch.start()
     left = lax.div(me * piece, 128) * 128
@@ -731,8 +751,13 @@
         def _(tile):
             if half == 0:
                 bring(tile).wait()
+                swap(tile).wait()
             lanes = pl.ds(pl.multiple_of(tile * 256, 256), 256)
-            both = jnp.dot(normed_ref[lines, :], pair[:, lanes], preferred_element_type=jnp.float32)
+            both = jnp.dot(
+                normed_ref[lines, :],
+                pair[:, :, :, lanes].reshape(width, 256),
+                preferred_element_type=jnp.float32,
+            )
             gate, up = both[:, :128], both[:, 128:]
             hidden[:, pl.ds(pl.multiple_of(tile * 128, 128), 128)] = (
                 gate / (1.0 + jnp.exp(-gate)) * up
@@ -749,8 +774,6 @@
             )
             terms[half, spot, :] = term.T.astype(jnp.bfloat16)
 
-        if half == 0:
-            pl.semaphore_wait(barrier, n - 1)
         sums[half].open()
     view.wait()
     turned[...] = window[...].astype(jnp.float32).T
@@ -782,13 +805,15 @@
         in_specs=[VMEM_SPEC, any_spec, any_spec, any_spec],
         out_specs=VMEM_SPEC,
         scratch_shapes=[
-            pltpu.VMEM(w_pair.shape, half),
+            pltpu.VMEM((w_pair.shape[0], 2) + w_pair.shape[1:], half),
             pltpu.VMEM(w_down.shape, half),
-            pltpu.VMEM((part, w_pair.shape[1] // 2), half),
+            pltpu.VMEM((part, w_pair.shape[2] // 2), half),
             pltpu.VMEM((halves, width, part), half),
             pltpu.VMEM((rows, piece + 64), half),
             pltpu.VMEM((piece + 64, rows), jnp.float32),
-            dma((w_pair.shape[1] // 256,)),
+            dma((w_pair.shape[2] // 256,)),
+            dma((w_pair.shape[2] // 256,)),
+            dma((w_pair.shape[2] // 256,)),
             dma,
             dma,
         ]
@@ -864,7 +889,8 @@
         tokens,
         attn_gain,
     )
-    w_pair = lax.all_gather(w_second, "blk", axis=0, tiled=True)
+    same_core = [list(range(core, n_blocks, 2)) for core in range(2)]
+    w_pair = lax.all_gather(w_second, "blk", axis=0, axis_index_groups=same_core)
     attended = attend(
         HEADS // groups,
         slot_prompt,

time: 204 us -> 209 us (1.025)
  Pallas kernels: 170 us -> 176 us
    pallas_call x1, Pallas kernels: 35.6 us -> 41.3 us  [feed_forward(): pl.pallas_call(functools.partial(hidden_kernel, n), name='feed_forward',...]
  transfers between devices with their start and end apart: 1 -> 1, of which waited for: 0 -> 0; matrix products, arithmetic and copies ran while one was open for 4% -> 4% of each run, Pallas kernels for 44% -> 43%
where the time goes in v11:
time: 209 us
  Pallas kernels  176 us (84%)
  between operations  13.6 us (7%)
  local copies, waits for them, and re-layouts  8.94 us (4%)
  other arithmetic  6.63 us (3%)
  matrix products  3.99 us (2%)
    pallas_call x1, Pallas kernels, sum_middle(): pl.pallas_call(functools.partial(middle_kernel, n), name='sum_middle', co...  67.4 us
    pallas_call x1, Pallas kernels, regroup(): pl.pallas_call(functools.partial(regroup_kernel, n_kv, n_blk), name='regr...  44.3 us
    pallas_call x1, Pallas kernels, feed_forward(): pl.pallas_call(functools.partial(hidden_kernel, n), name='feed_forward',...  41.3 us
    pallas_call x1, Pallas kernels, attend(): pl.pallas_call(attention_kernel, name='attend', grid=(heads,), out_shape=...  22.9 us
  transfers between devices with their start and end apart: 1, of which 0 were waited for; matrix products, arithmetic and copies ran while one was open for 4% of the time, Pallas kernels for 43%

profile of v11, /device:TPU:1, one launch (start us, length us, event | category | flops | bytes accessed | tf_op | source)
XLA Modules:
  0.0 209.1 jit_solution(17327856282410854748)
XLA Ops:
  6.6 0.9 dynamic_slice.10
  7.4 0.2 convert_reduce_fusion
  7.7 1.7 gather_fusion
  9.4 0.9 slice.10.cache_ref
  10.3 0.6 slice_bitcast_fusion.extra_ref
  11.0 0.5 reshape.74
  11.5 1.2 convert_element_type.41
  12.7 0.5 reshape.76
  13.4 1.0 copy.24.second_ref
  14.6 0.1 reshape.71
  14.8 0.6 reshape.80.gain_ref
  15.5 0.8 pad_maximum_fusion.1.first_ref
  16.3 44.3 %regroup.1 = (f32[480,512]{1,0:T(8,128)}, bf16[160,1792]{1,0:T(8,128)(2,1)}, bf16[16,2,2,80,128]{4,3,2,1,0:T(8,128)(2,1)}) custom-call(bf16[8,20,480]{2,1,0:T(8,128)(2,1)} %pad_maximum_fusion.1.first_ref, bf16[8,20,1792]{2,1,0:T(8,128)(2,1)} %copy.24.second_ref, bf16[16,2,80,128]{3,2,1,0:T(8,128)(2,1)} %slice.10.cache_ref, ...), custom_call_target="tpu_custom_call" | custom-call | tf_op jit(solution)/shard_map/regroup/pallas_call | solution.py:248
  60.7 0.6 reshape.84.gain_ref
  61.3 0.6 dynamic_slice.11
  61.8 0.6 dynamic_slice.9
  62.5 0.7 add_convert_fusion
  63.1 1.0 multiply_sine_fusion
  64.2 22.9 %attend.1 = bf16[4,80,512]{2,1,0:T(8,128)(2,1)} custom-call(s32[128]{0:T(128)} %prompt_ref.1, s32[16]{0:T(128)} %prefix_ref.1, s32[16]{0:T(128)} %new_ref.1, f32[480,512]{1,0:T(8,128)} %get-tuple-element.10.projected_ref, f32[40,512]{1,0:T(8,128)} %get-tuple-element.16.cosine_ref, f32[40,512]{1,0:T(8,128)} %get-tuple-element.15.sine_ref, ...), custom_call_target="tpu_custom_call" | custom-call | flops 4831838208 | bytes 1474560 | tf_op jit(solution)/shard_map/attend/pallas_call | solution.py:429
  87.1 4.0 %convolution_convert_fusion = bf16[512,2560]{1,0:T(8,128)(2,1)} fusion(bf16[320,512]{1,0:T(8,128)(2,1)} %bitcast.35, bf16[320,2560]{1,0:T(8,128)(2,1)S(1)} %copy-done), kind=kOutput, calls=%fused_computation.1 | convolution fusion | flops 840171520 | bytes 4587520 | tf_op jit(solution)/shard_map/dot_general | solution.py:904
  91.1 67.4 %sum_middle.1 = (bf16[512,2560]{1,0:T(8,128)(2,1)}, bf16[512,2560]{1,0:T(8,128)(2,1)}) custom-call(bf16[8,2,32,2560]{3,2,1,0:T(8,128)(2,1)} %bitcast.30, bf16[512,2560]{1,0:T(8,128)(2,1)} %token_ref.3, f32[1,2560]{1,0:T(1,128)} %reshape.84.gain_ref), custom_call_target="tpu_custom_call" | custom-call | bytes 200000000 | tf_op jit(solution)/shard_map/sum_middle/pallas_call | solution.py:677
  158.4 0.6 iota_compare_fusion.2
  159.1 41.3 %feed_forward.1 = f32[320,512]{1,0:T(8,128)} custom-call(bf16[512,2560]{1,0:T(8,128)(2,1)} %get-tuple-element.12.normed_ref, bf16[512,2560]{1,0:T(8,128)(2,1)} %get-tuple-element.13.middle_hbm, bf16[8,160,1792]{2,1,0:T(8,128)(2,1)} %bitcast.29, bf16[864,2560]{1,0:T(8,128)(2,1)} %down_hbm.1), custom_call_target="tpu_custom_call" | custom-call | tf_op jit(solution)/shard_map/feed_forward/pallas_call | solution.py:801
  200.4 1.9 fusion
  (37 shorter events, 0.7 us)
Async XLA Ops:
  6.5 80.5 %copy-start = (bf16[320,2560]{1,0:T(8,128)(2,1)S(1)}, bf16[320,2560]{1,0:T(8,128)(2,1)}, u32[]{:S(2)}) copy-start(bf16[320,2560]{1,0:T(8,128)(2,1)} %param.22) | copy-start | bytes 4915204
  6.5 4.4 %copy-start.1 = (f32[20,6912]{1,0:T(8,128)S(1)}, f32[20,6912]{1,0:T(8,128)}, u32[]{:S(2)}) copy-start(f32[20,6912]{1,0:T(8,128)} %param.20) | copy-start | bytes 1658884
  6.5 152.6 %all-gather.3.cloned.1.call-start = ((), (), s32[]{:S(2)}) async-start(), calls=%async_computation | async-start | bytes 5160960 | tf_op jit(solution)/shard_map/all_gather | solution.py:893
  11.5 2.9 %copy-start.3 = (f32[20,640]{1,0:T(8,128)S(1)}, f32[20,640]{1,0:T(8,128)}, u32[]{:S(2)}) copy-start(f32[20,640]{1,0:T(8,128)} %param.18) | copy-start | bytes 153604
  11.5 3.0 %copy-start.4 = (f32[20,640]{1,0:T(8,128)S(1)}, f32[20,640]{1,0:T(8,128)}, u32[]{:S(2)}) copy-start(f32[20,640]{1,0:T(8,128)} %param.19) | copy-start | bytes 153604
  11.5 3.1 %copy-start.2 = (f32[20,2560]{1,0:T(8,128)S(1)}, f32[20,2560]{1,0:T(8,128)}, u32[]{:S(2)}) copy-start(f32[20,2560]{1,0:T(8,128)} %param.17) | copy-start | bytes 614404
  12.7 2.1 %copy-start.5 = (f32[2560]{0:T(1024)S(1)}, f32[2560]{0:T(1024)}, u32[]{:S(2)}) copy-start(f32[2560]{0:T(1024)} %param.15) | copy-start | bytes 30724
  15.5 45.2 %copy-start.6 = (f32[2560]{0:T(1024)S(1)}, f32[2560]{0:T(1024)}, u32[]{:S(2)}) copy-start(f32[2560]{0:T(1024)} %param.16) | copy-start | bytes 30724
  15.5 45.8 %copy-start.7 = (s32[16]{0:T(128)S(1)}, s32[16]{0:T(128)}, u32[]{:S(2)}) copy-start(s32[16]{0:T(128)} %prefix_ref.1) | copy-start | bytes 196
  15.5 46.4 %copy-start.8 = (s32[16]{0:T(128)S(1)}, s32[16]{0:T(128)}, u32[]{:S(2)}) copy-start(s32[16]{0:T(128)} %new_ref.1) | copy-start | bytes 196
Sparse Core Ops, SparseCore 0:
  60.8 93.6 all-gather.2

commit v12 on v10

--- a/solution.py
+++ b/solution.py
@@ -697,16 +697,22 @@
     rows, width = normed_ref.shape
     halves, part = terms.shape[0], terms.shape[2]
     piece = width // n
-    tiles = pair.shape[1] // 256
+    tiles = pair.shape[3] // 256
     units = down.shape[0]
     barrier = hail(n, me)
 
     def bring(tile):
         lanes = pl.ds(pl.multiple_of(tile * 256, 256), 256)
-        return pltpu.make_async_copy(pair_hbm.at[:, lanes], pair.at[:, lanes], pair_sem.at[tile])
+        return [
+            pltpu.make_async_copy(
+                pair_hbm.at[:, side, :, lanes], pair.at[side, :, :, lanes], pair_sem.at[tile, side]
+            )
+            for side in range(2)
+        ]
 
     for tile in range(tiles):
-        bring(tile).start()
+        for copy in bring(tile):
+            copy.start()
     fetch = pltpu.make_async_copy(down_hbm, down, down_sem)
     fetch.start()
     left = lax.div(me * piece, 128) * 128
@@ -730,9 +736,14 @@
         @pl.loop(0, tiles)
         def _(tile):
             if half == 0:
-                bring(tile).wait()
+                for copy in bring(tile):
+                    copy.wait()
             lanes = pl.ds(pl.multiple_of(tile * 256, 256), 256)
-            both = jnp.dot(normed_ref[lines, :], pair[:, lanes], preferred_element_type=jnp.float32)
+            both = jnp.dot(
+                normed_ref[lines, :],
+                pair[:, :, :, lanes].reshape(width, 256),
+                preferred_element_type=jnp.float32,
+            )
             gate, up = both[:, :128], both[:, 128:]
             hidden[:, pl.ds(pl.multiple_of(tile * 128, 128), 128)] = (
                 gate / (1.0 + jnp.exp(-gate)) * up
@@ -782,13 +793,13 @@
         in_specs=[VMEM_SPEC, any_spec, any_spec, any_spec],
         out_specs=VMEM_SPEC,
         scratch_shapes=[
-            pltpu.VMEM(w_pair.shape, half),
+            pltpu.VMEM((2, w_pair.shape[0]) + w_pair.shape[2:], half),
             pltpu.VMEM(w_down.shape, half),
-            pltpu.VMEM((part, w_pair.shape[1] // 2), half),
+            pltpu.VMEM((part, w_pair.shape[3] // 2), half),
             pltpu.VMEM((halves, width, part), half),
             pltpu.VMEM((rows, piece + 64), half),
             pltpu.VMEM((piece + 64, rows), jnp.float32),
-            dma((w_pair.shape[1] // 256,)),
+            dma((w_pair.shape[3] // 256, 2)),
             dma,
             dma,
         ]
@@ -864,7 +875,10 @@
         tokens,
         attn_gain,
     )
-    w_pair = lax.all_gather(w_second, "blk", axis=0, tiled=True)
+    line = n_blocks // 2
+    facing = [[spot, spot + line] for spot in range(line)]
+    sides = [list(range(line)), list(range(line, n_blocks))]
+    w_both = lax.all_gather(w_second, "blk", axis=0, axis_index_groups=facing)
     attended = attend(
         HEADS // groups,
         slot_prompt,
@@ -875,6 +889,8 @@
         jnp.sin(angles),
         arrived.reshape(prompts * CAP, 2, HD, BLOCK),
     ).reshape(-1, new_rows)
+    attended, w_both = lax.optimization_barrier((attended, w_both))
+    w_pair = lax.all_gather(w_both, "blk", axis=0, axis_index_groups=sides)
     projected_out = lax.dot_general(
         attended, w_out, (((0,), (0,)), ((), ())), preferred_element_type=jnp.float32
     )

time: 204 us -> 185 us (0.907)
  Pallas kernels: 170 us -> 149 us
    pallas_call x1, Pallas kernels: 67.4 us -> 46.3 us  [sum_middle(): pl.pallas_call(functools.partial(middle_kernel, n), name='sum_middle', co...]
  transfers between devices with their start and end apart: 1 -> 2, of which waited for: 0 -> 1; matrix products, arithmetic and copies ran while one was open for 4% -> 4% of each run, Pallas kernels for 44% -> 38%
where the time goes in v12:
time: 185 us
  Pallas kernels  149 us (81%)
  between operations  13.6 us (7%)
  local copies, waits for them, and re-layouts  8.97 us (5%)
  other arithmetic  6.6 us (4%)
  matrix products  4 us (2%)
    pallas_call x1, Pallas kernels, sum_middle(): pl.pallas_call(functools.partial(middle_kernel, n), name='sum_middle', co...  46.3 us
    pallas_call x1, Pallas kernels, regroup(): pl.pallas_call(functools.partial(regroup_kernel, n_kv, n_blk), name='regr...  44.3 us
    pallas_call x1, Pallas kernels, feed_forward(): pl.pallas_call(functools.partial(hidden_kernel, n), name='feed_forward',...  35.9 us
    pallas_call x1, Pallas kernels, attend(): pl.pallas_call(attention_kernel, name='attend', grid=(heads,), out_shape=...  22.9 us
    dot_general x1, matrix products, shards(): lax.dot_general(attended, w_out, (((0,), (0,)), ((), ())), preferred_elem...  4 us
  transfers between devices with their start and end apart: 2, of which 1 were waited for; matrix products, arithmetic and copies ran while one was open for 4% of the time, Pallas kernels for 38%

profile of v12, /device:TPU:1, one launch (start us, length us, event | category | flops | bytes accessed | tf_op | source)
XLA Modules:
  0.0 184.5 jit_solution(2486531000777253217)
XLA Ops:
  6.6 0.9 dynamic_slice.10
  7.7 1.7 gather_fusion
  9.4 0.9 slice.10.cache_ref
  10.3 0.6 slice_bitcast_fusion.extra_ref
  11.0 0.5 reshape.74
  11.5 1.2 convert_element_type.41
  12.7 0.5 reshape.76
  13.4 1.0 copy.28.second_ref
  14.8 0.6 reshape.80.gain_ref
  15.5 0.8 pad_maximum_fusion.1.first_ref
  16.3 44.3 %regroup.1 = (f32[480,512]{1,0:T(8,128)}, bf16[160,1792]{1,0:T(8,128)(2,1)}, bf16[16,2,2,80,128]{4,3,2,1,0:T(8,128)(2,1)}) custom-call(bf16[8,20,480]{2,1,0:T(8,128)(2,1)} %pad_maximum_fusion.1.first_ref, bf16[8,20,1792]{2,1,0:T(8,128)(2,1)} %copy.28.second_ref, bf16[16,2,80,128]{3,2,1,0:T(8,128)(2,1)} %slice.10.cache_ref, ...), custom_call_target="tpu_custom_call" | custom-call | tf_op jit(solution)/shard_map/regroup/pallas_call | solution.py:248
  60.5 0.2 all-gather.7.cloned.1.call-start
  60.8 0.6 dynamic_slice.11
  61.4 0.7 add_convert_fusion
  62.0 1.0 multiply_sine_fusion
  63.1 22.9 %attend.1 = bf16[4,80,512]{2,1,0:T(8,128)(2,1)} custom-call(s32[128]{0:T(128)} %prompt_ref.1, s32[16]{0:T(128)} %prefix_ref.1, s32[16]{0:T(128)} %new_ref.1, f32[480,512]{1,0:T(8,128)} %get-tuple-element.12.projected_ref, f32[40,512]{1,0:T(8,128)} %get-tuple-element.20.cosine_ref, f32[40,512]{1,0:T(8,128)} %get-tuple-element.19.sine_ref, ...), custom_call_target="tpu_custom_call" | custom-call | flops 4831838208 | bytes 1474560 | tf_op jit(solution)/shard_map/attend/pallas_call | solution.py:429
  86.0 0.6 dynamic_slice.9
  86.7 0.6 reshape.84.gain_ref
  87.3 0.6 iota_compare_fusion.2
  87.9 4.0 %convolution_convert_fusion = bf16[512,2560]{1,0:T(8,128)(2,1)} fusion(bf16[320,512]{1,0:T(8,128)(2,1)} %bitcast.37, bf16[320,2560]{1,0:T(8,128)(2,1)S(1)} %copy-done), kind=kOutput, calls=%fused_computation.1 | convolution fusion | flops 840171520 | bytes 4587520 | tf_op jit(solution)/shard_map/dot_general | solution.py:894
  91.9 46.3 %sum_middle.1 = (bf16[512,2560]{1,0:T(8,128)(2,1)}, bf16[512,2560]{1,0:T(8,128)(2,1)}) custom-call(bf16[8,2,32,2560]{3,2,1,0:T(8,128)(2,1)} %bitcast.31, bf16[512,2560]{1,0:T(8,128)(2,1)} %token_ref.3, f32[1,2560]{1,0:T(1,128)} %reshape.84.gain_ref), custom_call_target="tpu_custom_call" | custom-call | bytes 200000000 | tf_op jit(solution)/shard_map/sum_middle/pallas_call | solution.py:677
  138.3 1.7 all-gather.7.cloned.1.call-done
  139.9 35.9 %feed_forward.1 = f32[320,512]{1,0:T(8,128)} custom-call(bf16[512,2560]{1,0:T(8,128)(2,1)} %get-tuple-element.16.normed_ref, bf16[512,2560]{1,0:T(8,128)(2,1)} %get-tuple-element.17.middle_hbm, bf16[8,2,160,1792]{3,2,1,0:T(8,128)(2,1)} %bitcast.30, bf16[864,2560]{1,0:T(8,128)(2,1)} %down_hbm.1), custom_call_target="tpu_custom_call" | custom-call | tf_op jit(solution)/shard_map/feed_forward/pallas_call | solution.py:789
  175.8 1.9 %fusion = bf16[512,320]{0,1:T(8,128)(2,1)} fusion(f32[320,512]{1,0:T(8,128)} %feed_forward.1, pred[512]{0:T(512)(128)(4,1)S(1)} %iota_compare_fusion.2), kind=kLoop, calls=%fused_computation.4 | loop fusion | flops 163840 | bytes 983552 | tf_op jit(solution)/shard_map/convert_element_type | solution.py:901
  (40 shorter events, 1.0 us)
Async XLA Ops:
  6.5 81.4 %copy-start = (bf16[320,2560]{1,0:T(8,128)(2,1)S(1)}, bf16[320,2560]{1,0:T(8,128)(2,1)}, u32[]{:S(2)}) copy-start(bf16[320,2560]{1,0:T(8,128)(2,1)} %param.22) | copy-start | bytes 4915204
  6.5 4.4 %copy-start.1 = (f32[20,6912]{1,0:T(8,128)S(1)}, f32[20,6912]{1,0:T(8,128)}, u32[]{:S(2)}) copy-start(f32[20,6912]{1,0:T(8,128)} %param.20) | copy-start | bytes 1658884
  6.5 79.5 %all-gather.5.cloned.1.call-start = ((), (), s32[]{:S(2)}) async-start(), calls=%async_computation | async-start | bytes 1720320 | tf_op jit(solution)/shard_map/all_gather | solution.py:881
  11.5 2.9 %copy-start.3 = (f32[20,640]{1,0:T(8,128)S(1)}, f32[20,640]{1,0:T(8,128)}, u32[]{:S(2)}) copy-start(f32[20,640]{1,0:T(8,128)} %param.18) | copy-start | bytes 153604
  11.5 3.0 %copy-start.4 = (f32[20,640]{1,0:T(8,128)S(1)}, f32[20,640]{1,0:T(8,128)}, u32[]{:S(2)}) copy-start(f32[20,640]{1,0:T(8,128)} %param.19) | copy-start | bytes 153604
  11.5 3.1 %copy-start.2 = (f32[20,2560]{1,0:T(8,128)S(1)}, f32[20,2560]{1,0:T(8,128)}, u32[]{:S(2)}) copy-start(f32[20,2560]{1,0:T(8,128)} %param.17) | copy-start | bytes 614404
  12.7 2.1 %copy-start.5 = (f32[2560]{0:T(1024)S(1)}, f32[2560]{0:T(1024)}, u32[]{:S(2)}) copy-start(f32[2560]{0:T(1024)} %param.15) | copy-start | bytes 30724
  15.5 45.3 %copy-start.7 = (s32[16]{0:T(128)S(1)}, s32[16]{0:T(128)}, u32[]{:S(2)}) copy-start(s32[16]{0:T(128)} %prefix_ref.1) | copy-start | bytes 196
  60.5 79.4 %all-gather.7.cloned.1.call-start = ((), (), s32[]{:S(2)}) async-start(), calls=%async_computation.1 | async-start | bytes 10321920 | tf_op jit(solution)/shard_map/all_gather | solution.py:893
  63.1 23.0 %copy-start.8 = (s32[16]{0:T(128)S(1)}, s32[16]{0:T(128)}, u32[]{:S(2)}) copy-start(s32[16]{0:T(128)} %new_ref.1) | copy-start | bytes 196
  63.1 23.6 %copy-start.6 = (f32[2560]{0:T(1024)S(1)}, f32[2560]{0:T(1024)}, u32[]{:S(2)}) copy-start(f32[2560]{0:T(1024)} %param.16) | copy-start | bytes 30724
Sparse Core Ops, SparseCore 0:
  60.7 24.8 all-gather.4
  87.2 52.6 all-gather.6
